TPU v7x, 32 devices: a whole 2x2x4 slice. The times are simulated.
32 devices in a mesh: tm: 4 (over x, core), row: 2 (over y), col: 4 (over z).
Axes of the slice: x: 2, y: 2, z: 4, core: 2. Of those that a mesh axis runs over, the one named last changes fastest.
Arguments:
- first_inverse: bfloat16 [4, 1536, 1536], P('tm', ('row', 'col')), as said below
- second_diag: bfloat16 [4, 1536, 1536], P('tm', ('row', 'col')), as said below
- coupling: bfloat16 [4, 3, 1536, 1536], P('tm', None, ('row', 'col'))
- arrow_rows: float32 [4, 2, 8, 1536], P('tm')
- tip_block: float32 [8, 8], replicated, may hold values from -6 to 6
Outputs:
- separator_update: float32 [4, 1536, 1536], P('tm', ('row', 'col'))
- separator_fill: float32 [4, 1536, 1536], P('tm', ('row', 'col'))
- reduced_tip: float32 [8, 8], replicated
Inputs may be any that keep to these rules, and one draw needn't show every extreme that they name: For every p, first_inverse[p] is lower triangular with a positive diagonal. For every p, second_diag[p] is symmetric, and second_diag[p] minus coupling[p, 1] first_inverse[p]^T first_inverse[p] coupling[p, 1]^T is positive definite.
All inputs are finite; a program needn't handle non-finite values.
Results may differ from a plain program's by a relative error of at most 0.009.
Values may be sent and summed in bfloat16 or wider, within the bound.
No kernel may reach another device: no remote copies, remote signals or barrier semaphores. Data moves between devices by JAX's collectives and lax.ppermute only.
A program may use at most 128 MiB of HBM per device.

v0:
```python
import jax
import jax.numpy as jnp
from jax import lax
from jax.sharding import PartitionSpec as P


def from_behind(block, axis, distance):
    devices = range(lax.axis_size(axis))
    route = [(i - distance, i) for i in devices if i - distance in devices]
    return lax.ppermute(block, axis, route)


def right_solve(factor, rhs_rows):
    return lax.linalg.triangular_solve(
        factor, rhs_rows, left_side=False, lower=True, transpose_a=True
    )


def outer_rows(left_rows, right_rows):
    return jnp.einsum("ik,jk->ij", left_rows, right_rows, preferred_element_type=jnp.float32)


def gather_block(one_share):
    return lax.all_gather(one_share, ("row", "col"), axis=0, tiled=True)


def spread_panels(first_panel, second_panel):
    return (
        lax.all_gather(first_panel, ("row", "col"), axis=0, tiled=True),
        lax.all_gather(second_panel, ("row", "col"), axis=0, tiled=True),
    )


def shards(first_inverse, second_diag, coupling, arrow_rows, tip_block):
    share = coupling.shape[2]
    inverse_whole = gather_block(first_inverse[0])
    rhs_first = jnp.concatenate([coupling[0, 0], coupling[0, 1]], axis=0)
    solved_first = outer_rows(rhs_first, inverse_whole)
    top_own = solved_first[:share].astype(jnp.bfloat16)
    mid_own = solved_first[share:].astype(jnp.bfloat16)
    arrow_one = jnp.einsum(
        "ik,jk->ij",
        arrow_rows[0, 0],
        inverse_whole.astype(jnp.float32),
        precision=lax.Precision.HIGHEST,
    )
    top_whole, mid_whole = spread_panels(top_own, mid_own)
    sep_first = outer_rows(top_own, top_whole)
    fill_rows = -outer_rows(top_own, mid_whole)
    arrow_two_rows = arrow_rows[0, 1] - outer_rows(arrow_one.astype(jnp.bfloat16), mid_whole)
    tip_first = jnp.einsum("ik,jk->ij", arrow_one, arrow_one, precision=lax.Precision.HIGHEST)
    second_share = (second_diag[0].astype(jnp.float32) - outer_rows(mid_own, mid_whole)).astype(
        jnp.bfloat16
    )
    second_ready = gather_block(second_share)
    factor_two = jnp.linalg.cholesky(second_ready.astype(jnp.float32))
    rhs_second = jnp.concatenate(
        [fill_rows, coupling[0, 2].astype(jnp.float32), arrow_two_rows], axis=0
    )
    solved_second = right_solve(factor_two, rhs_second)
    upper_own = solved_second[:share].astype(jnp.bfloat16)
    lower_own = solved_second[share : 2 * share].astype(jnp.bfloat16)
    arrow_two = solved_second[2 * share :]
    tip_second = jnp.einsum("ik,jk->ij", arrow_two, arrow_two, precision=lax.Precision.HIGHEST)
    upper_whole, lower_whole = spread_panels(upper_own, lower_own)
    sep_second = outer_rows(upper_own, upper_whole)
    fill_block = -outer_rows(upper_own, lower_whole)
    handed = outer_rows(lower_own, lower_whole)
    incoming = from_behind(handed, "tm", 1)
    tip_total = lax.psum(tip_first + tip_second, "tm")
    separator_update = sep_first + sep_second + incoming
    return (separator_update[None], fill_block[None], tip_block - tip_total)


def solution(mesh):
    return jax.shard_map(
        shards,
        mesh=mesh,
        in_specs=(
            P("tm", ("row", "col"), None),
            P("tm", ("row", "col"), None),
            P("tm", None, ("row", "col"), None),
            P("tm", None, None, None),
            P(),
        ),
        out_specs=(P("tm", ("row", "col"), None), P("tm", ("row", "col"), None), P()),
        check_vma=False,
    )
```

profile of v0, /device:TPU:0, one launch (start us, length us, event | category | flops | bytes accessed | tf_op | source)
XLA Modules:
  0.0 1064.2 jit_solution(15958643128094356016)
XLA Ops:
  9.5 82.6 %all-gather.18.cloned.1.call-done = bf16[1,1536,1536]{2,1,0:T(8,128)(2,1)} async-done(((bf16[1,192,1536]{2,1,0:T(8,128)(2,1)}), bf16[1,1536,1536]{2,1,0:T(8,128)(2,1)}) %all-gather.18.cloned.1.call-update) | async-done | bytes 4718608 | tf_op jit(solution)/shard_map/all_gather | solution.py:24
  92.2 4.4 fusion.5
  97.7 77.8 %all-gather.10.cloned.1.call-done = bf16[1536,1536]{1,0:T(8,128)(2,1)} async-done(((bf16[192,1536]{1,0:T(8,128)(2,1)}), bf16[1536,1536]{1,0:T(8,128)(2,1)}) %all-gather.10.cloned.1.call-update) | async-done | bytes 4718608 | tf_op jit(solution)/shard_map/all_gather | solution.py:30
  175.5 4.8 fusion.11
  180.4 6.2 fusion.1
  191.3 66.9 %all-gather.12.cloned.1.call-done = bf16[1536,1536]{1,0:T(8,128)(2,1)} async-done(((bf16[192,1536]{1,0:T(8,128)(2,1)}), bf16[1536,1536]{1,0:T(8,128)(2,1)}) %all-gather.12.cloned.1.call-update) | async-done | bytes 4718608 | tf_op jit(solution)/shard_map/all_gather | solution.py:24
  258.2 6.6 copy.11
  264.8 7.9 copy.12
  272.8 6.5 fusion
  279.3 3.6 copy-done
  282.9 11.7 %cholesky.341 = f32[128,128]{1,0:T(8,128)S(1)} custom-call(f32[128,128]{1,0:T(8,128)S(1)} %cholesky.892), custom_call_target="Cholesky" | custom-call | tf_op jit(solution)/shard_map/jit(cholesky)/cholesky | solution.py:56
  294.7 9.8 custom-call.94
  304.5 4.8 cholesky.371
  314.0 11.9 %cholesky.362 = f32[128,128]{1,0:T(8,128)S(1)} custom-call(f32[128,128]{1,0:T(8,128)S(1)} %cholesky.896), custom_call_target="Cholesky" | custom-call | tf_op jit(solution)/shard_map/jit(cholesky)/cholesky | solution.py:56
  326.5 9.8 custom-call.95
  340.7 11.7 %cholesky.385 = f32[128,128]{1,0:T(8,128)S(1)} custom-call(f32[128,128]{1,0:T(8,128)S(1)} %cholesky.901), custom_call_target="Cholesky" | custom-call | tf_op jit(solution)/shard_map/jit(cholesky)/cholesky | solution.py:56
  353.7 9.8 custom-call.96
  365.2 3.3 convolution_subtract_fusion.1
  368.6 11.7 %cholesky.715 = f32[128,128]{1,0:T(8,128)S(1)} custom-call(f32[128,128]{1,0:T(8,128)S(1)} %cholesky.906), custom_call_target="Cholesky" | custom-call | tf_op jit(solution)/shard_map/jit(cholesky)/cholesky | solution.py:56
  381.6 9.8 custom-call.97
  392.9 3.6 fusion.28
  396.5 12.1 %cholesky.734 = f32[128,128]{1,0:T(8,128)S(1)} custom-call(f32[128,128]{1,0:T(8,128)S(1)} %cholesky.911), custom_call_target="Cholesky" | custom-call | tf_op jit(solution)/shard_map/jit(cholesky)/cholesky | solution.py:56
  409.9 9.8 custom-call.98
  421.1 3.8 fusion.31
  424.9 11.7 %cholesky.754 = f32[128,128]{1,0:T(8,128)S(1)} custom-call(f32[128,128]{1,0:T(8,128)S(1)} %cholesky.916), custom_call_target="Cholesky" | custom-call | tf_op jit(solution)/shard_map/jit(cholesky)/cholesky | solution.py:56
  438.0 9.9 custom-call.99
  449.2 3.8 fusion.34
  453.0 11.7 %cholesky.774 = f32[128,128]{1,0:T(8,128)S(1)} custom-call(f32[128,128]{1,0:T(8,128)S(1)} %cholesky.921), custom_call_target="Cholesky" | custom-call | tf_op jit(solution)/shard_map/jit(cholesky)/cholesky | solution.py:56
  466.1 9.8 custom-call.100
  477.1 3.8 fusion.37
  480.9 11.9 %cholesky.794 = f32[128,128]{1,0:T(8,128)S(1)} custom-call(f32[128,128]{1,0:T(8,128)S(1)} %cholesky.926), custom_call_target="Cholesky" | custom-call | tf_op jit(solution)/shard_map/jit(cholesky)/cholesky | solution.py:56
  494.2 9.8 custom-call.101
  505.1 3.6 fusion.43
  508.7 11.7 %cholesky.814 = f32[128,128]{1,0:T(8,128)S(1)} custom-call(f32[128,128]{1,0:T(8,128)S(1)} %cholesky.931), custom_call_target="Cholesky" | custom-call | tf_op jit(solution)/shard_map/jit(cholesky)/cholesky | solution.py:56
  521.7 10.2 custom-call.102
  533.0 3.3 fusion.46
  536.3 11.7 %cholesky.834 = f32[128,128]{1,0:T(8,128)S(1)} custom-call(f32[128,128]{1,0:T(8,128)S(1)} %cholesky.936), custom_call_target="Cholesky" | custom-call | tf_op jit(solution)/shard_map/jit(cholesky)/cholesky | solution.py:56
  549.3 9.8 custom-call.103
  562.9 11.9 %cholesky.854 = f32[128,128]{1,0:T(8,128)S(1)} custom-call(f32[128,128]{1,0:T(8,128)S(1)} %cholesky.941), custom_call_target="Cholesky" | custom-call | tf_op jit(solution)/shard_map/jit(cholesky)/cholesky | solution.py:56
  576.1 9.8 custom-call.104
  589.0 11.7 %cholesky.872 = f32[128,128]{1,0:T(8,128)S(1)} custom-call(f32[128,128]{1,0:T(8,128)S(1)} %convolution_subtract_fusion.16), custom_call_target="Cholesky" | custom-call | tf_op jit(solution)/shard_map/jit(cholesky)/cholesky | solution.py:56
  610.4 8.6 select_select_fusion
  619.0 43.1 %while.1 = (s32[]{:T(128)}, f32[1536,1536]{1,0:T(8,128)}, s32[12,2]{0,1:T(2,128)S(1)}, f32[12,128,128]{2,1,0:T(8,128)}, s32[]{:T(128)}) while((s32[]{:T(128)}, f32[1536,1536]{1,0:T(8,128)}, s32[12,2]{0,1:T(2,128)S(1)}, f32[12,128,128]{2,1,0:T(8,128)}, s32[]{:T(128)}) %tuple.111), condition=%wide.while_cond, body=%wide.while_body.sunk | while | flops 2 | bytes 132205 | solution.py:14
  619.7 2.9 bitcast_dynamic-update-slice_fusion.2
  623.3 2.9 bitcast_dynamic-update-slice_fusion.2
  626.9 2.9 bitcast_dynamic-update-slice_fusion.2
  630.5 2.9 bitcast_dynamic-update-slice_fusion.2
  634.0 2.9 bitcast_dynamic-update-slice_fusion.2
  637.6 2.9 bitcast_dynamic-update-slice_fusion.2
  641.2 2.9 bitcast_dynamic-update-slice_fusion.2
  644.8 2.9 bitcast_dynamic-update-slice_fusion.2
  648.4 2.9 bitcast_dynamic-update-slice_fusion.2
  652.0 2.9 bitcast_dynamic-update-slice_fusion.2
  655.6 2.9 bitcast_dynamic-update-slice_fusion.2
  662.1 119.7 %custom-call.105 = f32[12,128,128]{1,2,0:T(8,128)} custom-call(f32[12,128,128]{2,1,0:T(8,128)} %get-tuple-element.10), custom_call_target="InvertDiagBlocksLowerTriangular" | custom-call | tf_op jit(solution)/shard_map/triangular_solve | solution.py:14
  809.2 3.1 convolution_subtract_fusion.12
  815.8 76.7 %all-gather.16.cloned.1.call-done = bf16[1536,1536]{1,0:T(8,128)(2,1)} async-done(((bf16[192,1536]{1,0:T(8,128)(2,1)}), bf16[1536,1536]{1,0:T(8,128)(2,1)}) %all-gather.16.cloned.1.call-update) | async-done | bytes 4718608 | tf_op jit(solution)/shard_map/all_gather | solution.py:30
  892.5 5.0 fusion.132
  899.0 73.1 %all-gather.8.cloned.1.call-done = bf16[1536,1536]{1,0:T(8,128)(2,1)} async-done(((bf16[192,1536]{1,0:T(8,128)(2,1)}), bf16[1536,1536]{1,0:T(8,128)(2,1)}) %all-gather.8.cloned.1.call-update) | async-done | bytes 4718608 | tf_op jit(solution)/shard_map/all_gather | solution.py:29
  972.1 5.2 fusion.138
  978.4 5.7 psum.7
  984.7 5.0 fusion.8
  989.7 62.1 %all-gather.14.cloned.1.call-done = bf16[1536,1536]{1,0:T(8,128)(2,1)} async-done(((bf16[192,1536]{1,0:T(8,128)(2,1)}), bf16[1536,1536]{1,0:T(8,128)(2,1)}) %all-gather.14.cloned.1.call-update) | async-done | bytes 4718608 | tf_op jit(solution)/shard_map/all_gather | solution.py:29
  1051.8 5.4 fusion.10
  (140 shorter events, 92.6 us)
Async XLA Ops:
  7.2 85.0 %all-gather.18.cloned.1.call-start = ((), (), s32[]{:S(2)}) async-start(), calls=%async_computation.5 | async-start | bytes 5308416 | tf_op jit(solution)/shard_map/all_gather | solution.py:24
  7.9 167.6 %all-gather.10.cloned.1.call-start = ((), (), s32[]{:S(2)}) async-start(), calls=%async_computation.1 | async-start | bytes 5308416 | tf_op jit(solution)/shard_map/all_gather | solution.py:30
  96.5 91.5 %copy-start.4 = (bf16[384,1536]{1,0:T(8,128)(2,1)}, bf16[384,1536]{1,0:T(8,128)(2,1)S(1)}, u32[]{:S(2)}) copy-start(bf16[384,1536]{1,0:T(8,128)(2,1)S(1)} %fusion.5) | copy-start | bytes 3538948
  96.5 79.0 %copy-start.8 = (bf16[1,192,1536]{2,1,0:T(8,128)(2,1)S(1)}, bf16[1,192,1536]{2,1,0:T(8,128)(2,1)}, u32[]{:S(2)}) copy-start(bf16[1,192,1536]{2,1,0:T(8,128)(2,1)} %param.6) | copy-start | bytes 1769476
  97.7 82.8 %copy-start.6 = (f32[1,2,8,1536]{3,2,1,0:T(8,128)S(1)}, f32[1,2,8,1536]{3,2,1,0:T(8,128)}, u32[]{:S(2)}) copy-start(f32[1,2,8,1536]{3,2,1,0:T(8,128)} %param.8) | copy-start | bytes 294916
  97.7 160.5 %all-gather.12.cloned.1.call-start = ((), (), s32[]{:S(2)}) async-start(), calls=%async_computation.2 | async-start | bytes 5308416 | tf_op jit(solution)/shard_map/all_gather | solution.py:24
  180.4 712.1 %all-gather.16.cloned.1.call-start = ((), (), s32[]{:S(2)}) async-start(), calls=%async_computation.4 | async-start | bytes 5308416 | tf_op jit(solution)/shard_map/all_gather | solution.py:30
  180.4 6.2 copy-start.2
  279.3 3.6 copy-start
  610.4 171.4 %copy-start.1 = (f32[392,1536]{1,0:T(8,128)S(1)}, f32[392,1536]{1,0:T(8,128)}, u32[]{:S(2)}) copy-start(f32[392,1536]{1,0:T(8,128)} %pad_maximum_fusion) | copy-start | bytes 7225348
  781.8 2.8 copy-start.5
  812.8 1.8 copy-start.3
  814.6 157.5 %all-gather.8.cloned.1.call-start = ((), (), s32[]{:S(2)}) async-start(), calls=%async_computation | async-start | bytes 5308416 | tf_op jit(solution)/shard_map/all_gather | solution.py:29
  815.2 236.6 %all-gather.14.cloned.1.call-start = ((), (), s32[]{:S(2)}) async-start(), calls=%async_computation.3 | async-start | bytes 5308416 | tf_op jit(solution)/shard_map/all_gather | solution.py:29
  897.5 154.3 %collective-permute-start = (f32[192,1536]{1,0:T(8,128)}, f32[192,1536]{1,0:T(8,128)S(1)}, u32[]{:S(2)}, u32[]{:S(2)}) collective-permute-start(f32[192,1536]{1,0:T(8,128)} %fusion.132), channel_id=1, source_target_pairs={{0,8},{8,16},{16,24},{1,9},{9,17},{17,25},{2,10},{10,18},{18,26},{... | collective-permute-start | bytes 3538952 | tf_op jit(solution)/shard_map/ppermute | solution.py:10
  899.0 85.1 %copy-start.7 = (f32[8,8]{1,0:T(8,128)S(1)}, f32[8,8]{1,0:T(8,128)}, u32[]{:S(2)}) copy-start(f32[8,8]{1,0:T(8,128)} %param.9) | copy-start | bytes 772
Sparse Core Ops, SparseCore 0:
  10.1 82.0 all-gather.17
  97.8 77.6 all-gather.9
  180.5 77.6 all-gather.11
  814.7 77.6 all-gather.15
  894.4 77.6 all-gather.7
  974.1 77.6 all-gather.13
where the time goes:
time: 1070 us; the launch traced here: 1060 us
  waiting for transfers between devices  441 us (41%)
  other arithmetic  403 us (38%)
  matrix products  121 us (11%)
  local copies, waits for them, and re-layouts  68.9 us (6%)
  between operations  22.4 us (2%)
    another operation x46, other arithmetic, shards(): factor_two = jnp.linalg.cholesky(second_ready.astype(jnp.float32))  265 us
    all_gather x2, waiting for transfers between devices, spread_panels(): lax.all_gather(second_panel, ('row', 'col'), axis=0, tiled=True)  154 us
    all_gather x2, waiting for transfers between devices, gather_block(): return lax.all_gather(one_share, ('row', 'col'), axis=0, tiled=True)  150 us
    all_gather x2, waiting for transfers between devices, spread_panels(): lax.all_gather(first_panel, ('row', 'col'), axis=0, tiled=True)  135 us
    another operation x3, other arithmetic, right_solve(): lax.linalg.triangular_solve(factor, rhs_rows, left_side=False, lower=True...  128 us
    another operation x22, matrix products, shards(): factor_two = jnp.linalg.cholesky(second_ready.astype(jnp.float32))  50.1 us
    another operation x36, local copies, waits for them, and re-layouts  43 us
    dot_general x8, matrix products, outer_rows(): jnp.einsum('ik,jk->ij', left_rows, right_rows, preferred_element_type=jnp...  32.9 us
  transfers between devices with their start and end apart: 7, of which 6 were waited for; matrix products, arithmetic and copies ran while one was open for 3% of the time, Pallas kernels for 0%

commit v1 on v0

v1 whole, which is shorter than its diff:
```python
import functools
import jax
import jax.numpy as jnp
from jax import lax
from jax.experimental import pallas as pl
from jax.experimental.pallas import tpu as pltpu
from jax.sharding import PartitionSpec as P

F32, BF16 = jnp.float32, jnp.bfloat16
NT = (((1,), (1,)), ((), ()))
NN = (((1,), (0,)), ((), ()))

def mm(a, b, dims=NN):
    return lax.dot_general(a, b, dims, preferred_element_type=F32)

def split(a):
    hi = a.astype(BF16)
    return hi, (a - hi.astype(F32)).astype(BF16)

def mm3(a, b):
    return mm(a[0], b[0]) + (mm(a[0], b[1]) + mm(a[1], b[0]))

def spd_inverse(block, quick):
    size = block.shape[0]
    eye = (lax.broadcasted_iota(jnp.int32, (size, size), 0)
           == lax.broadcasted_iota(jnp.int32, (size, size), 1)).astype(F32)
    start = eye / jnp.sum(jnp.abs(block), axis=0, keepdims=True)
    parts = split(block)
    guess = start
    for _ in range(quick):
        short = guess.astype(BF16)
        guess = 2.0 * guess - mm(short, mm(parts[0], short).astype(BF16))
    def gap_of(x):
        gap = eye - mm3(parts, split(x))
        return gap, jnp.max(jnp.sum(jnp.abs(gap), axis=0, keepdims=True))
    gap, worst = gap_of(guess)
    good = worst < 0.5
    guess = jnp.where(good, guess, start)
    def go(state):
        turn, worst, _ = state
        return jnp.logical_and(turn < 60, worst > 2e-2)
    def step(state):
        turn, worst, x = state
        gap, _ = gap_of(x)
        x = x + mm3(split(x), split(gap))
        _, worst = gap_of(x)
        return turn + 1, worst, x
    _, _, guess = lax.while_loop(go, step, (0, jnp.where(good, worst, 1.0), guess))
    gap, _ = gap_of(guess)
    return guess + mm3(split(guess), split(gap))

def eliminate_kernel(size, quick, s_in, r_in, g_ref, s_ref, r_ref, low_ref):
    n = s_in.shape[0]
    nb = n // size
    s_ref[...] = s_in[...]
    r_ref[...] = r_in[...]
    at = lambda k: pl.ds(k * size, size)
    for k in range(nb):
        inverse = spd_inverse(s_ref[at(k), at(k)], quick).astype(BF16)
        row = r_ref[:, at(k)].astype(BF16)
        g_ref[:, at(k)] = mm(row, inverse)
        for j in range(k + 1, nb):
            low_ref[at(j), at(k)] = mm(s_ref[at(j), at(k)].astype(BF16), inverse).astype(BF16)
        for j in range(k + 1, nb):
            low = low_ref[at(j), at(k)]
            r_ref[:, at(j)] -= mm(row, low, NT)
            for i in range(j, nb):
                s_ref[at(i), at(j)] -= mm(s_ref[at(i), at(k)].astype(BF16), low, NT)
    for k in range(nb - 2, -1, -1):
        rest = pl.ds((k + 1) * size, n - (k + 1) * size)
        g_ref[:, at(k)] -= mm(g_ref[:, rest].astype(BF16), low_ref[rest, at(k)])

def eliminate(block, rows, size=256, quick=4):
    n, r = block.shape[0], rows.shape[0]
    v = pl.BlockSpec(memory_space=pltpu.VMEM)
    return pl.pallas_call(
        functools.partial(eliminate_kernel, size, quick),
        out_shape=jax.ShapeDtypeStruct((r, n), F32),
        in_specs=[v, v], out_specs=v,
        scratch_shapes=[pltpu.VMEM((n, n), F32), pltpu.VMEM((r, n), F32), pltpu.VMEM((n, n), BF16)],
        compiler_params=pltpu.CompilerParams(vmem_limit_bytes=60 << 20),
        cost_estimate=pl.CostEstimate(flops=2 * n**3, bytes_accessed=4 * n * n + 8 * n * r, transcendentals=0),
        name="eliminate",
    )(block, rows)


def from_behind(block, axis, distance):
    devices = range(lax.axis_size(axis))
    route = [(i - distance, i) for i in devices if i - distance in devices]
    return lax.ppermute(block, axis, route)


def gather_block(one_share):
    return lax.all_gather(one_share, ("row", "col"), axis=0, tiled=True)


def shards(first_inverse, second_diag, coupling, arrow_rows, tip_block):
    share, n = coupling.shape[2:]
    size = 256 if n % 256 == 0 else 128
    top_share, mid_share, low_share = (coupling[0, i] for i in range(3))
    inverse = gather_block(first_inverse[0])
    mid_rhs = gather_block(mid_share)
    diag = gather_block(second_diag[0])
    top_rhs = gather_block(top_share)
    low_rhs = gather_block(low_share)
    mid = mm(mid_rhs, inverse, NT).astype(BF16)
    top_own = mm(top_share, inverse, NT).astype(BF16)
    arrow_one = jnp.einsum(
        "ik,jk->ij", arrow_rows[0, 0], inverse.astype(F32), precision=lax.Precision.HIGHEST
    )
    block = diag.astype(F32) - mm(mid, mid, NT)
    fill_rows = -mm(top_own, mid, NT)
    arrow_two_rows = arrow_rows[0, 1] - mm(arrow_one.astype(BF16), mid, NT)
    rows = jnp.concatenate([fill_rows, low_share.astype(F32), arrow_two_rows], axis=0)
    solved = eliminate(block, rows, size)
    upper = solved[:share].astype(BF16)
    lower = solved[share : 2 * share].astype(BF16)
    left = (top_own.astype(F32) - mm(upper, mid)).astype(BF16)
    own_update = mm(mm(left, inverse).astype(BF16), top_rhs, NT)
    fill_block = -mm(upper, low_rhs, NT)
    handed = mm(lower, low_rhs, NT)
    tip_terms = jnp.einsum("ik,jk->ij", arrow_one, arrow_one, precision=lax.Precision.HIGHEST)
    tip_terms += jnp.einsum(
        "ik,jk->ij", solved[2 * share :], arrow_two_rows, precision=lax.Precision.HIGHEST
    )
    incoming = from_behind(handed, "tm", 1)
    tip_total = lax.psum(tip_terms, "tm")
    return ((own_update + incoming)[None], fill_block[None], tip_block - tip_total)


def solution(mesh):
    return jax.shard_map(
        shards,
        mesh=mesh,
        in_specs=(
            P("tm", ("row", "col"), None),
            P("tm", ("row", "col"), None),
            P("tm", None, ("row", "col"), None),
            P("tm", None, None, None),
            P(),
        ),
        out_specs=(P("tm", ("row", "col"), None), P("tm", ("row", "col"), None), P()),
        check_vma=False,
    )
```

time: 1070 us -> 424 us (0.40)
  other arithmetic: 403 us -> 6.69 us
  waiting for transfers between devices: 441 us -> 295 us
  local copies, waits for them, and re-layouts: 68.9 us -> 2.75 us
  matrix products: 121 us -> 60.2 us
  Pallas kernels: 0 us -> 35.5 us
    another operation x50 -> x1, other arithmetic: 393 us -> 1.81 us  [the longest x46 265 us: shards(): factor_two = jnp.linalg.cholesky(second_ready.astype(jnp.float32))]
    all_gather x4 -> x0, waiting for transfers between devices: 290 us -> none  [the longest x2 154 us: spread_panels(): lax.all_gather(second_panel, ('row', 'col'), axis=0, tiled=True)]
    all_gather x2 -> x5, waiting for transfers between devices: 150 us -> 292 us  [gather_block(): return lax.all_gather(one_share, ('row', 'col'), axis=0, tiled=True)]
    another operation x45 -> x0, matrix products: 81 us -> none  [the longest x22 50.1 us: shards(): factor_two = jnp.linalg.cholesky(second_ready.astype(jnp.float32))]
    another operation x49 -> x0, local copies, waits for them, and re-layouts: 48 us -> none
    pallas_call x0 -> x1, Pallas kernels: none -> 35.5 us  [eliminate(): pl.pallas_call(functools.partial(eliminate_kernel, size, quick), out_shap...]
    dot_general x10 -> x11, matrix products: 40.2 us -> 60 us  [the longest x9 52.8 us: mm(): return lax.dot_general(a, b, dims, preferred_element_type=F32)]
  transfers between devices with their start and end apart: 7 -> 6, of which waited for: 6 -> 5; matrix products, arithmetic and copies ran while one was open for 3% -> 15% of each run, Pallas kernels for 0% -> 8%
where the time goes in v1:
time: 424 us
  waiting for transfers between devices  295 us (70%)
  matrix products  60.2 us (14%)
  Pallas kernels  35.5 us (8%)
  between operations  13.9 us (3%)
  blocking collectives  8.74 us (2%)
  other arithmetic  6.69 us (2%)
    all_gather x5, waiting for transfers between devices, gather_block(): return lax.all_gather(one_share, ('row', 'col'), axis=0, tiled=True)  292 us
    dot_general x9, matrix products, mm(): return lax.dot_general(a, b, dims, preferred_element_type=F32)  52.8 us
    pallas_call x1, Pallas kernels, eliminate(): pl.pallas_call(functools.partial(eliminate_kernel, size, quick), out_shap...  35.5 us
    psum x1, blocking collectives, shards(): tip_total = lax.psum(tip_terms, 'tm')  8.74 us
  transfers between devices with their start and end apart: 6, of which 5 were waited for; matrix products, arithmetic and copies ran while one was open for 15% of the time, Pallas kernels for 8%

profile of v1, /device:TPU:0, one launch (start us, length us, event | category | flops | bytes accessed | tf_op | source)
XLA Modules:
  0.0 424.0 jit_solution(15836564737299807215)
XLA Ops:
  7.2 0.0 copy-start.2
  7.2 0.0 all-gather.11.cloned.1.call-start
  7.2 0.7 all-gather.11.cloned.1.call-update
  7.9 0.0 all-gather.15.cloned.1.call-start
  8.0 2.7 fusion.43
  10.6 0.0 all-gather.15.cloned.1.call-update
  10.7 0.0 all-gather.13.cloned.1.call-start
  10.7 0.7 all-gather.13.cloned.1.call-update
  11.4 0.0 all-gather.19.cloned.1.call-start
  11.5 0.5 all-gather.19.cloned.1.call-update
  12.0 0.0 all-gather.17.cloned.1.call-start
  12.0 0.5 all-gather.17.cloned.1.call-update
  12.6 79.6 %all-gather.11.cloned.1.call-done = bf16[1,1536,1536]{2,1,0:T(8,128)(2,1)} async-done(((bf16[1,192,1536]{2,1,0:T(8,128)(2,1)}), bf16[1,1536,1536]{2,1,0:T(8,128)(2,1)}) %all-gather.11.cloned.1.call-update) | async-done | bytes 4718608 | tf_op jit(solution)/shard_map/all_gather | solution.py:94
  92.2 0.0 copy-done.2
  92.2 6.1 %fusion.9 = f32[8,1536]{1,0:T(8,128)S(1)} fusion(bf16[1,1536,1536]{2,1,0:T(8,128)(2,1)} %all-gather.11.cloned.1.call-done, f32[1,2,8,1536]{3,2,1,0:T(8,128)S(1)} %copy-done.2), kind=kOutput, calls=%fused_computation.11 | convolution fusion | flops 226492416 | bytes 4816896 | tf_op jit(solution)/shard_map/ik,jk->ij/dot_general | solution.py:108
  98.3 74.3 %all-gather.15.cloned.1.call-done = bf16[1,1,1536,1536]{3,2,1,0:T(8,128)(2,1)} async-done(((bf16[1,1,192,1536]{3,2,1,0:T(8,128)(2,1)}), bf16[1,1,1536,1536]{3,2,1,0:T(8,128)(2,1)}) %all-gather.15.cloned.1.call-update) | async-done | bytes 4718608 | tf_op jit(solution)/shard_map/all_gather | solution.py:94
  172.6 10.8 %convolution_convert_fusion = bf16[1536,1536]{1,0:T(8,128)(2,1)S(1)} fusion(bf16[1,1,1536,1536]{3,2,1,0:T(8,128)(2,1)} %all-gather.15.cloned.1.call-done, bf16[1,1536,1536]{2,1,0:T(8,128)(2,1)} %all-gather.11.cloned.1.call-done), kind=kOutput, calls=%fused_computation.1 | convolution fusion | flops 7250116608 | bytes 14155776 | tf_op jit(solution)/shard_map/dot_general | solution.py:14
  183.4 0.0 copy-start.1
  183.4 0.0 copy-start
  183.4 1.3 convolution_subtract_fusion.1
  184.7 2.7 copy-done
  187.5 2.7 fusion.26
  190.2 0.0 copy-done.1
  190.2 0.0 copy-start.4
  190.2 1.7 convolution_negate_fusion
  191.9 0.0 copy-done.4
  191.9 1.6 pad_maximum_fusion.r_in
  193.5 59.0 %all-gather.13.cloned.1.call-done = bf16[1,1536,1536]{2,1,0:T(8,128)(2,1)} async-done(((bf16[1,192,1536]{2,1,0:T(8,128)(2,1)}), bf16[1,1536,1536]{2,1,0:T(8,128)(2,1)}) %all-gather.13.cloned.1.call-update) | async-done | bytes 4718608 | tf_op jit(solution)/shard_map/all_gather | solution.py:94
  252.5 15.2 %convert_subtract_fusion.s_in = f32[1536,1536]{1,0:T(8,128)} fusion(bf16[1536,1536]{1,0:T(8,128)(2,1)} %copy-done.1, bf16[1,1536,1536]{2,1,0:T(8,128)(2,1)} %all-gather.13.cloned.1.call-done), kind=kOutput, calls=%fused_computation | convolution fusion | flops 7252475904 | bytes 18874368 | tf_op jit(solution)/shard_map/dot_general | solution.py:14
  267.7 35.5 %eliminate.1 = f32[392,1536]{1,0:T(8,128)} custom-call(f32[1536,1536]{1,0:T(8,128)} %convert_subtract_fusion.s_in, f32[392,1536]{1,0:T(8,128)} %pad_maximum_fusion.r_in), custom_call_target="tpu_custom_call" | custom-call | flops 7247757312 | bytes 14254080 | tf_op jit(solution)/shard_map/eliminate/pallas_call | solution.py:76
  303.2 1.8 convert.4
  305.0 0.0 copy-start.3
  305.0 27.7 %all-gather.19.cloned.1.call-done = bf16[1,1,1536,1536]{3,2,1,0:T(8,128)(2,1)} async-done(((bf16[1,1,192,1536]{3,2,1,0:T(8,128)(2,1)}), bf16[1,1,1536,1536]{3,2,1,0:T(8,128)(2,1)}) %all-gather.19.cloned.1.call-update) | async-done | bytes 4718608 | tf_op jit(solution)/shard_map/all_gather | solution.py:94
  332.7 5.0 %fusion.2 = f32[192,1536]{1,0:T(8,128)} fusion(bf16[1,1,1536,1536]{3,2,1,0:T(8,128)(2,1)} %all-gather.19.cloned.1.call-done, bf16[392,1536]{1,0:T(8,128)(2,1)S(1)} %convert.4), kind=kOutput, calls=%fused_computation.4 | convolution fusion | flops 905969664 | bytes 6488064 | tf_op jit(solution)/shard_map/dot_general | solution.py:14
  337.7 1.4 collective-permute-start
  339.1 0.2 fusion.44
  339.3 1.1 convolution_add_fusion
  340.3 8.7 %psum.7 = f32[8,8]{1,0:T(8,128)S(1)} all-reduce(f32[8,8]{1,0:T(8,128)S(1)} %convolution_add_fusion), channel_id=1, replica_groups=mesh['tm'=4,'row'=2,'col'=4] {'tm'}, use_global_device_ids=true, to_apply=%region_0.0 | all-reduce | flops 64 | bytes 512 | tf_op jit(solution)/shard_map/psum | solution.py:127
  349.1 0.0 copy-done.3
  349.1 0.6 sub.15
  349.7 5.0 %fusion.17 = f32[1,192,1536]{2,1,0:T(8,128)} fusion(bf16[1,1,1536,1536]{3,2,1,0:T(8,128)(2,1)} %all-gather.19.cloned.1.call-done, bf16[392,1536]{1,0:T(8,128)(2,1)S(1)} %convert.4), kind=kOutput, calls=%fused_computation.17 | convolution fusion | flops 906264576 | bytes 6488064 | tf_op jit(solution)/shard_map/dot_general | solution.py:14
  354.7 6.0 %fusion.29 = bf16[192,1536]{1,0:T(8,128)(2,1)S(1)} fusion(bf16[1,1536,1536]{2,1,0:T(8,128)(2,1)} %all-gather.11.cloned.1.call-done, bf16[1536,1536]{1,0:T(8,128)(2,1)} %copy-done.1, bf16[192,1536]{1,0:T(8,128)(2,1)} %copy-done.4, bf16[392,1536]{1,0:T(8,128)(2,1)S(1)} %convert.4), kind=kOutput, calls=%fused_computation.23 | convolution fusion | flops 1813118976 | bytes 11206656 | tf_op jit(solution)/shard_map/dot_general | solution.py:14
  360.7 51.7 %all-gather.17.cloned.1.call-done = bf16[1,1,1536,1536]{3,2,1,0:T(8,128)(2,1)} async-done(((bf16[1,1,192,1536]{3,2,1,0:T(8,128)(2,1)}), bf16[1,1,1536,1536]{3,2,1,0:T(8,128)(2,1)}) %all-gather.17.cloned.1.call-update) | async-done | bytes 4718608 | tf_op jit(solution)/shard_map/all_gather | solution.py:94
  412.4 0.0 collective-permute-done
  412.4 5.0 %fusion.23 = f32[1,192,1536]{2,1,0:T(8,128)} fusion(f32[192,1536]{1,0:T(8,128)S(1)} %collective-permute-done, bf16[192,1536]{1,0:T(8,128)(2,1)S(1)} %fusion.29, bf16[1,1,1536,1536]{3,2,1,0:T(8,128)(2,1)} %all-gather.17.cloned.1.call-done), kind=kOutput, calls=%fused_computation.20 | convolution fusion | flops 906264576 | bytes 7667712 | tf_op jit(solution)/shard_map/dot_general | solution.py:14
Async XLA Ops:
  7.2 85.0 %copy-start.2 = (f32[1,2,8,1536]{3,2,1,0:T(8,128)S(1)}, f32[1,2,8,1536]{3,2,1,0:T(8,128)}, u32[]{:S(2)}) copy-start(f32[1,2,8,1536]{3,2,1,0:T(8,128)} %param.8) | copy-start | bytes 294916
  7.2 85.0 %all-gather.11.cloned.1.call-start = ((), (), s32[]{:S(2)}) async-start(), calls=%async_computation | async-start | bytes 5308416 | tf_op jit(solution)/shard_map/all_gather | solution.py:94
  7.9 164.7 %all-gather.15.cloned.1.call-start = ((), (), s32[]{:S(2)}) async-start(), calls=%async_computation.2 | async-start | bytes 5308416 | tf_op jit(solution)/shard_map/all_gather | solution.py:94
  10.7 241.8 %all-gather.13.cloned.1.call-start = ((), (), s32[]{:S(2)}) async-start(), calls=%async_computation.1 | async-start | bytes 5308416 | tf_op jit(solution)/shard_map/all_gather | solution.py:94
  11.4 321.3 %all-gather.19.cloned.1.call-start = ((), (), s32[]{:S(2)}) async-start(), calls=%async_computation.4 | async-start | bytes 5308416 | tf_op jit(solution)/shard_map/all_gather | solution.py:94
  12.0 400.4 %all-gather.17.cloned.1.call-start = ((), (), s32[]{:S(2)}) async-start(), calls=%async_computation.3 | async-start | bytes 5308416 | tf_op jit(solution)/shard_map/all_gather | solution.py:94
  183.4 6.8 %copy-start.1 = (bf16[1536,1536]{1,0:T(8,128)(2,1)}, bf16[1536,1536]{1,0:T(8,128)(2,1)S(1)}, u32[]{:S(2)}) copy-start(bf16[1536,1536]{1,0:T(8,128)(2,1)S(1)} %convolution_convert_fusion) | copy-start | bytes 14155780
  183.4 4.1 copy-start
  190.2 1.7 copy-start.4
  305.0 44.1 %copy-start.3 = (f32[8,8]{1,0:T(8,128)S(1)}, f32[8,8]{1,0:T(8,128)}, u32[]{:S(2)}) copy-start(f32[8,8]{1,0:T(8,128)} %param.9) | copy-start | bytes 772
  337.7 74.7 %collective-permute-start = (f32[192,1536]{1,0:T(8,128)}, f32[192,1536]{1,0:T(8,128)S(1)}, u32[]{:S(2)}, u32[]{:S(2)}) collective-permute-start(f32[192,1536]{1,0:T(8,128)} %fusion.2), channel_id=1, source_target_pairs={{0,8},{8,16},{16,24},{1,9},{9,17},{17,25},{2,10},{10,18},{18,26},{... | collective-permute-start | bytes 3538952 | tf_op jit(solution)/shard_map/ppermute | solution.py:90
Sparse Core Ops, SparseCore 0:
  10.1 82.0 all-gather.10
  94.8 77.6 all-gather.14
  174.7 77.7 all-gather.12
  255.0 77.6 all-gather.18
  334.6 77.7 all-gather.16

commit v2 on v1

--- a/solution.py
+++ b/solution.py
@@ -84,48 +84,144 @@
     )(block, rows)
 
 
-def from_behind(block, axis, distance):
-    devices = range(lax.axis_size(axis))
-    route = [(i - distance, i) for i in devices if i - distance in devices]
-    return lax.ppermute(block, axis, route)
-
-
-def gather_block(one_share):
-    return lax.all_gather(one_share, ("row", "col"), axis=0, tiled=True)
+AXES = ("tm", "row", "col")
+
+
+def places():
+    tms, rows, cols = (lax.axis_size(a) for a in AXES)
+    flat = lambda t, r, c: (t * rows + r) * cols + c
+    return [(t, r, c) for t in range(tms) for r in range(rows) for c in range(cols)], flat, rows, cols
+
+
+def move(block, target):
+    devices, flat, _, _ = places()
+    route = [(flat(*d), flat(*target(*d))) for d in devices if target(*d) is not None]
+    return lax.ppermute(block, AXES, route)
+
+
+def swapped(t, r, c):
+    half = lax.axis_size("col") // 2
+    if t % 2 == c // half:
+        return t, r, c
+    return t ^ 1, r, (c + half) % (2 * half)
+
+
+def along(axis, step):
+    def target(t, r, c):
+        rows, half = lax.axis_size("row"), lax.axis_size("col") // 2
+        if axis == "core":
+            return t ^ 1, r, c
+        if axis == "row":
+            return t, (r + step) % rows, c
+        return t, r, c // half * half + (c % half + step) % half
+    return target
+
+
+def after(value, *others):
+    return lax.optimization_barrier((value, *others))[0]
+
+
+def spread(own):
+    rows, half = lax.axis_size("row"), lax.axis_size("col") // 2
+    if rows == 2 and half == 2:
+        by_row = move(own, along("row", 1))
+        by_col = move(own, along("col", 1))
+        cut = own.shape[0] * 3 // 4 // 16 * 16
+        first = move(by_col[:cut], along("row", 1))
+        second = move(by_row[cut:], along("col", 1))
+        return [(0, 0, 0, own), (1, 0, 0, by_row), (0, 1, 0, by_col), (1, 1, 0, first), (1, 1, cut, second)]
+    return None
+
+
+def groups():
+    devices, flat, rows, cols = places()
+    half = cols // 2
+    return [
+        [flat(2 * x + core, r, h * half + c) for r in range(rows) for core in range(2) for c in range(half)]
+        for x in range(lax.axis_size("tm") // 2)
+        for h in range(2)
+    ]
+
+
+def gather(own, natural):
+    share = own.shape[0]
+    rows, cols = lax.axis_size("row"), lax.axis_size("col")
+    half = cols // 2
+    pieces = spread(own)
+    if pieces is None:
+        return lax.all_gather(own, AXES, axis=0, tiled=True, axis_index_groups=groups())
+    pieces = [(0, *p) for p in pieces]
+    pieces += [(1, j, i, k, move(block, along("core", 1))) for _, j, i, k, block in pieces]
+    if not natural:
+        return jnp.concatenate([p[-1] for p in pieces], axis=0)
+    core = lax.axis_index("tm") % 2
+    row, col = lax.axis_index("row"), lax.axis_index("col") % half
+    whole = jnp.zeros((share * rows * cols,) + own.shape[1:], own.dtype)
+    for s, j, i, k, block in pieces:
+        index = ((row - j) % rows * 2 + (core - s) % 2) * half + (col - i) % half
+        whole = lax.dynamic_update_slice(whole, block, (index * share + k, 0))
+    return whole
+
+
+def handed_to(t, r, c):
+    tms, half = lax.axis_size("tm"), lax.axis_size("col") // 2
+    part = t // 2 * 2 + c // half + 1
+    return None if part >= tms else (part, r, c % half + t % 2 * half)
+
+
+def thin(rows):
+    terms = []
+    for _ in range(3):
+        terms.append(rows.astype(BF16))
+        rows = rows - terms[-1].astype(F32)
+    return jnp.concatenate(terms, axis=0)
 
 
 def shards(first_inverse, second_diag, coupling, arrow_rows, tip_block):
     share, n = coupling.shape[2:]
     size = 256 if n % 256 == 0 else 128
-    top_share, mid_share, low_share = (coupling[0, i] for i in range(3))
-    inverse = gather_block(first_inverse[0])
-    mid_rhs = gather_block(mid_share)
-    diag = gather_block(second_diag[0])
-    top_rhs = gather_block(top_share)
-    low_rhs = gather_block(low_share)
+    half = lax.axis_size("col") // 2
+    core, col = lax.axis_index("tm") % 2, lax.axis_index("col")
+    stays = core == col // half
+    arrows = move(arrow_rows[0], swapped)
+    inverse_own = move(first_inverse[0], swapped)
+    mid_share = move(after(coupling[0, 1], inverse_own), swapped)
+    inverse = gather(inverse_own, False)
+    diag_share = move(after(second_diag[0], mid_share), swapped)
+    mid_rhs = gather(mid_share, True)
+    low_share = move(after(coupling[0, 2], diag_share), swapped)
+    diag = gather(diag_share, True)
+    top_share = move(after(coupling[0, 0], low_share), swapped)
+    low_rhs = gather(low_share, True)
+    top_rhs = gather(top_share, True)
+
     mid = mm(mid_rhs, inverse, NT).astype(BF16)
+    fixed = arrows.shape[1]
+    thin_one = mm(thin(arrows[0]), inverse, NT)
+    arrow_one = thin_one[:fixed] + thin_one[fixed : 2 * fixed] + thin_one[2 * fixed :]
     top_own = mm(top_share, inverse, NT).astype(BF16)
-    arrow_one = jnp.einsum(
-        "ik,jk->ij", arrow_rows[0, 0], inverse.astype(F32), precision=lax.Precision.HIGHEST
-    )
     block = diag.astype(F32) - mm(mid, mid, NT)
     fill_rows = -mm(top_own, mid, NT)
-    arrow_two_rows = arrow_rows[0, 1] - mm(arrow_one.astype(BF16), mid, NT)
+    arrow_two_rows = arrows[1] - mm(arrow_one.astype(BF16), mid, NT)
     rows = jnp.concatenate([fill_rows, low_share.astype(F32), arrow_two_rows], axis=0)
     solved = eliminate(block, rows, size)
     upper = solved[:share].astype(BF16)
     lower = solved[share : 2 * share].astype(BF16)
+    incoming = move(mm(lower, low_rhs, NT).astype(BF16), handed_to)
+    fill_block = -mm(upper, low_rhs, NT)
+    fill_far = move(fill_block.astype(BF16), swapped)
     left = (top_own.astype(F32) - mm(upper, mid)).astype(BF16)
     own_update = mm(mm(left, inverse).astype(BF16), top_rhs, NT)
-    fill_block = -mm(upper, low_rhs, NT)
-    handed = mm(lower, low_rhs, NT)
+    far_update = move(own_update.astype(BF16), swapped)
     tip_terms = jnp.einsum("ik,jk->ij", arrow_one, arrow_one, precision=lax.Precision.HIGHEST)
     tip_terms += jnp.einsum(
         "ik,jk->ij", solved[2 * share :], arrow_two_rows, precision=lax.Precision.HIGHEST
     )
-    incoming = from_behind(handed, "tm", 1)
-    tip_total = lax.psum(tip_terms, "tm")
-    return ((own_update + incoming)[None], fill_block[None], tip_block - tip_total)
+    speaks = jnp.logical_and(stays, col % half == 0)
+    tip_total = lax.psum(jnp.where(speaks, tip_terms, 0.0), ("tm", "col"))
+    fill_block = jnp.where(stays, fill_block, fill_far.astype(F32))
+    update = jnp.where(stays, own_update, far_update.astype(F32)) + incoming.astype(F32)
+    return (update[None], fill_block[None], tip_block - tip_total)
 
 
 def solution(mesh):

time: 424 us -> 312 us (0.74); the launches traced: 424 us -> 307 us
  waiting for transfers between devices: 295 us -> 43.3 us
  starting transfers between devices: 1.55 us -> 103 us
  blocking collectives: 8.74 us -> 44.3 us
  local copies, waits for them, and re-layouts: 2.75 us -> 26 us
  matrix products: 60.2 us -> 44.7 us
  between operations: 13.9 us -> 1.92 us
    all_gather x5 -> x0, waiting for transfers between devices: 292 us -> none  [gather_block(): return lax.all_gather(one_share, ('row', 'col'), axis=0, tiled=True)]
    ppermute x1 -> x54, starting transfers between devices: 1.35 us -> 103 us  [move(): return lax.ppermute(block, AXES, route)]
    ppermute x1 -> x54, waiting for transfers between devices: 0.01 us -> 43.3 us  [move(): return lax.ppermute(block, AXES, route)]
    psum x1, blocking collectives: 8.74 us -> 44.3 us  [shards(): tip_total = lax.psum(jnp.where(speaks, tip_terms, 0.0), ('tm', 'col'))]
    dynamic_update_slice x0 -> x39, local copies, waits for them, and re-layouts: none -> 18.8 us  [gather(): whole = lax.dynamic_update_slice(whole, block, (index * share + k, 0))]
    dot_general x9 -> x10, matrix products: 52.8 us -> 43.5 us  [mm(): return lax.dot_general(a, b, dims, preferred_element_type=F32)]
    dot_general x1 -> x0, matrix products: 6.09 us -> none  [shards(): jnp.einsum('ik,jk->ij', arrow_rows[0, 0], inverse.astype(F32), precision=...]
    broadcast_in_dim x0 -> x2, other arithmetic: none -> 4.46 us  [shards(): return (update[None], fill_block[None], tip_block - tip_total)]
  transfers between devices with their start and end apart: 6 -> 54, of which waited for: 5 -> 11; matrix products, arithmetic and copies ran while one was open for 15% -> 25% of each run, Pallas kernels for 8% -> 12%
where the time goes in v2:
time: 312 us; the launch traced here: 307 us
  starting transfers between devices  103 us (33%)
  matrix products  44.7 us (14%)
  blocking collectives  44.3 us (14%)
  waiting for transfers between devices  43.3 us (14%)
  Pallas kernels  35.5 us (11%)
  local copies, waits for them, and re-layouts  26 us (8%)
  other arithmetic  8.6 us (3%)
    ppermute x54, starting transfers between devices, move(): return lax.ppermute(block, AXES, route)  103 us
    psum x1, blocking collectives, shards(): tip_total = lax.psum(jnp.where(speaks, tip_terms, 0.0), ('tm', 'col'))  44.3 us
    dot_general x10, matrix products, mm(): return lax.dot_general(a, b, dims, preferred_element_type=F32)  43.5 us
    ppermute x54, waiting for transfers between devices, move(): return lax.ppermute(block, AXES, route)  43.3 us
    pallas_call x1, Pallas kernels, eliminate(): pl.pallas_call(functools.partial(eliminate_kernel, size, quick), out_shap...  35.5 us
    dynamic_update_slice x39, local copies, waits for them, and re-layouts, gather(): whole = lax.dynamic_update_slice(whole, block, (index * share + k, 0))  18.8 us
  transfers between devices with their start and end apart: 54, of which 11 were waited for; matrix products, arithmetic and copies ran while one was open for 25% of the time, Pallas kernels for 12%

profile of v2, /device:TPU:0, one launch (start us, length us, event | category | flops | bytes accessed | tf_op | source)
XLA Modules:
  0.0 307.1 jit_solution(10655838596037244224)
XLA Ops:
  0.6 1.9 collective-permute-start
  2.5 1.5 collective-permute-start.32
  4.0 1.5 slice_bitcast_fusion.2
  6.5 3.1 collective-permute-start.5
  9.5 1.6 collective-permute-start.6
  11.1 18.1 %collective-permute-start.9 = (bf16[192,1536]{1,0:T(8,128)(2,1)S(1)}, bf16[192,1536]{1,0:T(8,128)(2,1)S(1)}, u32[]{:S(2)}, u32[]{:S(2)}) collective-permute-start(bf16[192,1536]{1,0:T(8,128)(2,1)S(1)} %collective-permute-done), channel_id=1, source_target_pairs={{0,8},{1,9},{2,10},{3,11},{4,12},{5,13},{6,14},{7,15},{8,0},{9,1},... | collective-permute-start | bytes 1769480 | tf_op jit(solution)/shard_map/ppermute | solution.py:99
  31.0 1.5 collective-permute-start.23
  33.0 5.5 %collective-permute-done.7 = bf16[144,1536]{1,0:T(8,128)(2,1)S(1)} collective-permute-done((bf16[144,1536]{1,0:T(8,128)(2,1)S(1)}, bf16[144,1536]{1,0:T(8,128)(2,1)S(1)}, u32[]{:S(2)}, u32[]{:S(2)}) %collective-permute-start.7) | collective-permute-done | bytes 442400 | tf_op jit(solution)/shard_map/ppermute | solution.py:99
  38.4 3.4 %collective-permute-start.24 = (bf16[192,1536]{1,0:T(8,128)(2,1)S(1)}, bf16[192,1536]{1,0:T(8,128)(2,1)S(1)}, u32[]{:S(2)}, u32[]{:S(2)}) collective-permute-start(bf16[192,1536]{1,0:T(8,128)(2,1)S(1)} %collective-permute-done.1), channel_id=1, source_target_pairs={{0,1},{1,0},{2,3},{3,2},{4,5},{5,4},{6,7},{7,6},{8,9},{9,8},{10,11... | collective-permute-start | bytes 1769480 | tf_op jit(solution)/shard_map/ppermute | solution.py:99
  42.4 14.9 %collective-permute-start.27 = (bf16[192,1536]{1,0:T(8,128)(2,1)S(1)}, bf16[192,1536]{1,0:T(8,128)(2,1)S(1)}, u32[]{:S(2)}, u32[]{:S(2)}) collective-permute-start(bf16[192,1536]{1,0:T(8,128)(2,1)S(1)} %collective-permute-done.1), channel_id=1, source_target_pairs={{0,8},{1,9},{2,10},{3,11},{4,12},{5,13},{6,14},{7,15},{8,0},{9,1},... | collective-permute-start | bytes 1769480 | tf_op jit(solution)/shard_map/ppermute | solution.py:99
  57.4 0.9 collective-permute-start.11
  58.9 5.0 %collective-permute-start.12 = (bf16[144,1536]{1,0:T(8,128)(2,1)S(1)}, bf16[144,1536]{1,0:T(8,128)(2,1)S(1)}, u32[]{:S(2)}, u32[]{:S(2)}) collective-permute-start(bf16[144,1536]{1,0:T(8,128)(2,1)S(1)} %collective-permute-done.7), channel_id=1, source_target_pairs={{0,8},{1,9},{2,10},{3,11},{4,12},{5,13},{6,14},{7,15},{8,0},{9,1},... | collective-permute-start | bytes 1327112 | tf_op jit(solution)/shard_map/ppermute | solution.py:99
  64.7 1.5 collective-permute-start.25
  66.2 2.1 collective-permute-start.26
  69.0 1.3 fusion.6
  70.5 4.1 %collective-permute-done.25 = bf16[144,1536]{1,0:T(8,128)(2,1)S(1)} collective-permute-done((bf16[144,1536]{1,0:T(8,128)(2,1)S(1)}, bf16[144,1536]{1,0:T(8,128)(2,1)S(1)}, u32[]{:S(2)}, u32[]{:S(2)}) %collective-permute-start.25) | collective-permute-done | bytes 442400 | tf_op jit(solution)/shard_map/ppermute | solution.py:99
  74.5 2.0 collective-permute-start.15
  76.6 6.5 %collective-permute-start.18 = (bf16[192,1536]{1,0:T(8,128)(2,1)S(1)}, bf16[192,1536]{1,0:T(8,128)(2,1)S(1)}, u32[]{:S(2)}, u32[]{:S(2)}) collective-permute-start(bf16[192,1536]{1,0:T(8,128)(2,1)S(1)} %collective-permute-done.2), channel_id=1, source_target_pairs={{0,8},{1,9},{2,10},{3,11},{4,12},{5,13},{6,14},{7,15},{8,0},{9,1},... | collective-permute-start | bytes 1769480 | tf_op jit(solution)/shard_map/ppermute | solution.py:99
  83.3 3.9 %collective-permute-done.14 = bf16[192,1536]{1,0:T(8,128)(2,1)S(1)} collective-permute-done((bf16[192,1536]{1,0:T(8,128)(2,1)S(1)}, bf16[192,1536]{1,0:T(8,128)(2,1)S(1)}, u32[]{:S(2)}, u32[]{:S(2)}) %collective-permute-start.14) | collective-permute-done | bytes 589856 | tf_op jit(solution)/shard_map/ppermute | solution.py:99
  87.2 3.4 %collective-permute-start.29 = (bf16[192,1536]{1,0:T(8,128)(2,1)S(1)}, bf16[192,1536]{1,0:T(8,128)(2,1)S(1)}, u32[]{:S(2)}, u32[]{:S(2)}) collective-permute-start(bf16[192,1536]{1,0:T(8,128)(2,1)S(1)} %collective-permute-done.24), channel_id=1, source_target_pairs={{0,8},{1,9},{2,10},{3,11},{4,12},{5,13},{6,14},{7,15},{8,0},{9,1},... | collective-permute-start | bytes 1769480 | tf_op jit(solution)/shard_map/ppermute | solution.py:99
  90.7 2.0 collective-permute-done.15
  92.7 1.8 collective-permute-start.30
  94.7 2.0 collective-permute-start.16
  97.3 1.7 collective-permute-start.4
  99.8 7.8 %convolution_convert_fusion = bf16[1536,1536]{1,0:T(8,128)(2,1)S(1)} fusion(bf16[1536,1536]{1,0:T(8,128)(2,1)S(1)} %constant_dynamic-update-slice_fusion.30, bf16[1536,1536]{1,0:T(8,128)(2,1)S(1)} %constant_dynamic-update-slice_fusion), kind=kOutput, calls=%fused_computation.1 | convolution fusion | flops 7250116608 | bytes 14155776 | tf_op jit(solution)/shard_map/dot_general | solution.py:14
  107.6 1.3 fusion.13
  108.9 1.5 collective-permute-start.44
  110.4 3.4 %collective-permute-start.47 = (bf16[192,1536]{1,0:T(8,128)(2,1)S(1)}, bf16[192,1536]{1,0:T(8,128)(2,1)S(1)}, u32[]{:S(2)}, u32[]{:S(2)}) collective-permute-start(bf16[192,1536]{1,0:T(8,128)(2,1)S(1)} %collective-permute-done.3), channel_id=1, source_target_pairs={{0,8},{1,9},{2,10},{3,11},{4,12},{5,13},{6,14},{7,15},{8,0},{9,1},... | collective-permute-start | bytes 1769480 | tf_op jit(solution)/shard_map/ppermute | solution.py:99
  114.0 15.1 %collective-permute-done.44 = bf16[192,1536]{1,0:T(8,128)(2,1)S(1)} collective-permute-done((bf16[192,1536]{1,0:T(8,128)(2,1)S(1)}, bf16[192,1536]{1,0:T(8,128)(2,1)S(1)}, u32[]{:S(2)}, u32[]{:S(2)}) %collective-permute-start.44) | collective-permute-done | bytes 589856 | tf_op jit(solution)/shard_map/ppermute | solution.py:99
  131.4 2.8 broadcast.12.clone.3
  134.2 2.0 constant_dynamic-update-slice_fusion.29
  136.2 2.7 convolution_convert_fusion.3
  139.0 1.8 collective-permute-start.45
  140.8 1.7 convolution_negate_fusion.1
  142.6 1.6 pad_maximum_fusion.r_in
  144.8 10.4 %convert_subtract_fusion.s_in = f32[1536,1536]{1,0:T(8,128)} fusion(bf16[1536,1536]{1,0:T(8,128)(2,1)S(1)} %constant_dynamic-update-slice_fusion.40, bf16[1536,1536]{1,0:T(8,128)(2,1)S(1)} %convolution_convert_fusion), kind=kOutput, calls=%fused_computation | convolution fusion | flops 7252475904 | bytes 18874368 | tf_op jit(solution)/shard_map/dot_general | solution.py:14
  155.2 35.5 %eliminate.1 = f32[392,1536]{1,0:T(8,128)} custom-call(f32[1536,1536]{1,0:T(8,128)} %convert_subtract_fusion.s_in, f32[392,1536]{1,0:T(8,128)} %pad_maximum_fusion.r_in), custom_call_target="tpu_custom_call" | custom-call | flops 7247757312 | bytes 14254080 | tf_op jit(solution)/shard_map/eliminate/pallas_call | solution.py:76
  190.8 1.8 convert.4
  192.6 3.4 %fusion.4 = f32[192,1536]{1,0:T(8,128)S(1)} fusion(bf16[1536,1536]{1,0:T(8,128)(2,1)} %copy-done.1, bf16[392,1536]{1,0:T(8,128)(2,1)S(1)} %convert.4), kind=kOutput, calls=%fused_computation.19 | convolution fusion | flops 905969664 | bytes 6488064 | tf_op jit(solution)/shard_map/dot_general | solution.py:14
  196.4 1.8 constant_dynamic-update-slice_fusion.16
  198.2 2.0 collective-permute-start.34
  200.9 0.9 constant_dynamic-update-slice_fusion.14
  201.8 10.0 %collective-permute-done.33 = bf16[192,1536]{1,0:T(8,128)(2,1)S(1)} collective-permute-done((bf16[192,1536]{1,0:T(8,128)(2,1)}, bf16[192,1536]{1,0:T(8,128)(2,1)S(1)}, u32[]{:S(2)}, u32[]{:S(2)}) %collective-permute-start.33) | collective-permute-done | bytes 589856 | tf_op jit(solution)/shard_map/ppermute | solution.py:99
  211.7 0.9 constant_dynamic-update-slice_fusion.28
  212.6 1.0 collective-permute-done.34
  213.7 0.9 constant_dynamic-update-slice_fusion.27
  214.6 1.6 collective-permute-start.35
  216.3 1.9 constant_dynamic-update-slice_fusion.13
  218.2 1.7 collective-permute-start.36
  219.9 1.9 constant_dynamic-update-slice_fusion.12
  223.2 1.0 collective-permute-done.36
  224.9 5.0 %fusion.26 = (bf16[192,1536]{1,0:T(8,128)(2,1)}, f32[192,1536]{1,0:T(8,128)S(1)}) fusion(bf16[1536,1536]{1,0:T(8,128)(2,1)} %constant_dynamic-update-slice_fusion.10, bf16[392,1536]{1,0:T(8,128)(2,1)S(1)} %convert.4), kind=kOutput, calls=%fused_computation.93 | convolution fusion | flops 906559488 | bytes 7077888 | tf_op jit(solution)/shard_map/dot_general | solution.py:14
  229.9 2.5 convolution_convert_fusion.1
  232.4 3.2 %collective-permute-start.52 = (bf16[192,1536]{1,0:T(8,128)(2,1)}, bf16[192,1536]{1,0:T(8,128)(2,1)}, u32[]{:S(2)}, u32[]{:S(2)}) collective-permute-start(bf16[192,1536]{1,0:T(8,128)(2,1)} %convolution_convert_fusion.1), channel_id=1, source_target_pairs={{0,8},{1,9},{2,16},{3,17},{4,12},{5,13},{6,20},{7,21},{8,10},{9,11... | collective-permute-start | bytes 1769480 | tf_op jit(solution)/shard_map/ppermute | solution.py:99
  237.1 6.0 %collective-permute-start.53 = (bf16[192,1536]{1,0:T(8,128)(2,1)}, bf16[192,1536]{1,0:T(8,128)(2,1)}, u32[]{:S(2)}, u32[]{:S(2)}) collective-permute-start(bf16[192,1536]{1,0:T(8,128)(2,1)} %get-tuple-element.21), channel_id=1, source_target_pairs={{0,0},{1,1},{2,8},{3,9},{4,4},{5,5},{6,12},{7,13},{8,2},{9,3},{10,... | collective-permute-start | bytes 1769480 | tf_op jit(solution)/shard_map/ppermute | solution.py:99
  243.0 0.9 constant_dynamic-update-slice_fusion.24
  243.9 0.8 constant_dynamic-update-slice_fusion.23
  244.8 0.9 constant_dynamic-update-slice_fusion.22
  247.2 7.4 %fusion.25 = (bf16[192,1536]{1,0:T(8,128)(2,1)}, f32[192,1536]{1,0:T(8,128)S(1)}) fusion(bf16[1536,1536]{1,0:T(8,128)(2,1)} %constant_dynamic-update-slice_fusion.20, bf16[1536,1536]{1,0:T(8,128)(2,1)} %copy-done, f32[192,1536]{1,0:T(8,128)S(1)} %fusion.4, bf16[192,1536]{1,0:T(8,128)(2,1)} %copy-done.4), kind=kOutput, calls=%fused_computation.92 | convolution fusion | flops 1813413888 | bytes 12976128 | tf_op jit(solution)/shard_map/dot_general | solution.py:14
  254.6 1.7 collective-permute-start.42
  256.3 1.0 fusion
  257.3 44.3 %psum.7 = f32[8,8]{1,0:T(8,128)S(1)} all-reduce(f32[8,8]{1,0:T(8,128)S(1)} %fusion), channel_id=1, replica_groups=mesh['tm'=4,'row'=2,'col'=4] {'tm','col'}, use_global_device_ids=true, to_apply=%region_0.1 | all-reduce | flops 64 | bytes 512 | tf_op jit(solution)/shard_map/psum | solution.py:221
  302.2 2.2 select_bitcast_fusion
  304.4 2.3 add_bitcast_fusion
  (145 shorter events, 17.5 us)
Async XLA Ops:
  0.6 28.6 %copy-start.7 = (bf16[1,192,1536]{2,1,0:T(8,128)(2,1)S(1)}, bf16[1,192,1536]{2,1,0:T(8,128)(2,1)}, u32[]{:S(2)}) copy-start(bf16[1,192,1536]{2,1,0:T(8,128)(2,1)} %param.6) | copy-start | bytes 1769476
  0.6 5.1 %collective-permute-start = (bf16[192,1536]{1,0:T(8,128)(2,1)}, bf16[192,1536]{1,0:T(8,128)(2,1)S(1)}, u32[]{:S(2)}, u32[]{:S(2)}) collective-permute-start(bf16[192,1536]{1,0:T(8,128)(2,1)} %bitcast.45), channel_id=1, source_target_pairs={{0,0},{1,1},{2,8},{3,9},{4,4},{5,5},{6,12},{7,13},{8,2},{9,3},{10,... | collective-permute-start | bytes 1769480 | tf_op jit(solution)/shard_map/ppermute | solution.py:99
  2.5 8.6 %collective-permute-start.32 = (f32[2,8,1536]{2,1,0:T(8,128)}, f32[2,8,1536]{2,1,0:T(8,128)S(1)}, u32[]{:S(2)}, u32[]{:S(2)}) collective-permute-start(f32[2,8,1536]{2,1,0:T(8,128)} %bitcast.47), channel_id=1, source_target_pairs={{0,0},{1,1},{2,8},{3,9},{4,4},{5,5},{6,12},{7,13},{8,2},{9,3},{10,... | collective-permute-start | bytes 294920 | tf_op jit(solution)/shard_map/ppermute | solution.py:99
  5.8 23.5 %collective-permute-start.1 = (bf16[192,1536]{1,0:T(8,128)(2,1)S(1)}, bf16[192,1536]{1,0:T(8,128)(2,1)S(1)}, u32[]{:S(2)}, u32[]{:S(2)}) collective-permute-start(bf16[192,1536]{1,0:T(8,128)(2,1)S(1)} %get-tuple-element.7), channel_id=1, source_target_pairs={{0,0},{1,1},{2,8},{3,9},{4,4},{5,5},{6,12},{7,13},{8,2},{9,3},{10,... | collective-permute-start | bytes 1769480 | tf_op jit(solution)/shard_map/ppermute | solution.py:99
  6.5 24.1 %collective-permute-start.5 = (bf16[192,1536]{1,0:T(8,128)(2,1)S(1)}, bf16[192,1536]{1,0:T(8,128)(2,1)S(1)}, u32[]{:S(2)}, u32[]{:S(2)}) collective-permute-start(bf16[192,1536]{1,0:T(8,128)(2,1)S(1)} %collective-permute-done), channel_id=1, source_target_pairs={{0,4},{1,5},{2,6},{3,7},{4,0},{5,1},{6,2},{7,3},{8,12},{9,13},{10,... | collective-permute-start | bytes 1769480 | tf_op jit(solution)/shard_map/ppermute | solution.py:99
  9.5 20.5 %collective-permute-start.6 = (bf16[192,1536]{1,0:T(8,128)(2,1)S(1)}, bf16[192,1536]{1,0:T(8,128)(2,1)S(1)}, u32[]{:S(2)}, u32[]{:S(2)}) collective-permute-start(bf16[192,1536]{1,0:T(8,128)(2,1)S(1)} %collective-permute-done), channel_id=1, source_target_pairs={{0,1},{1,0},{2,3},{3,2},{4,5},{5,4},{6,7},{7,6},{8,9},{9,8},{10,11... | collective-permute-start | bytes 1769480 | tf_op jit(solution)/shard_map/ppermute | solution.py:99
  11.1 46.1 %collective-permute-start.9 = (bf16[192,1536]{1,0:T(8,128)(2,1)S(1)}, bf16[192,1536]{1,0:T(8,128)(2,1)S(1)}, u32[]{:S(2)}, u32[]{:S(2)}) collective-permute-start(bf16[192,1536]{1,0:T(8,128)(2,1)S(1)} %collective-permute-done), channel_id=1, source_target_pairs={{0,8},{1,9},{2,10},{3,11},{4,12},{5,13},{6,14},{7,15},{8,0},{9,1},... | collective-permute-start | bytes 1769480 | tf_op jit(solution)/shard_map/ppermute | solution.py:99
  29.3 28.1 %collective-permute-start.2 = (bf16[192,1536]{1,0:T(8,128)(2,1)S(1)}, bf16[192,1536]{1,0:T(8,128)(2,1)S(1)}, u32[]{:S(2)}, u32[]{:S(2)}) collective-permute-start(bf16[192,1536]{1,0:T(8,128)(2,1)S(1)} %bitcast.46), channel_id=1, source_target_pairs={{0,0},{1,1},{2,8},{3,9},{4,4},{5,5},{6,12},{7,13},{8,2},{9,3},{10,... | collective-permute-start | bytes 1769480 | tf_op jit(solution)/shard_map/ppermute | solution.py:99
  30.0 8.4 %collective-permute-start.7 = (bf16[144,1536]{1,0:T(8,128)(2,1)S(1)}, bf16[144,1536]{1,0:T(8,128)(2,1)S(1)}, u32[]{:S(2)}, u32[]{:S(2)}) collective-permute-start(bf16[144,1536]{1,0:T(8,128)(2,1)S(1)} %slice.86), channel_id=1, source_target_pairs={{0,4},{1,5},{2,6},{3,7},{4,0},{5,1},{6,2},{7,3},{8,12},{9,13},{10,... | collective-permute-start | bytes 1327112 | tf_op jit(solution)/shard_map/ppermute | solution.py:99
  30.6 11.7 %collective-permute-start.8 = (bf16[48,1536]{1,0:T(8,128)(2,1)S(1)}, bf16[48,1536]{1,0:T(8,128)(2,1)S(1)}, u32[]{:S(2)}, u32[]{:S(2)}) collective-permute-start(bf16[48,1536]{1,0:T(8,128)(2,1)S(1)} %slice.87), channel_id=1, source_target_pairs={{0,1},{1,0},{2,3},{3,2},{4,5},{5,4},{6,7},{7,6},{8,9},{9,8},{10,11... | collective-permute-start | bytes 442376 | tf_op jit(solution)/shard_map/ppermute | solution.py:99
  31.0 27.7 %collective-permute-start.23 = (bf16[192,1536]{1,0:T(8,128)(2,1)S(1)}, bf16[192,1536]{1,0:T(8,128)(2,1)S(1)}, u32[]{:S(2)}, u32[]{:S(2)}) collective-permute-start(bf16[192,1536]{1,0:T(8,128)(2,1)S(1)} %collective-permute-done.1), channel_id=1, source_target_pairs={{0,4},{1,5},{2,6},{3,7},{4,0},{5,1},{6,2},{7,3},{8,12},{9,13},{10,... | collective-permute-start | bytes 1769480 | tf_op jit(solution)/shard_map/ppermute | solution.py:99
  38.4 20.5 %collective-permute-start.24 = (bf16[192,1536]{1,0:T(8,128)(2,1)S(1)}, bf16[192,1536]{1,0:T(8,128)(2,1)S(1)}, u32[]{:S(2)}, u32[]{:S(2)}) collective-permute-start(bf16[192,1536]{1,0:T(8,128)(2,1)S(1)} %collective-permute-done.1), channel_id=1, source_target_pairs={{0,1},{1,0},{2,3},{3,2},{4,5},{5,4},{6,7},{7,6},{8,9},{9,8},{10,11... | collective-permute-start | bytes 1769480 | tf_op jit(solution)/shard_map/ppermute | solution.py:99
  42.4 40.8 %collective-permute-start.27 = (bf16[192,1536]{1,0:T(8,128)(2,1)S(1)}, bf16[192,1536]{1,0:T(8,128)(2,1)S(1)}, u32[]{:S(2)}, u32[]{:S(2)}) collective-permute-start(bf16[192,1536]{1,0:T(8,128)(2,1)S(1)} %collective-permute-done.1), channel_id=1, source_target_pairs={{0,8},{1,9},{2,10},{3,11},{4,12},{5,13},{6,14},{7,15},{8,0},{9,1},... | collective-permute-start | bytes 1769480 | tf_op jit(solution)/shard_map/ppermute | solution.py:99
  57.3 6.7 %collective-permute-start.10 = (bf16[192,1536]{1,0:T(8,128)(2,1)S(1)}, bf16[192,1536]{1,0:T(8,128)(2,1)S(1)}, u32[]{:S(2)}, u32[]{:S(2)}) collective-permute-start(bf16[192,1536]{1,0:T(8,128)(2,1)S(1)} %collective-permute-done.5), channel_id=1, source_target_pairs={{0,8},{1,9},{2,10},{3,11},{4,12},{5,13},{6,14},{7,15},{8,0},{9,1},... | collective-permute-start | bytes 1769480 | tf_op jit(solution)/shard_map/ppermute | solution.py:99
  57.4 7.3 %collective-permute-start.11 = (bf16[192,1536]{1,0:T(8,128)(2,1)S(1)}, bf16[192,1536]{1,0:T(8,128)(2,1)S(1)}, u32[]{:S(2)}, u32[]{:S(2)}) collective-permute-start(bf16[192,1536]{1,0:T(8,128)(2,1)S(1)} %collective-permute-done.6), channel_id=1, source_target_pairs={{0,8},{1,9},{2,10},{3,11},{4,12},{5,13},{6,14},{7,15},{8,0},{9,1},... | collective-permute-start | bytes 1769480 | tf_op jit(solution)/shard_map/ppermute | solution.py:99
  58.7 9.7 %collective-permute-start.13 = (bf16[48,1536]{1,0:T(8,128)(2,1)S(1)}, bf16[48,1536]{1,0:T(8,128)(2,1)S(1)}, u32[]{:S(2)}, u32[]{:S(2)}) collective-permute-start(bf16[48,1536]{1,0:T(8,128)(2,1)S(1)} %collective-permute-done.8), channel_id=1, source_target_pairs={{0,8},{1,9},{2,10},{3,11},{4,12},{5,13},{6,14},{7,15},{8,0},{9,1},... | collective-permute-start | bytes 442376 | tf_op jit(solution)/shard_map/ppermute | solution.py:99
  58.9 7.4 %collective-permute-start.12 = (bf16[144,1536]{1,0:T(8,128)(2,1)S(1)}, bf16[144,1536]{1,0:T(8,128)(2,1)S(1)}, u32[]{:S(2)}, u32[]{:S(2)}) collective-permute-start(bf16[144,1536]{1,0:T(8,128)(2,1)S(1)} %collective-permute-done.7), channel_id=1, source_target_pairs={{0,8},{1,9},{2,10},{3,11},{4,12},{5,13},{6,14},{7,15},{8,0},{9,1},... | collective-permute-start | bytes 1327112 | tf_op jit(solution)/shard_map/ppermute | solution.py:99
  63.9 26.7 %collective-permute-start.3 = (bf16[192,1536]{1,0:T(8,128)(2,1)S(1)}, bf16[192,1536]{1,0:T(8,128)(2,1)S(1)}, u32[]{:S(2)}, u32[]{:S(2)}) collective-permute-start(bf16[192,1536]{1,0:T(8,128)(2,1)S(1)} %get-tuple-element.9), channel_id=1, source_target_pairs={{0,0},{1,1},{2,8},{3,9},{4,4},{5,5},{6,12},{7,13},{8,2},{9,3},{10,... | collective-permute-start | bytes 1769480 | tf_op jit(solution)/shard_map/ppermute | solution.py:99
  64.7 9.8 %collective-permute-start.25 = (bf16[144,1536]{1,0:T(8,128)(2,1)S(1)}, bf16[144,1536]{1,0:T(8,128)(2,1)S(1)}, u32[]{:S(2)}, u32[]{:S(2)}) collective-permute-start(bf16[144,1536]{1,0:T(8,128)(2,1)S(1)} %slice.90), channel_id=1, source_target_pairs={{0,4},{1,5},{2,6},{3,7},{4,0},{5,1},{6,2},{7,3},{8,12},{9,13},{10,... | collective-permute-start | bytes 1327112 | tf_op jit(solution)/shard_map/ppermute | solution.py:99
  66.2 10.4 %collective-permute-start.26 = (bf16[48,1536]{1,0:T(8,128)(2,1)S(1)}, bf16[48,1536]{1,0:T(8,128)(2,1)S(1)}, u32[]{:S(2)}, u32[]{:S(2)}) collective-permute-start(bf16[48,1536]{1,0:T(8,128)(2,1)S(1)} %slice.91), channel_id=1, source_target_pairs={{0,1},{1,0},{2,3},{3,2},{4,5},{5,4},{6,7},{7,6},{8,9},{9,8},{10,11... | collective-permute-start | bytes 442376 | tf_op jit(solution)/shard_map/ppermute | solution.py:99
  68.4 18.8 %collective-permute-start.14 = (bf16[192,1536]{1,0:T(8,128)(2,1)S(1)}, bf16[192,1536]{1,0:T(8,128)(2,1)S(1)}, u32[]{:S(2)}, u32[]{:S(2)}) collective-permute-start(bf16[192,1536]{1,0:T(8,128)(2,1)S(1)} %collective-permute-done.2), channel_id=1, source_target_pairs={{0,4},{1,5},{2,6},{3,7},{4,0},{5,1},{6,2},{7,3},{8,12},{9,13},{10,... | collective-permute-start | bytes 1769480 | tf_op jit(solution)/shard_map/ppermute | solution.py:99
  68.9 67.2 %copy-start = (bf16[1536,1536]{1,0:T(8,128)(2,1)}, bf16[1536,1536]{1,0:T(8,128)(2,1)S(1)}, u32[]{:S(2)}) copy-start(bf16[1536,1536]{1,0:T(8,128)(2,1)S(1)} %constant_dynamic-update-slice_fusion) | copy-start | bytes 14155780
  74.5 18.2 %collective-permute-start.15 = (bf16[192,1536]{1,0:T(8,128)(2,1)S(1)}, bf16[192,1536]{1,0:T(8,128)(2,1)S(1)}, u32[]{:S(2)}, u32[]{:S(2)}) collective-permute-start(bf16[192,1536]{1,0:T(8,128)(2,1)S(1)} %collective-permute-done.2), channel_id=1, source_target_pairs={{0,1},{1,0},{2,3},{3,2},{4,5},{5,4},{6,7},{7,6},{8,9},{9,8},{10,11... | collective-permute-start | bytes 1769480 | tf_op jit(solution)/shard_map/ppermute | solution.py:99
  76.6 37.3 %collective-permute-start.18 = (bf16[192,1536]{1,0:T(8,128)(2,1)S(1)}, bf16[192,1536]{1,0:T(8,128)(2,1)S(1)}, u32[]{:S(2)}, u32[]{:S(2)}) collective-permute-start(bf16[192,1536]{1,0:T(8,128)(2,1)S(1)} %collective-permute-done.2), channel_id=1, source_target_pairs={{0,8},{1,9},{2,10},{3,11},{4,12},{5,13},{6,14},{7,15},{8,0},{9,1},... | collective-permute-start | bytes 1769480 | tf_op jit(solution)/shard_map/ppermute | solution.py:99
  83.1 11.5 %collective-permute-start.28 = (bf16[192,1536]{1,0:T(8,128)(2,1)S(1)}, bf16[192,1536]{1,0:T(8,128)(2,1)S(1)}, u32[]{:S(2)}, u32[]{:S(2)}) collective-permute-start(bf16[192,1536]{1,0:T(8,128)(2,1)S(1)} %collective-permute-done.23), channel_id=1, source_target_pairs={{0,8},{1,9},{2,10},{3,11},{4,12},{5,13},{6,14},{7,15},{8,0},{9,1},... | collective-permute-start | bytes 1769480 | tf_op jit(solution)/shard_map/ppermute | solution.py:99
  87.2 9.5 %collective-permute-start.29 = (bf16[192,1536]{1,0:T(8,128)(2,1)S(1)}, bf16[192,1536]{1,0:T(8,128)(2,1)S(1)}, u32[]{:S(2)}, u32[]{:S(2)}) collective-permute-start(bf16[192,1536]{1,0:T(8,128)(2,1)S(1)} %collective-permute-done.24), channel_id=1, source_target_pairs={{0,8},{1,9},{2,10},{3,11},{4,12},{5,13},{6,14},{7,15},{8,0},{9,1},... | collective-permute-start | bytes 1769480 | tf_op jit(solution)/shard_map/ppermute | solution.py:99
  90.6 8.4 %collective-permute-start.31 = (bf16[48,1536]{1,0:T(8,128)(2,1)S(1)}, bf16[48,1536]{1,0:T(8,128)(2,1)S(1)}, u32[]{:S(2)}, u32[]{:S(2)}) collective-permute-start(bf16[48,1536]{1,0:T(8,128)(2,1)S(1)} %collective-permute-done.26), channel_id=1, source_target_pairs={{0,8},{1,9},{2,10},{3,11},{4,12},{5,13},{6,14},{7,15},{8,0},{9,1},... | collective-permute-start | bytes 442376 | tf_op jit(solution)/shard_map/ppermute | solution.py:99
  92.7 4.6 %collective-permute-start.30 = (bf16[144,1536]{1,0:T(8,128)(2,1)S(1)}, bf16[144,1536]{1,0:T(8,128)(2,1)S(1)}, u32[]{:S(2)}, u32[]{:S(2)}) collective-permute-start(bf16[144,1536]{1,0:T(8,128)(2,1)S(1)} %collective-permute-done.25), channel_id=1, source_target_pairs={{0,8},{1,9},{2,10},{3,11},{4,12},{5,13},{6,14},{7,15},{8,0},{9,1},... | collective-permute-start | bytes 1327112 | tf_op jit(solution)/shard_map/ppermute | solution.py:99
  94.7 14.3 %collective-permute-start.16 = (bf16[144,1536]{1,0:T(8,128)(2,1)S(1)}, bf16[144,1536]{1,0:T(8,128)(2,1)S(1)}, u32[]{:S(2)}, u32[]{:S(2)}) collective-permute-start(bf16[144,1536]{1,0:T(8,128)(2,1)S(1)} %slice.88), channel_id=1, source_target_pairs={{0,4},{1,5},{2,6},{3,7},{4,0},{5,1},{6,2},{7,3},{8,12},{9,13},{10,... | collective-permute-start | bytes 1327112 | tf_op jit(solution)/shard_map/ppermute | solution.py:99
  96.7 13.8 %collective-permute-start.17 = (bf16[48,1536]{1,0:T(8,128)(2,1)S(1)}, bf16[48,1536]{1,0:T(8,128)(2,1)S(1)}, u32[]{:S(2)}, u32[]{:S(2)}) collective-permute-start(bf16[48,1536]{1,0:T(8,128)(2,1)S(1)} %slice.89), channel_id=1, source_target_pairs={{0,1},{1,0},{2,3},{3,2},{4,5},{5,4},{6,7},{7,6},{8,9},{9,8},{10,11... | collective-permute-start | bytes 442376 | tf_op jit(solution)/shard_map/ppermute | solution.py:99
  97.3 33.9 %collective-permute-start.4 = (bf16[192,1536]{1,0:T(8,128)(2,1)S(1)}, bf16[192,1536]{1,0:T(8,128)(2,1)}, u32[]{:S(2)}, u32[]{:S(2)}) collective-permute-start(bf16[192,1536]{1,0:T(8,128)(2,1)S(1)} %get-tuple-element.10), channel_id=1, source_target_pairs={{0,0},{1,1},{2,8},{3,9},{4,4},{5,5},{6,12},{7,13},{8,2},{9,3},{10,... | collective-permute-start | bytes 1769480 | tf_op jit(solution)/shard_map/ppermute | solution.py:99
  99.0 31.0 %collective-permute-start.43 = (bf16[192,1536]{1,0:T(8,128)(2,1)S(1)}, bf16[192,1536]{1,0:T(8,128)(2,1)S(1)}, u32[]{:S(2)}, u32[]{:S(2)}) collective-permute-start(bf16[192,1536]{1,0:T(8,128)(2,1)S(1)} %collective-permute-done.3), channel_id=1, source_target_pairs={{0,4},{1,5},{2,6},{3,7},{4,0},{5,1},{6,2},{7,3},{8,12},{9,13},{10,... | collective-permute-start | bytes 1769480 | tf_op jit(solution)/shard_map/ppermute | solution.py:99
  107.6 37.2 %copy-start.1 = (bf16[1536,1536]{1,0:T(8,128)(2,1)}, bf16[1536,1536]{1,0:T(8,128)(2,1)S(1)}, u32[]{:S(2)}) copy-start(bf16[1536,1536]{1,0:T(8,128)(2,1)S(1)} %convolution_convert_fusion) | copy-start | bytes 14155780
  108.9 33.7 %copy-start.5 = (f32[8,1536]{1,0:T(8,128)}, f32[8,1536]{1,0:T(8,128)S(1)}, u32[]{:S(2)}) copy-start(f32[8,1536]{1,0:T(8,128)S(1)} %fusion.13) | copy-start | bytes 147460
  108.9 20.2 %collective-permute-start.44 = (bf16[192,1536]{1,0:T(8,128)(2,1)S(1)}, bf16[192,1536]{1,0:T(8,128)(2,1)S(1)}, u32[]{:S(2)}, u32[]{:S(2)}) collective-permute-start(bf16[192,1536]{1,0:T(8,128)(2,1)S(1)} %collective-permute-done.3), channel_id=1, source_target_pairs={{0,1},{1,0},{2,3},{3,2},{4,5},{5,4},{6,7},{7,6},{8,9},{9,8},{10,11... | collective-permute-start | bytes 1769480 | tf_op jit(solution)/shard_map/ppermute | solution.py:99
  110.4 90.5 %collective-permute-start.47 = (bf16[192,1536]{1,0:T(8,128)(2,1)S(1)}, bf16[192,1536]{1,0:T(8,128)(2,1)S(1)}, u32[]{:S(2)}, u32[]{:S(2)}) collective-permute-start(bf16[192,1536]{1,0:T(8,128)(2,1)S(1)} %collective-permute-done.3), channel_id=1, source_target_pairs={{0,8},{1,9},{2,10},{3,11},{4,12},{5,13},{6,14},{7,15},{8,0},{9,1},... | collective-permute-start | bytes 1769480 | tf_op jit(solution)/shard_map/ppermute | solution.py:99
  113.9 25.1 %collective-permute-start.19 = (bf16[192,1536]{1,0:T(8,128)(2,1)S(1)}, bf16[192,1536]{1,0:T(8,128)(2,1)S(1)}, u32[]{:S(2)}, u32[]{:S(2)}) collective-permute-start(bf16[192,1536]{1,0:T(8,128)(2,1)S(1)} %collective-permute-done.14), channel_id=1, source_target_pairs={{0,8},{1,9},{2,10},{3,11},{4,12},{5,13},{6,14},{7,15},{8,0},{9,1},... | collective-permute-start | bytes 1769480 | tf_op jit(solution)/shard_map/ppermute | solution.py:99
  129.1 13.3 %collective-permute-start.20 = (bf16[192,1536]{1,0:T(8,128)(2,1)S(1)}, bf16[192,1536]{1,0:T(8,128)(2,1)S(1)}, u32[]{:S(2)}, u32[]{:S(2)}) collective-permute-start(bf16[192,1536]{1,0:T(8,128)(2,1)S(1)} %collective-permute-done.15), channel_id=1, source_target_pairs={{0,8},{1,9},{2,10},{3,11},{4,12},{5,13},{6,14},{7,15},{8,0},{9,1},... | collective-permute-start | bytes 1769480 | tf_op jit(solution)/shard_map/ppermute | solution.py:99
  130.0 14.4 %collective-permute-start.22 = (bf16[48,1536]{1,0:T(8,128)(2,1)S(1)}, bf16[48,1536]{1,0:T(8,128)(2,1)S(1)}, u32[]{:S(2)}, u32[]{:S(2)}) collective-permute-start(bf16[48,1536]{1,0:T(8,128)(2,1)S(1)} %collective-permute-done.17), channel_id=1, source_target_pairs={{0,8},{1,9},{2,10},{3,11},{4,12},{5,13},{6,14},{7,15},{8,0},{9,1},... | collective-permute-start | bytes 442376 | tf_op jit(solution)/shard_map/ppermute | solution.py:99
  131.2 7.7 %copy-start.2 = (bf16[1536,1536]{1,0:T(8,128)(2,1)}, bf16[1536,1536]{1,0:T(8,128)(2,1)S(1)}, u32[]{:S(2)}) copy-start(bf16[1536,1536]{1,0:T(8,128)(2,1)S(1)} %constant_dynamic-update-slice_fusion.17) | copy-start | bytes 14155780
  131.2 13.0 %collective-permute-start.21 = (bf16[144,1536]{1,0:T(8,128)(2,1)S(1)}, bf16[144,1536]{1,0:T(8,128)(2,1)S(1)}, u32[]{:S(2)}, u32[]{:S(2)}) collective-permute-start(bf16[144,1536]{1,0:T(8,128)(2,1)S(1)} %collective-permute-done.16), channel_id=1, source_target_pairs={{0,8},{1,9},{2,10},{3,11},{4,12},{5,13},{6,14},{7,15},{8,0},{9,1},... | collective-permute-start | bytes 1327112 | tf_op jit(solution)/shard_map/ppermute | solution.py:99
  138.9 3.6 %copy-start.4 = (bf16[192,1536]{1,0:T(8,128)(2,1)}, bf16[192,1536]{1,0:T(8,128)(2,1)S(1)}, u32[]{:S(2)}) copy-start(bf16[192,1536]{1,0:T(8,128)(2,1)S(1)} %convolution_convert_fusion.3) | copy-start | bytes 1769476
  139.0 57.0 %collective-permute-start.45 = (bf16[144,1536]{1,0:T(8,128)(2,1)}, bf16[144,1536]{1,0:T(8,128)(2,1)}, u32[]{:S(2)}, u32[]{:S(2)}) collective-permute-start(bf16[144,1536]{1,0:T(8,128)(2,1)} %slice.101), channel_id=1, source_target_pairs={{0,4},{1,5},{2,6},{3,7},{4,0},{5,1},{6,2},{7,3},{8,12},{9,13},{10,... | collective-permute-start | bytes 1327112 | tf_op jit(solution)/shard_map/ppermute | solution.py:99
  142.4 55.8 %collective-permute-start.46 = (bf16[48,1536]{1,0:T(8,128)(2,1)}, bf16[48,1536]{1,0:T(8,128)(2,1)S(1)}, u32[]{:S(2)}, u32[]{:S(2)}) collective-permute-start(bf16[48,1536]{1,0:T(8,128)(2,1)} %slice.102), channel_id=1, source_target_pairs={{0,1},{1,0},{2,3},{3,2},{4,5},{5,4},{6,7},{7,6},{8,9},{9,8},{10,11... | collective-permute-start | bytes 442376 | tf_op jit(solution)/shard_map/ppermute | solution.py:99
  144.2 70.4 %collective-permute-start.48 = (bf16[192,1536]{1,0:T(8,128)(2,1)S(1)}, bf16[192,1536]{1,0:T(8,128)(2,1)}, u32[]{:S(2)}, u32[]{:S(2)}) collective-permute-start(bf16[192,1536]{1,0:T(8,128)(2,1)S(1)} %collective-permute-done.43), channel_id=1, source_target_pairs={{0,8},{1,9},{2,10},{3,11},{4,12},{5,13},{6,14},{7,15},{8,0},{9,1},... | collective-permute-start | bytes 1769480 | tf_op jit(solution)/shard_map/ppermute | solution.py:99
  144.4 73.8 %collective-permute-start.49 = (bf16[192,1536]{1,0:T(8,128)(2,1)S(1)}, bf16[192,1536]{1,0:T(8,128)(2,1)}, u32[]{:S(2)}, u32[]{:S(2)}) collective-permute-start(bf16[192,1536]{1,0:T(8,128)(2,1)S(1)} %collective-permute-done.44), channel_id=1, source_target_pairs={{0,8},{1,9},{2,10},{3,11},{4,12},{5,13},{6,14},{7,15},{8,0},{9,1},... | collective-permute-start | bytes 1769480 | tf_op jit(solution)/shard_map/ppermute | solution.py:99
  196.0 15.7 %collective-permute-start.33 = (bf16[192,1536]{1,0:T(8,128)(2,1)}, bf16[192,1536]{1,0:T(8,128)(2,1)S(1)}, u32[]{:S(2)}, u32[]{:S(2)}) collective-permute-start(bf16[192,1536]{1,0:T(8,128)(2,1)} %collective-permute-done.4), channel_id=1, source_target_pairs={{0,4},{1,5},{2,6},{3,7},{4,0},{5,1},{6,2},{7,3},{8,12},{9,13},{10,... | collective-permute-start | bytes 1769480 | tf_op jit(solution)/shard_map/ppermute | solution.py:99
  198.2 15.4 %collective-permute-start.34 = (bf16[192,1536]{1,0:T(8,128)(2,1)}, bf16[192,1536]{1,0:T(8,128)(2,1)S(1)}, u32[]{:S(2)}, u32[]{:S(2)}) collective-permute-start(bf16[192,1536]{1,0:T(8,128)(2,1)} %collective-permute-done.4), channel_id=1, source_target_pairs={{0,1},{1,0},{2,3},{3,2},{4,5},{5,4},{6,7},{7,6},{8,9},{9,8},{10,11... | collective-permute-start | bytes 1769480 | tf_op jit(solution)/shard_map/ppermute | solution.py:99
  200.9 36.1 %collective-permute-start.37 = (bf16[192,1536]{1,0:T(8,128)(2,1)}, bf16[192,1536]{1,0:T(8,128)(2,1)S(1)}, u32[]{:S(2)}, u32[]{:S(2)}) collective-permute-start(bf16[192,1536]{1,0:T(8,128)(2,1)} %collective-permute-done.4), channel_id=1, source_target_pairs={{0,8},{1,9},{2,10},{3,11},{4,12},{5,13},{6,14},{7,15},{8,0},{9,1},... | collective-permute-start | bytes 1769480 | tf_op jit(solution)/shard_map/ppermute | solution.py:99
  211.7 10.9 %collective-permute-start.51 = (bf16[48,1536]{1,0:T(8,128)(2,1)S(1)}, bf16[48,1536]{1,0:T(8,128)(2,1)S(1)}, u32[]{:S(2)}, u32[]{:S(2)}) collective-permute-start(bf16[48,1536]{1,0:T(8,128)(2,1)S(1)} %collective-permute-done.46), channel_id=1, source_target_pairs={{0,8},{1,9},{2,10},{3,11},{4,12},{5,13},{6,14},{7,15},{8,0},{9,1},... | collective-permute-start | bytes 442376 | tf_op jit(solution)/shard_map/ppermute | solution.py:99
  213.7 8.2 %collective-permute-start.50 = (bf16[144,1536]{1,0:T(8,128)(2,1)}, bf16[144,1536]{1,0:T(8,128)(2,1)S(1)}, u32[]{:S(2)}, u32[]{:S(2)}) collective-permute-start(bf16[144,1536]{1,0:T(8,128)(2,1)} %collective-permute-done.45), channel_id=1, source_target_pairs={{0,8},{1,9},{2,10},{3,11},{4,12},{5,13},{6,14},{7,15},{8,0},{9,1},... | collective-permute-start | bytes 1327112 | tf_op jit(solution)/shard_map/ppermute | solution.py:99
  214.6 17.7 %collective-permute-start.35 = (bf16[144,1536]{1,0:T(8,128)(2,1)S(1)}, bf16[144,1536]{1,0:T(8,128)(2,1)S(1)}, u32[]{:S(2)}, u32[]{:S(2)}) collective-permute-start(bf16[144,1536]{1,0:T(8,128)(2,1)S(1)} %slice.98), channel_id=1, source_target_pairs={{0,4},{1,5},{2,6},{3,7},{4,0},{5,1},{6,2},{7,3},{8,12},{9,13},{10,... | collective-permute-start | bytes 1327112 | tf_op jit(solution)/shard_map/ppermute | solution.py:99
  218.2 6.0 %collective-permute-start.36 = (bf16[48,1536]{1,0:T(8,128)(2,1)S(1)}, bf16[48,1536]{1,0:T(8,128)(2,1)S(1)}, u32[]{:S(2)}, u32[]{:S(2)}) collective-permute-start(bf16[48,1536]{1,0:T(8,128)(2,1)S(1)} %slice.99), channel_id=1, source_target_pairs={{0,1},{1,0},{2,3},{3,2},{4,5},{5,4},{6,7},{7,6},{8,9},{9,8},{10,11... | collective-permute-start | bytes 442376 | tf_op jit(solution)/shard_map/ppermute | solution.py:99
  221.9 22.1 %collective-permute-start.38 = (bf16[192,1536]{1,0:T(8,128)(2,1)S(1)}, bf16[192,1536]{1,0:T(8,128)(2,1)S(1)}, u32[]{:S(2)}, u32[]{:S(2)}) collective-permute-start(bf16[192,1536]{1,0:T(8,128)(2,1)S(1)} %collective-permute-done.33), channel_id=1, source_target_pairs={{0,8},{1,9},{2,10},{3,11},{4,12},{5,13},{6,14},{7,15},{8,0},{9,1},... | collective-permute-start | bytes 1769480 | tf_op jit(solution)/shard_map/ppermute | solution.py:99
  222.7 22.1 %collective-permute-start.39 = (bf16[192,1536]{1,0:T(8,128)(2,1)S(1)}, bf16[192,1536]{1,0:T(8,128)(2,1)S(1)}, u32[]{:S(2)}, u32[]{:S(2)}) collective-permute-start(bf16[192,1536]{1,0:T(8,128)(2,1)S(1)} %collective-permute-done.34), channel_id=1, source_target_pairs={{0,8},{1,9},{2,10},{3,11},{4,12},{5,13},{6,14},{7,15},{8,0},{9,1},... | collective-permute-start | bytes 1769480 | tf_op jit(solution)/shard_map/ppermute | solution.py:99
  224.2 22.3 %collective-permute-start.41 = (bf16[48,1536]{1,0:T(8,128)(2,1)S(1)}, bf16[48,1536]{1,0:T(8,128)(2,1)S(1)}, u32[]{:S(2)}, u32[]{:S(2)}) collective-permute-start(bf16[48,1536]{1,0:T(8,128)(2,1)S(1)} %collective-permute-done.36), channel_id=1, source_target_pairs={{0,8},{1,9},{2,10},{3,11},{4,12},{5,13},{6,14},{7,15},{8,0},{9,1},... | collective-permute-start | bytes 442376 | tf_op jit(solution)/shard_map/ppermute | solution.py:99
  224.9 5.0 %copy-start.3 = (bf16[1536,1536]{1,0:T(8,128)(2,1)S(1)}, bf16[1536,1536]{1,0:T(8,128)(2,1)}, u32[]{:S(2)}) copy-start(bf16[1536,1536]{1,0:T(8,128)(2,1)} %constant_dynamic-update-slice_fusion.10) | copy-start | bytes 14155780
  232.4 72.1 %collective-permute-start.52 = (bf16[192,1536]{1,0:T(8,128)(2,1)}, bf16[192,1536]{1,0:T(8,128)(2,1)}, u32[]{:S(2)}, u32[]{:S(2)}) collective-permute-start(bf16[192,1536]{1,0:T(8,128)(2,1)} %convolution_convert_fusion.1), channel_id=1, source_target_pairs={{0,8},{1,9},{2,16},{3,17},{4,12},{5,13},{6,20},{7,21},{8,10},{9,11... | collective-permute-start | bytes 1769480 | tf_op jit(solution)/shard_map/ppermute | solution.py:99
  237.1 65.2 %collective-permute-start.53 = (bf16[192,1536]{1,0:T(8,128)(2,1)}, bf16[192,1536]{1,0:T(8,128)(2,1)}, u32[]{:S(2)}, u32[]{:S(2)}) collective-permute-start(bf16[192,1536]{1,0:T(8,128)(2,1)} %get-tuple-element.21), channel_id=1, source_target_pairs={{0,0},{1,1},{2,8},{3,9},{4,4},{5,5},{6,12},{7,13},{8,2},{9,3},{10,... | collective-permute-start | bytes 1769480 | tf_op jit(solution)/shard_map/ppermute | solution.py:99
  243.9 1.8 collective-permute-start.40
  247.2 54.5 %copy-start.6 = (f32[8,8]{1,0:T(8,128)S(1)}, f32[8,8]{1,0:T(8,128)}, u32[]{:S(2)}) copy-start(f32[8,8]{1,0:T(8,128)} %param.9) | copy-start | bytes 772
  254.6 49.9 %collective-permute-start.42 = (bf16[192,1536]{1,0:T(8,128)(2,1)}, bf16[192,1536]{1,0:T(8,128)(2,1)S(1)}, u32[]{:S(2)}, u32[]{:S(2)}) collective-permute-start(bf16[192,1536]{1,0:T(8,128)(2,1)} %get-tuple-element.19), channel_id=1, source_target_pairs={{0,0},{1,1},{2,8},{3,9},{4,4},{5,5},{6,12},{7,13},{8,2},{9,3},{10,... | collective-permute-start | bytes 1769480 | tf_op jit(solution)/shard_map/ppermute | solution.py:99

commit v3 on v1

v3 whole, which is shorter than its diff:
```python
import functools
import jax
import jax.numpy as jnp
from jax import lax
from jax.experimental import pallas as pl
from jax.experimental.pallas import tpu as pltpu
from jax.sharding import PartitionSpec as P

F32, BF16 = jnp.float32, jnp.bfloat16
NT = (((1,), (1,)), ((), ()))
NN = (((1,), (0,)), ((), ()))
AXES = ("tm", "row", "col")
HIGHEST = lax.Precision.HIGHEST


def native(t, c):
    return t % 2 == c // (lax.axis_size("col") // 2)


def move(block, target):
    tms, rows, cols = (lax.axis_size(a) for a in AXES)
    flat = lambda t, r, c: (t * rows + r) * cols + c
    devices = [(t, r, c) for t in range(tms) for r in range(rows) for c in range(cols)]
    route = [(flat(*d), flat(*target(*d))) for d in devices if target(*d) is not None]
    return lax.ppermute(block, AXES, route)


def swapped(t, r, c):
    cols = lax.axis_size("col")
    return (t, r, c) if native(t, c) else (t ^ 1, r, (c + cols // 2) % cols)


def by_row(t, r, c):
    return t, r ^ 1, c


def by_col(t, r, c):
    return t, r, c ^ 1


def by_core(t, r, c):
    return t ^ 1, r, c


def only(keep, target):
    return lambda t, r, c: target(t, r, c) if native(t, c) == keep else None


def swap_or_row(t, r, c):
    return (by_row if native(t, c) else swapped)(t, r, c)


def handed_to(t, r, c):
    half = lax.axis_size("col") // 2
    part = t // 2 * 2 + c // half + 1
    return None if part >= lax.axis_size("tm") else (part, r, c % half + t % 2 * half)


def groups():
    tms, rows, cols = (lax.axis_size(a) for a in AXES)
    half = cols // 2
    return [
        [((2 * x + k) * rows + r) * cols + h * half + c for r in range(rows) for k in range(2) for c in range(half)]
        for x in range(tms // 2)
        for h in range(2)
    ]


def after(value, *others):
    return lax.optimization_barrier((value, *others))[0]


def spread(top, bottom, share):
    rows, half = lax.axis_size("row"), lax.axis_size("col") // 2
    core = lax.axis_index("tm") % 2
    r, c = lax.axis_index("row"), lax.axis_index("col") % half
    stays = core == lax.axis_index("col") // half
    cut = top.shape[0]
    both = jnp.concatenate([top, bottom], axis=0)
    if rows != 2 or half != 2:
        own = move(both, swapped)
        whole = [
            lax.all_gather(x, AXES, axis=0, tiled=False, axis_index_groups=groups())
            for x in (own[:cut], own[cut:])
        ]
        pieces = [[(w[i], 0) for i in range(rows * 2 * half)] for w in whole]
        places = jnp.arange(rows * 2 * half, dtype=jnp.int32)
        return own, pieces, jnp.concatenate([places, places]), (own,)
    first = move(both, swap_or_row)
    second = move(both, only(True, by_col))
    own = jnp.where(stays, both, first)
    top_diag = move(jnp.where(stays, second[:cut], first[:cut]), by_row)
    low_diag = move(first[cut:], by_col)
    low_row = move(first[cut:], only(False, by_row))
    top_col = move(first[:cut], only(False, by_col))
    top_last = move(top_col, only(False, by_row))
    low_last = move(low_row, only(False, by_col))
    third = jnp.where(stays, both, jnp.concatenate([top_col, low_row], axis=0))
    fourth = jnp.where(stays, second, jnp.concatenate([top_last, low_last], axis=0))
    mine = [first, top_diag, low_diag, third, fourth]
    other = [move(x, by_core) for x in mine]

    def place(k, stays, when, otherwise):
        dr, dc = (jnp.where(stays, a, b) for a, b in zip(when, otherwise))
        return ((r ^ dr) * 2 + k) * half + (c ^ dc)

    moves = ((1, 0), (0, 0)), ((1, 1), (1, 0)), ((1, 1), (0, 1)), ((0, 0), (0, 1)), ((0, 0), (1, 0)), ((0, 1), (1, 1))
    order = (0, 1, 3, 5), (0, 2, 4, 5)
    places = [
        place(k, s, *moves[i]) for o in order for k, s in ((core, stays), (1 - core, ~stays)) for i in o
    ]
    tops = [(x, 0) for side in (mine, other) for x in (side[0], side[1], side[3], side[4])]
    lows = [
        (x, f) for side in (mine, other) for x, f in ((side[0], cut), (side[2], 0), (side[3], cut), (side[4], cut))
    ]
    return own, (tops, lows), jnp.stack(places).astype(jnp.int32), (top_diag, low_diag)


def mm(a, b, dims=NN, precision=None):
    return lax.dot_general(a, b, dims, preferred_element_type=F32, precision=precision)


def split(a):
    hi = a.astype(BF16)
    return hi, (a - hi.astype(F32)).astype(BF16)


def mm3(a, b):
    return mm(a[0], b[0]) + (mm(a[0], b[1]) + mm(a[1], b[0]))


def grid_of(rows, cols, first_row=0, first_col=0):
    row = lax.broadcasted_iota(jnp.int32, (rows, cols), 0) + first_row
    return row, lax.broadcasted_iota(jnp.int32, (rows, cols), 1) + first_col


def copies(firsts, share, places, offset, pieces, whole, sems):
    started = []
    for i, (first, piece) in enumerate(zip(firsts, pieces)):
        at = pl.ds(pl.multiple_of(places[offset + i] * share, 8), share)
        started.append(pltpu.make_async_copy(piece.at[pl.ds(first, share)], whole.at[at], sems.at[i]))
        started[-1].start()
    return started


def wait(started):
    for copy in started:
        copy.wait()


def keep_lower(whole, size):
    n = whole.shape[0]
    for k in range(n // size):
        rows = pl.ds(k * size, size)
        row, col = grid_of(size, n, k * size)
        whole[rows, :] = jnp.where(col <= row, whole[rows, :].astype(F32), 0.0).astype(BF16)


def middle_kernel(size, share, firsts, places, *refs):
    count = len(firsts[0])
    tops, lows = refs[:count], refs[count : 2 * count]
    mid_ref, inverse, rhs, sems = refs[2 * count :]
    one = copies(firsts[0], share, places, 0, tops, inverse, sems.at[0])
    two = copies(firsts[1], share, places, count, lows, rhs, sems.at[1])
    wait(one)
    keep_lower(inverse, size)
    wait(two)
    for k in range(mid_ref.shape[0] // size):
        rows, depth = pl.ds(k * size, size), pl.ds(0, (k + 1) * size)
        mid_ref[:, rows] = mm(rhs[:, depth], inverse[rows, depth], NT).astype(BF16)


def spd_inverse(block, quick):
    size = block.shape[0]
    row, col = grid_of(size, size)
    eye = (row == col).astype(F32)
    start = eye / jnp.sum(jnp.abs(block), axis=0, keepdims=True)
    parts = split(block)
    guess = start
    for _ in range(quick):
        short = guess.astype(BF16)
        guess = 2.0 * guess - mm(short, mm(parts[0], short).astype(BF16))

    def gap_of(x):
        gap = eye - mm3(parts, split(x))
        return gap, jnp.max(jnp.sum(jnp.abs(gap), axis=0, keepdims=True))

    _, worst = gap_of(guess)
    good = worst < 0.5
    guess = jnp.where(good, guess, start)

    def go(state):
        turn, worst, _ = state
        return jnp.logical_and(turn < 60, worst > 2e-2)

    def step(state):
        turn, _, x = state
        gap, _ = gap_of(x)
        x = x + mm3(split(x), split(gap))
        return turn + 1, gap_of(x)[1], x

    guess = lax.while_loop(go, step, (0, jnp.where(good, worst, 1.0), guess))[2]
    return guess + mm3(split(guess), split(gap_of(guess)[0]))


def factor_kernel(size, quick, share, firsts, places, mid, diag, *refs):
    count = len(firsts)
    tops = refs[:count]
    low_ref, inv_ref, packed, block, sems = refs[count:]
    started = copies(firsts, share, places, 0, tops, packed, sems)
    blocks = mid.shape[0] // size
    at = lambda k: pl.ds(k * size, size)
    wait(started)
    for k in range(blocks):
        for j in range(k, blocks):
            own = packed[at(k), at(j)].astype(F32)
            if j == k:
                row, col = grid_of(size, size)
                own = jnp.where(col > row, own, 0.0)
                own = own + own.T + jnp.where(col == row, diag[:, at(k)], 0.0)
            else:
                own = own.T
            block[at(j), at(k)] = own - mm(mid[at(j), :], mid[at(k), :], NT)
    for k in range(blocks):
        inverse = spd_inverse(block[at(k), at(k)], quick).astype(BF16)
        inv_ref[at(k), :] = inverse
        for j in range(k + 1, blocks):
            low_ref[at(j), at(k)] = mm(block[at(j), at(k)].astype(BF16), inverse).astype(BF16)
        for j in range(k + 1, blocks):
            low = low_ref[at(j), at(k)]
            for i in range(j, blocks):
                block[at(i), at(j)] -= mm(block[at(i), at(k)].astype(BF16), low, NT)


def solve_kernel(size, share, firsts, places, mid, low_ref, inv, own_top, own_low, arrows, *refs):
    count = len(firsts)
    tops = refs[:count]
    upper_ref, left_ref, tip_ref, inverse, top, rows, solved, sems = refs[count:]
    started = copies(firsts, share, places, 0, tops, inverse, sems)
    n = mid.shape[0]
    blocks, fixed = n // size, arrows.shape[0] // 2
    at = lambda k: pl.ds(k * size, size)
    wait(started)
    keep_lower(inverse, size)
    terms, rest = [], arrows[:fixed]
    for _ in range(3):
        terms.append(rest.astype(BF16).astype(F32))
        rest = rest - terms[-1]
    thin = jnp.concatenate(terms, axis=0).astype(BF16)
    arrow_parts = mm(thin, inverse[...], NT)
    arrow_one = arrow_parts[:fixed] + arrow_parts[fixed : 2 * fixed] + arrow_parts[2 * fixed :]
    for k in range(blocks):
        depth = pl.ds(0, (k + 1) * size)
        top[:, at(k)] = mm(own_top[:, depth], inverse[at(k), depth], NT).astype(BF16)
    rows[:share] = -mm(top[...], mid[...], NT)
    rows[share : 2 * share] = own_low[...].astype(F32)
    arrow_two = arrows[fixed:] - mm(arrow_one.astype(BF16), mid[...], NT)
    rows[2 * share :] = arrow_two
    for k in range(blocks):
        row = rows[:, at(k)].astype(BF16)
        solved[:, at(k)] = mm(row, inv[at(k), :])
        if k + 1 < blocks:
            rest = pl.ds((k + 1) * size, n - (k + 1) * size)
            rows[:, rest] -= mm(row, low_ref[rest, at(k)], NT)
    for k in range(blocks - 2, -1, -1):
        rest = pl.ds((k + 1) * size, n - (k + 1) * size)
        solved[:, at(k)] -= mm(solved[:, rest].astype(BF16), low_ref[rest, at(k)])
    upper_ref[...] = solved[: 2 * share].astype(BF16)
    left = (top[...].astype(F32) - mm(upper_ref[:share], mid[...])).astype(BF16)
    for k in range(blocks):
        depth = pl.ds(k * size, n - k * size)
        left_ref[:, at(k)] = mm(left[:, k * size :], inverse[depth, at(k)]).astype(BF16)
    tip_ref[...] = mm(arrow_one, arrow_one, NT, HIGHEST) + mm(solved[2 * share :], arrow_two, NT, HIGHEST)


def product_kernel(share, firsts, offset, signs, places, left, *refs):
    count = len(firsts)
    pieces = refs[:count]
    outs, (whole, sems) = refs[count:-2], refs[-2:]
    started = copies(firsts, share, places, offset, pieces, whole, sems)
    wait(started)
    for i, sign in enumerate(signs):
        product = mm(left[i * share : (i + 1) * share], whole[...], NT)
        product = product if sign > 0 else -product
        outs[2 * i][...] = product
        outs[2 * i + 1][...] = product.astype(BF16)


VMEM = pl.BlockSpec(memory_space=pltpu.VMEM)
ANY = pl.BlockSpec(memory_space=pl.ANY)
SMEM = pl.BlockSpec(memory_space=pltpu.SMEM)


def call(kernel, name, outs, places, dense, pieces, scratch, flops):
    arrays = [array for array, _ in pieces]
    size = lambda x: x.size * x.dtype.itemsize
    return pl.pallas_call(
        kernel,
        out_shape=outs,
        in_specs=[SMEM] + [VMEM] * len(dense) + [ANY] * len(arrays),
        out_specs=[VMEM] * len(outs),
        scratch_shapes=scratch,
        compiler_params=pltpu.CompilerParams(vmem_limit_bytes=60 << 20),
        cost_estimate=pl.CostEstimate(
            flops=flops, bytes_accessed=sum(map(size, [*dense, *arrays, *outs])), transcendentals=0
        ),
        name=name,
    )(places, *dense, *arrays)


def shards(first_inverse, second_diag, coupling, arrow_rows, tip_block):
    share, n = coupling.shape[2:]
    size = 256 if n % 256 == 0 else 128
    cols = lax.axis_size("col")
    half, fixed = cols // 2, arrow_rows.shape[2]
    core, col = lax.axis_index("tm") % 2, lax.axis_index("col")
    stays = core == col // half
    shape = jax.ShapeDtypeStruct
    dma = pltpu.SemaphoreType.DMA

    row, column = grid_of(share, n, (lax.axis_index("row") * cols + col) * share)
    diag_own = jnp.sum(jnp.where(row == column, second_diag[0], 0), axis=0, keepdims=True)
    packed = jnp.where(column <= row, first_inverse[0], second_diag[0])
    packed = jnp.concatenate([packed, jnp.pad(diag_own, ((0, 15), (0, 0)))], axis=0)
    arrows = move(arrow_rows[0].reshape(2 * fixed, n), swapped)
    _, (tops, lows), places, gate = spread(packed, coupling[0, 1], share)
    low_share, top_share = after(coupling[0, 2], *gate), after(coupling[0, 0], *gate)
    own, (low_pieces, top_pieces), later, _ = spread(low_share, top_share, share)
    own_low, own_top = own[:share], own[share:]
    diag = sum(array[share : share + 1].astype(F32) for array, _ in tops)

    firsts = [[f for _, f in p] for p in (tops, lows)]
    count = len(tops)
    whole = pltpu.VMEM((n, n), BF16)
    (mid,) = call(
        functools.partial(middle_kernel, size, share, firsts), "middle",
        [shape((n, n), BF16)], places, [], tops + lows, [whole, whole, dma((2, count))], n**3,
    )
    low, inverses = call(
        functools.partial(factor_kernel, size, 4, share, firsts[0]), "factor",
        [shape((n, n), BF16), shape((n, size), BF16)], places, [mid, diag], tops,
        [whole, pltpu.VMEM((n, n), F32), dma((count,))], 2 * n**3,
    )
    solved, left, tip_terms = call(
        functools.partial(solve_kernel, size, share, firsts[0]), "solve",
        [shape((2 * share, n), BF16), shape((share, n), BF16), shape((fixed, fixed), F32)],
        places, [mid, low, inverses, own_top, own_low, arrows], tops,
        [whole, pltpu.VMEM((share, n), BF16), pltpu.VMEM((2 * share + fixed, n), F32),
         pltpu.VMEM((2 * share + fixed, n), F32), dma((count,))], 8 * share * n * n,
    )
    out = [shape((share, n), F32), shape((share, n), BF16)]
    firsts = [[f for _, f in p] for p in (low_pieces, top_pieces)]
    fill_block, fill_sent, _, handed = call(
        functools.partial(product_kernel, share, firsts[0], 0, (-1, 1)), "fill",
        out + out, later, [solved], low_pieces, [whole, dma((count,))], 4 * share * n * n,
    )
    incoming = move(handed, handed_to)
    fill_far = move(fill_sent, swapped)
    own_update, update_sent = call(
        functools.partial(product_kernel, share, firsts[1], count, (1,)), "update",
        out, later, [left], top_pieces, [whole, dma((count,))], 2 * share * n * n,
    )
    update_far = move(update_sent, swapped)
    speaks = jnp.logical_and(stays, col % half == 0) & (lax.axis_index("row") >= 0)
    tip_total = lax.psum(jnp.where(speaks, tip_terms, 0.0), ("tm", "col"))
    fill_block = jnp.where(stays, fill_block, fill_far.astype(F32))
    update = jnp.where(stays, own_update, update_far.astype(F32)) + incoming.astype(F32)
    return (update[None], fill_block[None], tip_block - tip_total)


def solution(mesh):
    return jax.shard_map(
        shards,
        mesh=mesh,
        in_specs=(
            P("tm", ("row", "col"), None),
            P("tm", ("row", "col"), None),
            P("tm", None, ("row", "col"), None),
            P("tm", None, None, None),
            P(),
        ),
        out_specs=(P("tm", ("row", "col"), None), P("tm", ("row", "col"), None), P()),
        check_vma=False,
    )
```

time: 424 us -> 287 us (0.68); the launches traced: 424 us -> 282 us
  waiting for transfers between devices: 295 us -> 54.3 us
  starting transfers between devices: 1.55 us -> 71.1 us
  matrix products: 60.2 us -> 0 us
  Pallas kernels: 35.5 us -> 80 us
  blocking collectives: 8.74 us -> 52.2 us
  between operations: 13.9 us -> 1.58 us
  other arithmetic: 6.69 us -> 15.5 us
  local copies, waits for them, and re-layouts: 2.75 us -> 7.66 us
    all_gather x5 -> x0, waiting for transfers between devices: 292 us -> none  [gather_block(): return lax.all_gather(one_share, ('row', 'col'), axis=0, tiled=True)]
    ppermute x1 -> x30, starting transfers between devices: 1.35 us -> 71.1 us  [move(): return lax.ppermute(block, AXES, route)]
    dot_general x12 -> x0, matrix products: 60.2 us -> none  [the longest x9 52.8 us: mm(): return lax.dot_general(a, b, dims, preferred_element_type=F32)]
    ppermute x1 -> x30, waiting for transfers between devices: 0.01 us -> 54.3 us  [move(): return lax.ppermute(block, AXES, route)]
    pallas_call x1 -> x5, Pallas kernels: 35.5 us -> 80 us  [call(): pl.pallas_call(kernel, out_shape=outs, in_specs=[SMEM] + [VMEM] * len(den...]
    psum x1, blocking collectives: 8.74 us -> 52.2 us  [shards(): tip_total = lax.psum(jnp.where(speaks, tip_terms, 0.0), ('tm', 'col'))]
    select_n x0 -> x6, other arithmetic: none -> 6.87 us  [the longest x2 3.4 us: spread(): third = jnp.where(stays, both, jnp.concatenate([top_col, low_row], axis=0))]
  transfers between devices with their start and end apart: 6 -> 30, of which waited for: 5 -> 5; matrix products, arithmetic and copies ran while one was open for 15% -> 5% of each run, Pallas kernels for 8% -> 28%
where the time goes in v3:
time: 287 us; the launch traced here: 282 us
  Pallas kernels  80 us (28%)
  starting transfers between devices  71.1 us (25%)
  waiting for transfers between devices  54.3 us (19%)
  blocking collectives  52.2 us (18%)
  other arithmetic  15.5 us (5%)
  local copies, waits for them, and re-layouts  7.66 us (3%)
    pallas_call x5, Pallas kernels, call(): pl.pallas_call(kernel, out_shape=outs, in_specs=[SMEM] + [VMEM] * len(den...  80 us
    ppermute x30, starting transfers between devices, move(): return lax.ppermute(block, AXES, route)  71.1 us
    ppermute x30, waiting for transfers between devices, move(): return lax.ppermute(block, AXES, route)  54.3 us
    psum x1, blocking collectives, shards(): tip_total = lax.psum(jnp.where(speaks, tip_terms, 0.0), ('tm', 'col'))  52.2 us
  transfers between devices with their start and end apart: 30, of which 5 were waited for; matrix products, arithmetic and copies ran while one was open for 5% of the time, Pallas kernels for 28%

profile of v3, /device:TPU:0, one launch (start us, length us, event | category | flops | bytes accessed | tf_op | source)
XLA Modules:
  0.0 282.4 jit_solution(6851989384219720055)
XLA Ops:
  0.7 1.8 fusion.4
  2.5 1.1 slice_bitcast_fusion
  3.6 0.8 copy-done.3
  4.5 1.2 fusion.3
  5.6 3.0 %collective-permute-start = (bf16[400,1536]{1,0:T(8,128)(2,1)}, bf16[400,1536]{1,0:T(8,128)(2,1)S(1)}, u32[]{:S(2)}, u32[]{:S(2)}) collective-permute-start(bf16[400,1536]{1,0:T(8,128)(2,1)} %fusion.3), channel_id=1, source_target_pairs={{0,4},{1,5},{2,8},{3,9},{4,0},{5,1},{6,12},{7,13},{8,2},{9,3},{10,... | collective-permute-start | bytes 3686408 | tf_op jit(solution)/shard_map/ppermute | solution.py:25
  8.6 3.5 %collective-permute-start.1 = (bf16[400,1536]{1,0:T(8,128)(2,1)}, bf16[400,1536]{1,0:T(8,128)(2,1)S(1)}, u32[]{:S(2)}, u32[]{:S(2)}) collective-permute-start(bf16[400,1536]{1,0:T(8,128)(2,1)} %fusion.3), channel_id=1, source_target_pairs={{0,1},{1,0},{4,5},{5,4},{10,11},{11,10},{14,15},{15,14},{16,17},{1... | collective-permute-start | bytes 3686408 | tf_op jit(solution)/shard_map/ppermute | solution.py:25
  12.1 11.4 %collective-permute-done.refs_0_.refs_8_ = bf16[400,1536]{1,0:T(8,128)(2,1)S(1)} collective-permute-done((bf16[400,1536]{1,0:T(8,128)(2,1)}, bf16[400,1536]{1,0:T(8,128)(2,1)S(1)}, u32[]{:S(2)}, u32[]{:S(2)}) %collective-permute-start) | collective-permute-done | bytes 1228832 | tf_op jit(solution)/shard_map/ppermute | solution.py:25
  23.5 16.0 %collective-permute-done.1 = bf16[400,1536]{1,0:T(8,128)(2,1)S(1)} collective-permute-done((bf16[400,1536]{1,0:T(8,128)(2,1)}, bf16[400,1536]{1,0:T(8,128)(2,1)S(1)}, u32[]{:S(2)}, u32[]{:S(2)}) %collective-permute-start.1) | collective-permute-done | bytes 1228832 | tf_op jit(solution)/shard_map/ppermute | solution.py:25
  39.5 0.1 fusion.14
  39.6 1.0 copy-done.7
  40.6 0.1 collective-permute-start.2
  40.7 1.3 collective-permute-start.11
  42.0 13.4 %collective-permute-done.11.refs_9_ = bf16[192,1536]{1,0:T(8,128)(2,1)S(1)} collective-permute-done((bf16[192,1536]{1,0:T(8,128)(2,1)S(1)}, bf16[192,1536]{1,0:T(8,128)(2,1)S(1)}, u32[]{:S(2)}, u32[]{:S(2)}) %collective-permute-start.11) | collective-permute-done | bytes 589856 | tf_op jit(solution)/shard_map/ppermute | solution.py:25
  55.4 0.0 collective-permute-done.2.refs_1_
  55.5 0.0 copy-start.9
  55.5 1.3 collective-permute-start.13
  56.8 2.7 collective-permute-start.18
  59.5 0.7 collective-permute-start.3
  60.2 0.7 collective-permute-start.4
  60.9 4.5 %collective-permute-start.7 = (bf16[400,1536]{1,0:T(8,128)(2,1)S(1)}, bf16[400,1536]{1,0:T(8,128)(2,1)}, u32[]{:S(2)}, u32[]{:S(2)}) collective-permute-start(bf16[400,1536]{1,0:T(8,128)(2,1)S(1)} %collective-permute-done.refs_0_.refs_8_), channel_id=1, source_target_pairs={{0,8},{1,9},{2,10},{3,11},{4,12},{5,13},{6,14},{7,15},{8,0},{9,1},... | collective-permute-start | bytes 3686408 | tf_op jit(solution)/shard_map/ppermute | solution.py:25
  65.4 0.7 collective-permute-start.6
  66.1 0.7 collective-permute-start.5
  66.9 0.3 maximum_select_fusion.refs_2_.refs_10_
  67.2 9.6 %collective-permute-done.13.refs_0_ = bf16[384,1536]{1,0:T(8,128)(2,1)} collective-permute-done((bf16[384,1536]{1,0:T(8,128)(2,1)S(1)}, bf16[384,1536]{1,0:T(8,128)(2,1)}, u32[]{:S(2)}, u32[]{:S(2)}) %collective-permute-start.13) | collective-permute-done | bytes 1179680 | tf_op jit(solution)/shard_map/ppermute | solution.py:25
  76.8 17.0 %collective-permute-start.9 = (bf16[400,1536]{1,0:T(8,128)(2,1)S(1)}, bf16[400,1536]{1,0:T(8,128)(2,1)}, u32[]{:S(2)}, u32[]{:S(2)}) collective-permute-start(bf16[400,1536]{1,0:T(8,128)(2,1)S(1)} %maximum_select_fusion.refs_2_.refs_10_), channel_id=1, source_target_pairs={{0,8},{1,9},{2,10},{3,11},{4,12},{5,13},{6,14},{7,15},{8,0},{9,1},... | collective-permute-start | bytes 3686408 | tf_op jit(solution)/shard_map/ppermute | solution.py:25
  93.7 3.9 %collective-permute-done.18 = bf16[384,1536]{1,0:T(8,128)(2,1)S(1)} collective-permute-done((bf16[384,1536]{1,0:T(8,128)(2,1)S(1)}, bf16[384,1536]{1,0:T(8,128)(2,1)S(1)}, u32[]{:S(2)}, u32[]{:S(2)}) %collective-permute-start.18) | collective-permute-done | bytes 1179680 | tf_op jit(solution)/shard_map/ppermute | solution.py:25
  97.7 3.0 %fusion.15 = (bf16[192,1536]{1,0:T(8,128)(2,1)}, bf16[192,1536]{1,0:T(8,128)(2,1)}, bf16[192,1536]{1,0:T(8,128)(2,1)}) fusion(bf16[384,1536]{1,0:T(8,128)(2,1)} %collective-permute-done.13.refs_0_, bf16[384,1536]{1,0:T(8,128)(2,1)S(1)} %collective-permute-done.18, pred[]{:T(512)S(6)} %eq.18), kind=kLoop, calls=%fused_computation.43 | loop fusion | flops 294912 | bytes 3538945 | tf_op jit(solution)/shard_map/slice | solution.py:95
  100.7 1.5 collective-permute-start.16
  102.2 1.6 collective-permute-start.17
  103.8 1.4 maximum_select_fusion.1.refs_3_.refs_11_
  105.1 0.5 collective-permute-start.10
  105.6 0.6 stack.72.places
  106.2 2.4 collective-permute-start.8
  108.7 0.7 collective-permute-start.19
  109.4 3.1 %maximum_select_fusion.2 = (bf16[384,1536]{1,0:T(8,128)(2,1)}, bf16[384,1536]{1,0:T(8,128)(2,1)S(1)}) fusion(bf16[384,1536]{1,0:T(8,128)(2,1)} %copy-done.9, bf16[192,1536]{1,0:T(8,128)(2,1)} %collective-permute-done.17, bf16[192,1536]{1,0:T(8,128)(2,1)} %collective-permute-done.16, pred[]{:T(512)S(6)} %eq.18, ...), kind=kLoop, calls=%fused_computation.8 | loop fusion | flops 3538944 | bytes 5898241 | tf_op jit(solution)/shard_map/jit(_where)/select_n | solution.py:98
  112.5 0.8 collective-permute-start.20
  113.3 1.1 fusion.16
  114.4 0.8 collective-permute-start.14
  115.3 13.3 %collective-permute-start.12 = (bf16[192,1536]{1,0:T(8,128)(2,1)S(1)}, bf16[192,1536]{1,0:T(8,128)(2,1)S(1)}, u32[]{:S(2)}, u32[]{:S(2)}) collective-permute-start(bf16[192,1536]{1,0:T(8,128)(2,1)S(1)} %copy-done.21), channel_id=1, source_target_pairs={{0,8},{1,9},{2,10},{3,11},{4,12},{5,13},{6,14},{7,15},{8,0},{9,1},... | collective-permute-start | bytes 1769480 | tf_op jit(solution)/shard_map/ppermute | solution.py:25
  128.6 1.3 collective-permute-start.26
  129.9 1.4 fusion.7.diag
  131.3 0.5 collective-permute-start.23
  131.8 0.3 maximum_select_fusion.3.refs_3_
  132.1 0.0 copy-start.22
  132.2 0.8 copy-done.22
  133.0 0.1 collective-permute-start.24
  133.1 11.2 %middle.1.mid = bf16[1536,1536]{1,0:T(8,128)(2,1)} custom-call(s32[16]{0:T(128)} %stack.72.places, bf16[400,1536]{1,0:T(8,128)(2,1)} %copy-done, bf16[208,1536]{1,0:T(8,128)(2,1)} %copy-done.12, bf16[400,1536]{1,0:T(8,128)(2,1)} %copy-done.1, bf16[400,1536]{1,0:T(8,128)(2,1)} %maximum_select_fusion.1.refs_3_.refs_11_, ...), custom_call_target="tpu_custom_call" | custom-call | flops 3623878656 | bytes 21921792 | tf_op jit(solution)/shard_map/middle/pallas_call | solution.py:297
  144.3 0.1 collective-permute-start.15
  144.4 0.5 collective-permute-start.27
  144.9 36.6 %factor.1 = (bf16[1536,1536]{1,0:T(8,128)(2,1)}, bf16[1536,256]{1,0:T(8,128)(2,1)}) custom-call(s32[16]{0:T(128)} %stack.72.places, bf16[1536,1536]{1,0:T(8,128)(2,1)} %middle.1.mid, f32[1,1536]{1,0:T(1,128)} %fusion.7.diag, bf16[400,1536]{1,0:T(8,128)(2,1)} %copy-done, bf16[208,1536]{1,0:T(8,128)(2,1)} %copy-done.12, bf16[400,1536]{1,0:T(8,128)(2,1)} %copy-done.1, ...), custom_call_target="tpu_custom_call" | custom-call | flops 7247757312 | bytes 18880512 | tf_op jit(solution)/shard_map/factor/pallas_call | solution.py:297
  181.5 0.1 collective-permute-start.22
  181.7 17.4 %solve.1 = (bf16[384,1536]{1,0:T(8,128)(2,1)}, bf16[192,1536]{1,0:T(8,128)(2,1)}, f32[8,8]{1,0:T(8,128)}) custom-call(s32[16]{0:T(128)} %stack.72.places, bf16[1536,1536]{1,0:T(8,128)(2,1)} %middle.1.mid, bf16[1536,1536]{1,0:T(8,128)(2,1)} %get-tuple-element.15.low_ref, bf16[1536,256]{1,0:T(8,128)(2,1)} %get-tuple-element.16.inv, ...), custom_call_target="tpu_custom_call" | custom-call | flops 3623878656 | bytes 21922048 | tf_op jit(solution)/shard_map/solve/pallas_call | solution.py:297
  199.2 1.0 copy-done.5
  200.2 0.3 copy-done.6
  200.5 8.2 %fill.1 = (f32[192,1536]{1,0:T(8,128)}, bf16[192,1536]{1,0:T(8,128)(2,1)}, f32[192,1536]{1,0:T(8,128)}, bf16[192,1536]{1,0:T(8,128)(2,1)}) custom-call(s32[16]{0:T(128)} %stack.72.places, bf16[384,1536]{1,0:T(8,128)(2,1)} %get-tuple-element.22.left, bf16[384,1536]{1,0:T(8,128)(2,1)} %collective-permute-done.13.refs_0_, ...), custom_call_target="tpu_custom_call" | custom-call | flops 1811939328 | bytes 12976128 | tf_op jit(solution)/shard_map/fill/pallas_call | solution.py:297
  208.7 1.7 collective-permute-start.29
  210.5 6.6 %update.1 = (f32[192,1536]{1,0:T(8,128)}, bf16[192,1536]{1,0:T(8,128)(2,1)}) custom-call(s32[16]{0:T(128)} %stack.72.places, bf16[192,1536]{1,0:T(8,128)(2,1)} %get-tuple-element.19.left, bf16[384,1536]{1,0:T(8,128)(2,1)} %collective-permute-done.13.refs_0_, bf16[192,1536]{1,0:T(8,128)(2,1)} %collective-permute-done.15.refs_1_, ...), custom_call_target="tpu_custom_call" | custom-call | flops 905969664 | bytes 10616832 | tf_op jit(solution)/shard_map/update/pallas_call | solution.py:297
  217.1 1.7 collective-permute-start.25
  218.8 7.4 %collective-permute-start.28 = (bf16[192,1536]{1,0:T(8,128)(2,1)}, bf16[192,1536]{1,0:T(8,128)(2,1)S(1)}, u32[]{:S(2)}, u32[]{:S(2)}) collective-permute-start(bf16[192,1536]{1,0:T(8,128)(2,1)} %get-tuple-element.23), channel_id=1, source_target_pairs={{0,8},{1,9},{2,16},{3,17},{4,12},{5,13},{6,20},{7,21},{8,10},{9,11... | collective-permute-start | bytes 1769480 | tf_op jit(solution)/shard_map/ppermute | solution.py:25
  226.2 52.2 %psum.7 = f32[8,8]{1,0:T(8,128)S(1)} all-reduce(f32[8,8]{1,0:T(8,128)S(1)} %broadcast_select_fusion.1), channel_id=1, replica_groups=mesh['tm'=4,'row'=2,'col'=4] {'tm','col'}, use_global_device_ids=true, to_apply=%region_1.2 | all-reduce | flops 64 | bytes 512 | tf_op jit(solution)/shard_map/psum | solution.py:365
  278.5 0.6 sub.17
  279.1 1.1 select_bitcast_fusion
  280.2 0.6 copy-done.19
  280.8 1.2 add_bitcast_fusion
  (77 shorter events, 0.3 us)
Async XLA Ops:
  0.6 1.9 copy-start.17
  3.6 0.8 copy-start.3
  5.6 17.9 %collective-permute-start = (bf16[400,1536]{1,0:T(8,128)(2,1)}, bf16[400,1536]{1,0:T(8,128)(2,1)S(1)}, u32[]{:S(2)}, u32[]{:S(2)}) collective-permute-start(bf16[400,1536]{1,0:T(8,128)(2,1)} %fusion.3), channel_id=1, source_target_pairs={{0,4},{1,5},{2,8},{3,9},{4,0},{5,1},{6,12},{7,13},{8,2},{9,3},{10,... | collective-permute-start | bytes 3686408 | tf_op jit(solution)/shard_map/ppermute | solution.py:25
  8.6 30.9 %collective-permute-start.1 = (bf16[400,1536]{1,0:T(8,128)(2,1)}, bf16[400,1536]{1,0:T(8,128)(2,1)S(1)}, u32[]{:S(2)}, u32[]{:S(2)}) collective-permute-start(bf16[400,1536]{1,0:T(8,128)(2,1)} %fusion.3), channel_id=1, source_target_pairs={{0,1},{1,0},{4,5},{5,4},{10,11},{11,10},{14,15},{15,14},{16,17},{1... | collective-permute-start | bytes 3686408 | tf_op jit(solution)/shard_map/ppermute | solution.py:25
  23.5 106.4 %copy-start = (bf16[400,1536]{1,0:T(8,128)(2,1)}, bf16[400,1536]{1,0:T(8,128)(2,1)S(1)}, u32[]{:S(2)}) copy-start(bf16[400,1536]{1,0:T(8,128)(2,1)S(1)} %collective-permute-done.refs_0_.refs_8_) | copy-start | bytes 3686404
  39.5 1.1 copy-start.7
  40.6 14.8 %copy-start.16 = (bf16[192,1536]{1,0:T(8,128)(2,1)S(1)}, bf16[192,1536]{1,0:T(8,128)(2,1)}, u32[]{:S(2)}) copy-start(bf16[192,1536]{1,0:T(8,128)(2,1)} %get-tuple-element.17) | copy-start | bytes 1769476
  40.6 14.9 %copy-start.15 = (bf16[192,1536]{1,0:T(8,128)(2,1)S(1)}, bf16[192,1536]{1,0:T(8,128)(2,1)}, u32[]{:S(2)}) copy-start(bf16[192,1536]{1,0:T(8,128)(2,1)} %get-tuple-element.18) | copy-start | bytes 1769476
  40.6 14.8 %collective-permute-start.2 = (bf16[208,1536]{1,0:T(8,128)(2,1)S(1)}, bf16[208,1536]{1,0:T(8,128)(2,1)S(1)}, u32[]{:S(2)}, u32[]{:S(2)}) collective-permute-start(bf16[208,1536]{1,0:T(8,128)(2,1)S(1)} %get-tuple-element.31), channel_id=1, source_target_pairs={{0,4},{1,5},{2,6},{3,7},{4,0},{5,1},{6,2},{7,3},{8,12},{9,13},{10,... | collective-permute-start | bytes 1916936 | tf_op jit(solution)/shard_map/ppermute | solution.py:25
  40.7 26.2 %copy-start.4 = (bf16[192,1536]{1,0:T(8,128)(2,1)S(1)}, bf16[192,1536]{1,0:T(8,128)(2,1)}, u32[]{:S(2)}) copy-start(bf16[192,1536]{1,0:T(8,128)(2,1)} %copy-done.3) | copy-start | bytes 1769476
  40.7 14.7 %collective-permute-start.11 = (bf16[192,1536]{1,0:T(8,128)(2,1)S(1)}, bf16[192,1536]{1,0:T(8,128)(2,1)S(1)}, u32[]{:S(2)}, u32[]{:S(2)}) collective-permute-start(bf16[192,1536]{1,0:T(8,128)(2,1)S(1)} %slice.82), channel_id=1, source_target_pairs={{0,1},{1,0},{2,3},{3,2},{4,5},{5,4},{6,7},{7,6},{8,9},{9,8},{10,11... | collective-permute-start | bytes 1769480 | tf_op jit(solution)/shard_map/ppermute | solution.py:25
  55.4 10.7 %copy-start.20 = (bf16[192,1536]{1,0:T(8,128)(2,1)}, bf16[192,1536]{1,0:T(8,128)(2,1)S(1)}, u32[]{:S(2)}) copy-start(bf16[192,1536]{1,0:T(8,128)(2,1)S(1)} %collective-permute-done.11.refs_9_) | copy-start | bytes 1769476
  55.4 10.7 %copy-start.12 = (bf16[208,1536]{1,0:T(8,128)(2,1)}, bf16[208,1536]{1,0:T(8,128)(2,1)S(1)}, u32[]{:S(2)}) copy-start(bf16[208,1536]{1,0:T(8,128)(2,1)S(1)} %collective-permute-done.2.refs_1_) | copy-start | bytes 1916932
  55.5 11.6 %copy-start.9 = (bf16[384,1536]{1,0:T(8,128)(2,1)}, bf16[384,1536]{1,0:T(8,128)(2,1)S(1)}, u32[]{:S(2)}) copy-start(bf16[384,1536]{1,0:T(8,128)(2,1)S(1)} %constant_dynamic-update-slice_fusion) | copy-start | bytes 3538948
  55.5 21.2 %collective-permute-start.13 = (bf16[384,1536]{1,0:T(8,128)(2,1)S(1)}, bf16[384,1536]{1,0:T(8,128)(2,1)}, u32[]{:S(2)}, u32[]{:S(2)}) collective-permute-start(bf16[384,1536]{1,0:T(8,128)(2,1)S(1)} %constant_dynamic-update-slice_fusion), channel_id=1, source_target_pairs={{0,4},{1,5},{2,8},{3,9},{4,0},{5,1},{6,12},{7,13},{8,2},{9,3},{10,... | collective-permute-start | bytes 3538952 | tf_op jit(solution)/shard_map/ppermute | solution.py:25
  56.8 40.9 %collective-permute-start.18 = (bf16[384,1536]{1,0:T(8,128)(2,1)S(1)}, bf16[384,1536]{1,0:T(8,128)(2,1)S(1)}, u32[]{:S(2)}, u32[]{:S(2)}) collective-permute-start(bf16[384,1536]{1,0:T(8,128)(2,1)S(1)} %constant_dynamic-update-slice_fusion), channel_id=1, source_target_pairs={{0,1},{1,0},{4,5},{5,4},{10,11},{11,10},{14,15},{15,14},{16,17},{1... | collective-permute-start | bytes 3538952 | tf_op jit(solution)/shard_map/ppermute | solution.py:25
  59.5 6.6 %collective-permute-start.3 = (bf16[208,1536]{1,0:T(8,128)(2,1)S(1)}, bf16[208,1536]{1,0:T(8,128)(2,1)S(1)}, u32[]{:S(2)}, u32[]{:S(2)}) collective-permute-start(bf16[208,1536]{1,0:T(8,128)(2,1)S(1)} %get-tuple-element.30), channel_id=1, source_target_pairs={{2,3},{3,2},{6,7},{7,6},{8,9},{9,8},{12,13},{13,12},{18,19},{19,18... | collective-permute-start | bytes 1916936 | tf_op jit(solution)/shard_map/ppermute | solution.py:25
  60.2 5.2 %collective-permute-start.4 = (bf16[192,1536]{1,0:T(8,128)(2,1)S(1)}, bf16[192,1536]{1,0:T(8,128)(2,1)S(1)}, u32[]{:S(2)}, u32[]{:S(2)}) collective-permute-start(bf16[192,1536]{1,0:T(8,128)(2,1)S(1)} %slice.82), channel_id=1, source_target_pairs={{2,6},{3,7},{6,2},{7,3},{8,12},{9,13},{12,8},{13,9},{18,22},{19,23... | collective-permute-start | bytes 1769480 | tf_op jit(solution)/shard_map/ppermute | solution.py:25
  60.9 51.6 %collective-permute-start.7 = (bf16[400,1536]{1,0:T(8,128)(2,1)S(1)}, bf16[400,1536]{1,0:T(8,128)(2,1)}, u32[]{:S(2)}, u32[]{:S(2)}) collective-permute-start(bf16[400,1536]{1,0:T(8,128)(2,1)S(1)} %collective-permute-done.refs_0_.refs_8_), channel_id=1, source_target_pairs={{0,8},{1,9},{2,10},{3,11},{4,12},{5,13},{6,14},{7,15},{8,0},{9,1},... | collective-permute-start | bytes 3686408 | tf_op jit(solution)/shard_map/ppermute | solution.py:25
  65.4 36.7 %collective-permute-start.6 = (bf16[192,1536]{1,0:T(8,128)(2,1)S(1)}, bf16[192,1536]{1,0:T(8,128)(2,1)S(1)}, u32[]{:S(2)}, u32[]{:S(2)}) collective-permute-start(bf16[192,1536]{1,0:T(8,128)(2,1)S(1)} %collective-permute-done.4), channel_id=1, source_target_pairs={{2,3},{3,2},{6,7},{7,6},{8,9},{9,8},{12,13},{13,12},{18,19},{19,18... | collective-permute-start | bytes 1769480 | tf_op jit(solution)/shard_map/ppermute | solution.py:25
  66.1 37.6 %collective-permute-start.5 = (bf16[208,1536]{1,0:T(8,128)(2,1)S(1)}, bf16[208,1536]{1,0:T(8,128)(2,1)S(1)}, u32[]{:S(2)}, u32[]{:S(2)}) collective-permute-start(bf16[208,1536]{1,0:T(8,128)(2,1)S(1)} %collective-permute-done.3), channel_id=1, source_target_pairs={{2,6},{3,7},{6,2},{7,3},{8,12},{9,13},{12,8},{13,9},{18,22},{19,23... | collective-permute-start | bytes 1916936 | tf_op jit(solution)/shard_map/ppermute | solution.py:25
  67.2 62.7 %copy-start.1 = (bf16[400,1536]{1,0:T(8,128)(2,1)}, bf16[400,1536]{1,0:T(8,128)(2,1)S(1)}, u32[]{:S(2)}) copy-start(bf16[400,1536]{1,0:T(8,128)(2,1)S(1)} %maximum_select_fusion.refs_2_.refs_10_) | copy-start | bytes 3686404
  67.2 36.6 %copy-start.8 = (bf16[400,1536]{1,0:T(8,128)(2,1)S(1)}, bf16[400,1536]{1,0:T(8,128)(2,1)}, u32[]{:S(2)}) copy-start(bf16[400,1536]{1,0:T(8,128)(2,1)} %copy-done.7) | copy-start | bytes 3686404
  76.8 38.5 %collective-permute-start.9 = (bf16[400,1536]{1,0:T(8,128)(2,1)S(1)}, bf16[400,1536]{1,0:T(8,128)(2,1)}, u32[]{:S(2)}, u32[]{:S(2)}) collective-permute-start(bf16[400,1536]{1,0:T(8,128)(2,1)S(1)} %maximum_select_fusion.refs_2_.refs_10_), channel_id=1, source_target_pairs={{0,8},{1,9},{2,10},{3,11},{4,12},{5,13},{6,14},{7,15},{8,0},{9,1},... | collective-permute-start | bytes 3686408 | tf_op jit(solution)/shard_map/ppermute | solution.py:25
  97.7 3.0 %copy-start.10 = (bf16[384,1536]{1,0:T(8,128)(2,1)}, bf16[384,1536]{1,0:T(8,128)(2,1)S(1)}, u32[]{:S(2)}) copy-start(bf16[384,1536]{1,0:T(8,128)(2,1)S(1)} %collective-permute-done.18) | copy-start | bytes 3538948
  100.7 5.6 %collective-permute-start.16 = (bf16[192,1536]{1,0:T(8,128)(2,1)}, bf16[192,1536]{1,0:T(8,128)(2,1)}, u32[]{:S(2)}, u32[]{:S(2)}) collective-permute-start(bf16[192,1536]{1,0:T(8,128)(2,1)} %get-tuple-element.34), channel_id=1, source_target_pairs={{2,3},{3,2},{6,7},{7,6},{8,9},{9,8},{12,13},{13,12},{18,19},{19,18... | collective-permute-start | bytes 1769480 | tf_op jit(solution)/shard_map/ppermute | solution.py:25
  102.2 4.1 %copy-start.13 = (bf16[208,1536]{1,0:T(8,128)(2,1)S(1)}, bf16[208,1536]{1,0:T(8,128)(2,1)}, u32[]{:S(2)}) copy-start(bf16[208,1536]{1,0:T(8,128)(2,1)} %copy-done.12) | copy-start | bytes 1916932
  102.2 6.5 %collective-permute-start.17 = (bf16[192,1536]{1,0:T(8,128)(2,1)}, bf16[192,1536]{1,0:T(8,128)(2,1)}, u32[]{:S(2)}, u32[]{:S(2)}) collective-permute-start(bf16[192,1536]{1,0:T(8,128)(2,1)} %get-tuple-element.36), channel_id=1, source_target_pairs={{2,6},{3,7},{6,2},{7,3},{8,12},{9,13},{12,8},{13,9},{18,22},{19,23... | collective-permute-start | bytes 1769480 | tf_op jit(solution)/shard_map/ppermute | solution.py:25
  105.1 23.5 %collective-permute-start.10 = (bf16[400,1536]{1,0:T(8,128)(2,1)}, bf16[400,1536]{1,0:T(8,128)(2,1)}, u32[]{:S(2)}, u32[]{:S(2)}) collective-permute-start(bf16[400,1536]{1,0:T(8,128)(2,1)} %maximum_select_fusion.1.refs_3_.refs_11_), channel_id=1, source_target_pairs={{0,8},{1,9},{2,10},{3,11},{4,12},{5,13},{6,14},{7,15},{8,0},{9,1},... | collective-permute-start | bytes 3686408 | tf_op jit(solution)/shard_map/ppermute | solution.py:25
  106.2 8.2 %collective-permute-start.8 = (bf16[208,1536]{1,0:T(8,128)(2,1)S(1)}, bf16[208,1536]{1,0:T(8,128)(2,1)S(1)}, u32[]{:S(2)}, u32[]{:S(2)}) collective-permute-start(bf16[208,1536]{1,0:T(8,128)(2,1)S(1)} %copy-done.13), channel_id=1, source_target_pairs={{0,8},{1,9},{2,10},{3,11},{4,12},{5,13},{6,14},{7,15},{8,0},{9,1},... | collective-permute-start | bytes 1916936 | tf_op jit(solution)/shard_map/ppermute | solution.py:25
  108.7 22.6 %collective-permute-start.19 = (bf16[192,1536]{1,0:T(8,128)(2,1)}, bf16[192,1536]{1,0:T(8,128)(2,1)S(1)}, u32[]{:S(2)}, u32[]{:S(2)}) collective-permute-start(bf16[192,1536]{1,0:T(8,128)(2,1)} %collective-permute-done.16), channel_id=1, source_target_pairs={{2,6},{3,7},{6,2},{7,3},{8,12},{9,13},{12,8},{13,9},{18,22},{19,23... | collective-permute-start | bytes 1769480 | tf_op jit(solution)/shard_map/ppermute | solution.py:25
  112.5 2.0 copy-start.26
  112.5 2.8 %copy-start.21 = (bf16[192,1536]{1,0:T(8,128)(2,1)S(1)}, bf16[192,1536]{1,0:T(8,128)(2,1)}, u32[]{:S(2)}) copy-start(bf16[192,1536]{1,0:T(8,128)(2,1)} %copy-done.20) | copy-start | bytes 1769476
  112.5 19.4 %copy-start.11 = (bf16[384,1536]{1,0:T(8,128)(2,1)S(1)}, bf16[384,1536]{1,0:T(8,128)(2,1)}, u32[]{:S(2)}) copy-start(bf16[384,1536]{1,0:T(8,128)(2,1)} %copy-done.10) | copy-start | bytes 3538948
  112.5 18.8 %collective-permute-start.20 = (bf16[192,1536]{1,0:T(8,128)(2,1)}, bf16[192,1536]{1,0:T(8,128)(2,1)S(1)}, u32[]{:S(2)}, u32[]{:S(2)}) collective-permute-start(bf16[192,1536]{1,0:T(8,128)(2,1)} %collective-permute-done.17), channel_id=1, source_target_pairs={{2,3},{3,2},{6,7},{7,6},{8,9},{9,8},{12,13},{13,12},{18,19},{19,18... | collective-permute-start | bytes 1769480 | tf_op jit(solution)/shard_map/ppermute | solution.py:25
  114.4 17.7 %copy-start.14 = (bf16[208,1536]{1,0:T(8,128)(2,1)}, bf16[208,1536]{1,0:T(8,128)(2,1)S(1)}, u32[]{:S(2)}) copy-start(bf16[208,1536]{1,0:T(8,128)(2,1)S(1)} %collective-permute-done.8.refs_5_) | copy-start | bytes 1916932
  114.4 29.8 %collective-permute-start.14 = (f32[16,1536]{1,0:T(8,128)S(1)}, f32[16,1536]{1,0:T(8,128)S(1)}, u32[]{:S(2)}, u32[]{:S(2)}) collective-permute-start(f32[16,1536]{1,0:T(8,128)S(1)} %bitcast.28), channel_id=1, source_target_pairs={{0,0},{1,1},{2,8},{3,9},{4,4},{5,5},{6,12},{7,13},{8,2},{9,3},{10,... | collective-permute-start | bytes 294920 | tf_op jit(solution)/shard_map/ppermute | solution.py:25
  115.3 16.8 %collective-permute-start.12 = (bf16[192,1536]{1,0:T(8,128)(2,1)S(1)}, bf16[192,1536]{1,0:T(8,128)(2,1)S(1)}, u32[]{:S(2)}, u32[]{:S(2)}) collective-permute-start(bf16[192,1536]{1,0:T(8,128)(2,1)S(1)} %copy-done.21), channel_id=1, source_target_pairs={{0,8},{1,9},{2,10},{3,11},{4,12},{5,13},{6,14},{7,15},{8,0},{9,1},... | collective-permute-start | bytes 1769480 | tf_op jit(solution)/shard_map/ppermute | solution.py:25
  128.6 15.7 %collective-permute-start.26 = (bf16[192,1536]{1,0:T(8,128)(2,1)}, bf16[192,1536]{1,0:T(8,128)(2,1)}, u32[]{:S(2)}, u32[]{:S(2)}) collective-permute-start(bf16[192,1536]{1,0:T(8,128)(2,1)} %get-tuple-element.35), channel_id=1, source_target_pairs={{0,4},{1,5},{2,6},{3,7},{4,0},{5,1},{6,2},{7,3},{8,12},{9,13},{10,... | collective-permute-start | bytes 1769480 | tf_op jit(solution)/shard_map/ppermute | solution.py:25
  131.3 67.8 %collective-permute-start.21 = (bf16[384,1536]{1,0:T(8,128)(2,1)}, bf16[384,1536]{1,0:T(8,128)(2,1)S(1)}, u32[]{:S(2)}, u32[]{:S(2)}) collective-permute-start(bf16[384,1536]{1,0:T(8,128)(2,1)} %collective-permute-done.13.refs_0_), channel_id=1, source_target_pairs={{0,8},{1,9},{2,10},{3,11},{4,12},{5,13},{6,14},{7,15},{8,0},{9,1},... | collective-permute-start | bytes 3538952 | tf_op jit(solution)/shard_map/ppermute | solution.py:25
  131.3 67.8 %collective-permute-start.23 = (bf16[384,1536]{1,0:T(8,128)(2,1)}, bf16[384,1536]{1,0:T(8,128)(2,1)S(1)}, u32[]{:S(2)}, u32[]{:S(2)}) collective-permute-start(bf16[384,1536]{1,0:T(8,128)(2,1)} %get-tuple-element.32.refs_2_), channel_id=1, source_target_pairs={{0,8},{1,9},{2,10},{3,11},{4,12},{5,13},{6,14},{7,15},{8,0},{9,1},... | collective-permute-start | bytes 3538952 | tf_op jit(solution)/shard_map/ppermute | solution.py:25
  132.1 12.1 %copy-start.2 = (bf16[384,1536]{1,0:T(8,128)(2,1)}, bf16[384,1536]{1,0:T(8,128)(2,1)S(1)}, u32[]{:S(2)}) copy-start(bf16[384,1536]{1,0:T(8,128)(2,1)S(1)} %maximum_select_fusion.3.refs_3_) | copy-start | bytes 3538948
  132.1 0.9 copy-start.22
  133.0 66.2 %collective-permute-start.24 = (bf16[384,1536]{1,0:T(8,128)(2,1)S(1)}, bf16[384,1536]{1,0:T(8,128)(2,1)}, u32[]{:S(2)}, u32[]{:S(2)}) collective-permute-start(bf16[384,1536]{1,0:T(8,128)(2,1)S(1)} %maximum_select_fusion.3.refs_3_), channel_id=1, source_target_pairs={{0,8},{1,9},{2,10},{3,11},{4,12},{5,13},{6,14},{7,15},{8,0},{9,1},... | collective-permute-start | bytes 3538952 | tf_op jit(solution)/shard_map/ppermute | solution.py:25
  144.3 37.3 %copy-start.23 = (f32[16,1536]{1,0:T(8,128)}, f32[16,1536]{1,0:T(8,128)S(1)}, u32[]{:S(2)}) copy-start(f32[16,1536]{1,0:T(8,128)S(1)} %collective-permute-done.14.arrows) | copy-start | bytes 294916
  144.3 37.3 %collective-permute-start.15 = (bf16[192,1536]{1,0:T(8,128)(2,1)}, bf16[192,1536]{1,0:T(8,128)(2,1)}, u32[]{:S(2)}, u32[]{:S(2)}) collective-permute-start(bf16[192,1536]{1,0:T(8,128)(2,1)} %get-tuple-element.36), channel_id=1, source_target_pairs={{0,1},{1,0},{2,3},{3,2},{4,5},{5,4},{6,7},{7,6},{8,9},{9,8},{10,11... | collective-permute-start | bytes 1769480 | tf_op jit(solution)/shard_map/ppermute | solution.py:25
  144.4 54.8 %collective-permute-start.27 = (bf16[192,1536]{1,0:T(8,128)(2,1)}, bf16[192,1536]{1,0:T(8,128)(2,1)}, u32[]{:S(2)}, u32[]{:S(2)}) collective-permute-start(bf16[192,1536]{1,0:T(8,128)(2,1)} %collective-permute-done.26.refs_1_), channel_id=1, source_target_pairs={{0,8},{1,9},{2,10},{3,11},{4,12},{5,13},{6,14},{7,15},{8,0},{9,1},... | collective-permute-start | bytes 1769480 | tf_op jit(solution)/shard_map/ppermute | solution.py:25
  181.5 28.9 %collective-permute-start.22 = (bf16[192,1536]{1,0:T(8,128)(2,1)}, bf16[192,1536]{1,0:T(8,128)(2,1)}, u32[]{:S(2)}, u32[]{:S(2)}) collective-permute-start(bf16[192,1536]{1,0:T(8,128)(2,1)} %collective-permute-done.15.refs_1_), channel_id=1, source_target_pairs={{0,8},{1,9},{2,10},{3,11},{4,12},{5,13},{6,14},{7,15},{8,0},{9,1},... | collective-permute-start | bytes 1769480 | tf_op jit(solution)/shard_map/ppermute | solution.py:25
  199.1 1.1 copy-start.5
  199.2 1.4 copy-start.6
  208.7 70.3 %collective-permute-start.29 = (bf16[192,1536]{1,0:T(8,128)(2,1)}, bf16[192,1536]{1,0:T(8,128)(2,1)S(1)}, u32[]{:S(2)}, u32[]{:S(2)}) collective-permute-start(bf16[192,1536]{1,0:T(8,128)(2,1)} %get-tuple-element.25), channel_id=1, source_target_pairs={{0,0},{1,1},{2,8},{3,9},{4,4},{5,5},{6,12},{7,13},{8,2},{9,3},{10,... | collective-permute-start | bytes 1769480 | tf_op jit(solution)/shard_map/ppermute | solution.py:25
  210.5 15.7 %copy-start.25 = (f32[8,8]{1,0:T(8,128)S(1)}, f32[8,8]{1,0:T(8,128)}, u32[]{:S(2)}) copy-start(f32[8,8]{1,0:T(8,128)} %get-tuple-element.26) | copy-start | bytes 772
  210.5 68.0 %copy-start.24 = (f32[8,8]{1,0:T(8,128)S(1)}, f32[8,8]{1,0:T(8,128)}, u32[]{:S(2)}) copy-start(f32[8,8]{1,0:T(8,128)} %param.9) | copy-start | bytes 772
  210.5 68.6 %copy-start.18 = (f32[192,1536]{1,0:T(8,128)S(1)}, f32[192,1536]{1,0:T(8,128)}, u32[]{:S(2)}) copy-start(f32[192,1536]{1,0:T(8,128)} %get-tuple-element.24) | copy-start | bytes 3538948
  217.1 63.1 %collective-permute-start.25 = (bf16[192,1536]{1,0:T(8,128)(2,1)}, bf16[192,1536]{1,0:T(8,128)(2,1)S(1)}, u32[]{:S(2)}, u32[]{:S(2)}) collective-permute-start(bf16[192,1536]{1,0:T(8,128)(2,1)} %get-tuple-element.21), channel_id=1, source_target_pairs={{0,0},{1,1},{2,8},{3,9},{4,4},{5,5},{6,12},{7,13},{8,2},{9,3},{10,... | collective-permute-start | bytes 1769480 | tf_op jit(solution)/shard_map/ppermute | solution.py:25
  218.8 61.4 %collective-permute-start.28 = (bf16[192,1536]{1,0:T(8,128)(2,1)}, bf16[192,1536]{1,0:T(8,128)(2,1)S(1)}, u32[]{:S(2)}, u32[]{:S(2)}) collective-permute-start(bf16[192,1536]{1,0:T(8,128)(2,1)} %get-tuple-element.23), channel_id=1, source_target_pairs={{0,8},{1,9},{2,16},{3,17},{4,12},{5,13},{6,20},{7,21},{8,10},{9,11... | collective-permute-start | bytes 1769480 | tf_op jit(solution)/shard_map/ppermute | solution.py:25
  279.1 1.7 copy-start.19

commit v4 on v3

--- a/solution.py
+++ b/solution.py
@@ -66,39 +66,54 @@
     ]
 
 
-def after(value, *others):
-    return lax.optimization_barrier((value, *others))[0]
-
-
-def spread(top, bottom, share):
+def square():
+    return lax.axis_size("row") == 2 and lax.axis_size("col") == 4
+
+
+def begin(both):
+    if not square():
+        return move(both, swapped), None
+    return move(both, swap_or_row), move(both, only(True, by_col))
+
+
+def spread(both, cut, begun):
     rows, half = lax.axis_size("row"), lax.axis_size("col") // 2
     core = lax.axis_index("tm") % 2
     r, c = lax.axis_index("row"), lax.axis_index("col") % half
     stays = core == lax.axis_index("col") // half
-    cut = top.shape[0]
-    both = jnp.concatenate([top, bottom], axis=0)
-    if rows != 2 or half != 2:
-        own = move(both, swapped)
+    first, second = begun
+    if not square():
         whole = [
             lax.all_gather(x, AXES, axis=0, tiled=False, axis_index_groups=groups())
-            for x in (own[:cut], own[cut:])
+            for x in (first[:cut], first[cut:])
         ]
         pieces = [[(w[i], 0) for i in range(rows * 2 * half)] for w in whole]
         places = jnp.arange(rows * 2 * half, dtype=jnp.int32)
-        return own, pieces, jnp.concatenate([places, places]), (own,)
-    first = move(both, swap_or_row)
-    second = move(both, only(True, by_col))
-    own = jnp.where(stays, both, first)
+        yield first
+        yield
+        yield pieces, jnp.concatenate([places, places])
+        return
+    gate = yield jnp.where(stays, both, first)
+    if gate is not None:
+        first, second, _ = lax.optimization_barrier((first, second, gate))
     top_diag = move(jnp.where(stays, second[:cut], first[:cut]), by_row)
     low_diag = move(first[cut:], by_col)
     low_row = move(first[cut:], only(False, by_row))
     top_col = move(first[:cut], only(False, by_col))
+    first_core = move(first, by_core)
+    gate = yield (top_diag, low_diag, low_row, top_col)
+    if gate is not None:
+        top_diag, low_diag, low_row, top_col, _ = lax.optimization_barrier(
+            (top_diag, low_diag, low_row, top_col, gate)
+        )
     top_last = move(top_col, only(False, by_row))
     low_last = move(low_row, only(False, by_col))
     third = jnp.where(stays, both, jnp.concatenate([top_col, low_row], axis=0))
+    middle = [top_diag, low_diag, third]
+    middle_core = [move(x, by_core) for x in middle]
     fourth = jnp.where(stays, second, jnp.concatenate([top_last, low_last], axis=0))
-    mine = [first, top_diag, low_diag, third, fourth]
-    other = [move(x, by_core) for x in mine]
+    mine = [first, *middle, fourth]
+    other = [first_core, *middle_core, move(fourth, by_core)]
 
     def place(k, stays, when, otherwise):
         dr, dc = (jnp.where(stays, a, b) for a, b in zip(when, otherwise))
@@ -113,7 +128,7 @@
     lows = [
         (x, f) for side in (mine, other) for x, f in ((side[0], cut), (side[2], 0), (side[3], cut), (side[4], cut))
     ]
-    return own, (tops, lows), jnp.stack(places).astype(jnp.int32), (top_diag, low_diag)
+    yield (tops, lows), jnp.stack(places).astype(jnp.int32)
 
 
 def mm(a, b, dims=NN, precision=None):
@@ -300,7 +315,7 @@
         in_specs=[SMEM] + [VMEM] * len(dense) + [ANY] * len(arrays),
         out_specs=[VMEM] * len(outs),
         scratch_shapes=scratch,
-        compiler_params=pltpu.CompilerParams(vmem_limit_bytes=60 << 20),
+        compiler_params=pltpu.CompilerParams(vmem_limit_bytes=36 << 20),
         cost_estimate=pl.CostEstimate(
             flops=flops, bytes_accessed=sum(map(size, [*dense, *arrays, *outs])), transcendentals=0
         ),
@@ -323,9 +338,17 @@
     packed = jnp.where(column <= row, first_inverse[0], second_diag[0])
     packed = jnp.concatenate([packed, jnp.pad(diag_own, ((0, 15), (0, 0)))], axis=0)
     arrows = move(arrow_rows[0].reshape(2 * fixed, n), swapped)
-    _, (tops, lows), places, gate = spread(packed, coupling[0, 1], share)
-    low_share, top_share = after(coupling[0, 2], *gate), after(coupling[0, 0], *gate)
-    own, (low_pieces, top_pieces), later, _ = spread(low_share, top_share, share)
+    both = jnp.concatenate([packed, coupling[0, 1]], axis=0)
+    cut = packed.shape[0]
+    one = spread(both, cut, begin(both))
+    next(one)
+    gate = one.send(None)
+    both = jnp.concatenate([coupling[0, 2], coupling[0, 0]], axis=0)
+    if gate is not None:
+        both, _ = lax.optimization_barrier((both, gate))
+    two = spread(both, share, begin(both))
+    own = next(two)
+    (tops, lows), places = one.send(None)
     own_low, own_top = own[:share], own[share:]
     diag = sum(array[share : share + 1].astype(F32) for array, _ in tops)
 
@@ -336,11 +359,13 @@
         functools.partial(middle_kernel, size, share, firsts), "middle",
         [shape((n, n), BF16)], places, [], tops + lows, [whole, whole, dma((2, count))], n**3,
     )
+    two.send(mid)
     low, inverses = call(
         functools.partial(factor_kernel, size, 4, share, firsts[0]), "factor",
         [shape((n, n), BF16), shape((n, size), BF16)], places, [mid, diag], tops,
         [whole, pltpu.VMEM((n, n), F32), dma((count,))], 2 * n**3,
     )
+    (low_pieces, top_pieces), later = two.send(inverses)
     solved, left, tip_terms = call(
         functools.partial(solve_kernel, size, share, firsts[0]), "solve",
         [shape((2 * share, n), BF16), shape((share, n), BF16), shape((fixed, fixed), F32)],
@@ -361,8 +386,7 @@
         out, later, [left], top_pieces, [whole, dma((count,))], 2 * share * n * n,
     )
     update_far = move(update_sent, swapped)
-    speaks = jnp.logical_and(stays, col % half == 0) & (lax.axis_index("row") >= 0)
-    tip_total = lax.psum(jnp.where(speaks, tip_terms, 0.0), ("tm", "col"))
+    tip_total = lax.psum(move(tip_terms, swapped), "tm")
     fill_block = jnp.where(stays, fill_block, fill_far.astype(F32))
     update = jnp.where(stays, own_update, update_far.astype(F32)) + incoming.astype(F32)
     return (update[None], fill_block[None], tip_block - tip_total)

time: 287 us -> 266 us (0.927)
  blocking collectives: 52.2 us -> 32.1 us
  waiting for transfers between devices: 54.3 us -> 35.6 us
  starting transfers between devices: 71.1 us -> 83.1 us
  local copies, waits for them, and re-layouts: 7.66 us -> 15.9 us
    psum x1, blocking collectives: 52.2 us -> 32.1 us  [shards(): tip_total = lax.psum(move(tip_terms, swapped), 'tm')]
    ppermute x30 -> x31, waiting for transfers between devices: 54.3 us -> 35.6 us  [move(): return lax.ppermute(block, AXES, route)]
    ppermute x30 -> x31, starting transfers between devices: 71.1 us -> 83.1 us  [move(): return lax.ppermute(block, AXES, route)]
    unnamed x55 -> x62, local copies, waits for them, and re-layouts: 4.7 us -> 14.5 us
    slice x1 -> x0, other arithmetic: 3.01 us -> none  [spread(): top_col = move(first[:cut], only(False, by_col))]
  transfers between devices with their start and end apart: 30 -> 31, of which waited for: 5 -> 4; matrix products, arithmetic and copies ran while one was open for 5% -> 4% of each run, Pallas kernels for 28% -> 30%
where the time goes in v4:
time: 266 us; the launch traced here: 264 us
  starting transfers between devices  83.1 us (31%)
  Pallas kernels  78.8 us (30%)
  waiting for transfers between devices  35.6 us (13%)
  blocking collectives  32.1 us (12%)
  other arithmetic  17.3 us (7%)
  local copies, waits for them, and re-layouts  15.9 us (6%)
    ppermute x31, starting transfers between devices, move(): return lax.ppermute(block, AXES, route)  83.1 us
    pallas_call x5, Pallas kernels, call(): pl.pallas_call(kernel, out_shape=outs, in_specs=[SMEM] + [VMEM] * len(den...  78.8 us
    ppermute x31, waiting for transfers between devices, move(): return lax.ppermute(block, AXES, route)  35.6 us
    psum x1, blocking collectives, shards(): tip_total = lax.psum(move(tip_terms, swapped), 'tm')  32.1 us
    unnamed x62, local copies, waits for them, and re-layouts  14.5 us
  transfers between devices with their start and end apart: 31, of which 4 were waited for; matrix products, arithmetic and copies ran while one was open for 4% of the time, Pallas kernels for 30%

profile of v4, /device:TPU:0, one launch (start us, length us, event | category | flops | bytes accessed | tf_op | source)
XLA Modules:
  0.0 264.3 jit_solution(8649249478736097263)
XLA Ops:
  0.7 1.8 fusion.4
  2.5 1.2 slice_bitcast_fusion.1
  3.7 1.2 fusion.3
  4.9 3.0 %collective-permute-start = (bf16[400,1536]{1,0:T(8,128)(2,1)}, bf16[400,1536]{1,0:T(8,128)(2,1)S(1)}, u32[]{:S(2)}, u32[]{:S(2)}) collective-permute-start(bf16[400,1536]{1,0:T(8,128)(2,1)} %fusion.3), channel_id=1, source_target_pairs={{0,4},{1,5},{2,8},{3,9},{4,0},{5,1},{6,12},{7,13},{8,2},{9,3},{10,... | collective-permute-start | bytes 3686408 | tf_op jit(solution)/shard_map/ppermute | solution.py:25
  7.9 3.5 %collective-permute-start.1 = (bf16[400,1536]{1,0:T(8,128)(2,1)}, bf16[400,1536]{1,0:T(8,128)(2,1)S(1)}, u32[]{:S(2)}, u32[]{:S(2)}) collective-permute-start(bf16[400,1536]{1,0:T(8,128)(2,1)} %fusion.3), channel_id=1, source_target_pairs={{0,1},{1,0},{4,5},{5,4},{10,11},{11,10},{14,15},{15,14},{16,17},{1... | collective-permute-start | bytes 3686408 | tf_op jit(solution)/shard_map/ppermute | solution.py:25
  11.4 11.4 %collective-permute-done.refs_0_.refs_8_ = bf16[400,1536]{1,0:T(8,128)(2,1)S(1)} collective-permute-done((bf16[400,1536]{1,0:T(8,128)(2,1)}, bf16[400,1536]{1,0:T(8,128)(2,1)S(1)}, u32[]{:S(2)}, u32[]{:S(2)}) %collective-permute-start) | collective-permute-done | bytes 1228832 | tf_op jit(solution)/shard_map/ppermute | solution.py:25
  22.8 16.0 %collective-permute-done.1 = bf16[400,1536]{1,0:T(8,128)(2,1)S(1)} collective-permute-done((bf16[400,1536]{1,0:T(8,128)(2,1)}, bf16[400,1536]{1,0:T(8,128)(2,1)S(1)}, u32[]{:S(2)}, u32[]{:S(2)}) %collective-permute-start.1) | collective-permute-done | bytes 1228832 | tf_op jit(solution)/shard_map/ppermute | solution.py:25
  38.9 1.0 copy-done.22
  39.9 0.8 collective-permute-start.3
  40.7 0.7 collective-permute-start.4
  41.5 0.7 collective-permute-start.5
  42.3 0.7 collective-permute-start.6
  43.0 1.3 collective-permute-start.2
  44.3 17.0 %collective-permute-start.7 = (bf16[400,1536]{1,0:T(8,128)(2,1)S(1)}, bf16[400,1536]{1,0:T(8,128)(2,1)S(1)}, u32[]{:S(2)}, u32[]{:S(2)}) collective-permute-start(bf16[400,1536]{1,0:T(8,128)(2,1)S(1)} %collective-permute-done.refs_0_.refs_8_), channel_id=1, source_target_pairs={{0,8},{1,9},{2,10},{3,11},{4,12},{5,13},{6,14},{7,15},{8,0},{9,1},... | collective-permute-start | bytes 3686408 | tf_op jit(solution)/shard_map/ppermute | solution.py:25
  61.3 0.7 collective-permute-start.12
  62.0 0.3 maximum_select_fusion.refs_2_.refs_10_
  62.3 7.0 %collective-permute-start.9 = (bf16[400,1536]{1,0:T(8,128)(2,1)S(1)}, bf16[400,1536]{1,0:T(8,128)(2,1)}, u32[]{:S(2)}, u32[]{:S(2)}) collective-permute-start(bf16[400,1536]{1,0:T(8,128)(2,1)S(1)} %maximum_select_fusion.refs_2_.refs_10_), channel_id=1, source_target_pairs={{0,8},{1,9},{2,10},{3,11},{4,12},{5,13},{6,14},{7,15},{8,0},{9,1},... | collective-permute-start | bytes 3686408 | tf_op jit(solution)/shard_map/ppermute | solution.py:25
  69.3 1.4 maximum_select_fusion.1.refs_3_.refs_11_
  70.7 1.1 pad_maximum_fusion
  71.8 0.5 collective-permute-start.13
  72.3 0.8 copy-done.10
  73.1 2.7 %collective-permute-start.15 = (bf16[384,1536]{1,0:T(8,128)(2,1)}, bf16[384,1536]{1,0:T(8,128)(2,1)}, u32[]{:S(2)}, u32[]{:S(2)}) collective-permute-start(bf16[384,1536]{1,0:T(8,128)(2,1)} %pad_maximum_fusion), channel_id=1, source_target_pairs={{0,1},{1,0},{4,5},{5,4},{10,11},{11,10},{14,15},{15,14},{16,17},{1... | collective-permute-start | bytes 3538952 | tf_op jit(solution)/shard_map/ppermute | solution.py:25
  75.8 1.1 copy-done.1
  76.9 4.7 %collective-permute-start.8 = (bf16[208,1536]{1,0:T(8,128)(2,1)S(1)}, bf16[208,1536]{1,0:T(8,128)(2,1)}, u32[]{:S(2)}, u32[]{:S(2)}) collective-permute-start(bf16[208,1536]{1,0:T(8,128)(2,1)S(1)} %collective-permute-done.2.refs_1_), channel_id=1, source_target_pairs={{0,8},{1,9},{2,10},{3,11},{4,12},{5,13},{6,14},{7,15},{8,0},{9,1},... | collective-permute-start | bytes 1916936 | tf_op jit(solution)/shard_map/ppermute | solution.py:25
  81.7 1.7 collective-permute-done.8.refs_5_
  83.5 1.3 copy-done.2
  84.8 1.1 copy-done.9
  85.8 1.1 copy-done.11
  86.9 7.9 %middle.1.mid = bf16[1536,1536]{1,0:T(8,128)(2,1)S(1)} custom-call(s32[16]{0:T(128)S(1)} %stack.72.places, bf16[400,1536]{1,0:T(8,128)(2,1)S(1)} %collective-permute-done.refs_0_.refs_8_, bf16[208,1536]{1,0:T(8,128)(2,1)S(1)} %collective-permute-done.2.refs_1_, bf16[400,1536]{1,0:T(8,128)(2,1)S(1)} %maximum_select_fusion.refs_2_.refs_10_, ...), custom_call_target="tpu_custom_call" | custom-call | flops 3623878656 | bytes 21921792 | tf_op jit(solution)/shard_map/middle/pallas_call | solution.py:312
  94.8 2.2 copy-done
  97.0 6.5 %collective-permute-done.15 = bf16[384,1536]{1,0:T(8,128)(2,1)} collective-permute-done((bf16[384,1536]{1,0:T(8,128)(2,1)}, bf16[384,1536]{1,0:T(8,128)(2,1)}, u32[]{:S(2)}, u32[]{:S(2)}) %collective-permute-start.15) | collective-permute-done | bytes 1179680 | tf_op jit(solution)/shard_map/ppermute | solution.py:25
  103.4 1.7 fusion.15
  105.2 0.8 collective-permute-start.18
  106.0 3.8 %collective-permute-start.22 = (bf16[384,1536]{1,0:T(8,128)(2,1)}, bf16[384,1536]{1,0:T(8,128)(2,1)S(1)}, u32[]{:S(2)}, u32[]{:S(2)}) collective-permute-start(bf16[384,1536]{1,0:T(8,128)(2,1)} %collective-permute-done.13.refs_0_), channel_id=1, source_target_pairs={{0,8},{1,9},{2,10},{3,11},{4,12},{5,13},{6,14},{7,15},{8,0},{9,1},... | collective-permute-start | bytes 3538952 | tf_op jit(solution)/shard_map/ppermute | solution.py:25
  109.8 1.3 collective-permute-start.16
  111.1 0.9 collective-permute-start.19
  112.1 0.8 fusion.7.diag
  112.9 46.4 %factor.1 = (bf16[1536,1536]{1,0:T(8,128)(2,1)S(1)}, bf16[1536,256]{1,0:T(8,128)(2,1)S(1)}) custom-call(s32[16]{0:T(128)S(1)} %stack.72.places, bf16[1536,1536]{1,0:T(8,128)(2,1)} %copy-done, f32[1,1536]{1,0:T(1,128)S(1)} %fusion.7.diag, bf16[400,1536]{1,0:T(8,128)(2,1)S(1)} %collective-permute-done.refs_0_.refs_8_, ...), custom_call_target="tpu_custom_call" | custom-call | flops 7247757312 | bytes 18880512 | tf_op jit(solution)/shard_map/factor/pallas_call | solution.py:312
  159.4 0.7 collective-permute-start.21
  160.1 0.7 collective-permute-start.20
  160.8 2.3 maximum_select_fusion.2
  163.1 5.2 %collective-permute-start.24 = (bf16[384,1536]{1,0:T(8,128)(2,1)S(1)}, bf16[384,1536]{1,0:T(8,128)(2,1)S(1)}, u32[]{:S(2)}, u32[]{:S(2)}) collective-permute-start(bf16[384,1536]{1,0:T(8,128)(2,1)S(1)} %get-tuple-element.42.refs_2_), channel_id=1, source_target_pairs={{0,8},{1,9},{2,10},{3,11},{4,12},{5,13},{6,14},{7,15},{8,0},{9,1},... | collective-permute-start | bytes 3538952 | tf_op jit(solution)/shard_map/ppermute | solution.py:25
  168.4 1.6 maximum_select_fusion.3.refs_3_
  170.0 4.8 %collective-permute-start.25 = (bf16[384,1536]{1,0:T(8,128)(2,1)S(1)}, bf16[384,1536]{1,0:T(8,128)(2,1)S(1)}, u32[]{:S(2)}, u32[]{:S(2)}) collective-permute-start(bf16[384,1536]{1,0:T(8,128)(2,1)S(1)} %maximum_select_fusion.3.refs_3_), channel_id=1, source_target_pairs={{0,8},{1,9},{2,10},{3,11},{4,12},{5,13},{6,14},{7,15},{8,0},{9,1},... | collective-permute-start | bytes 3538952 | tf_op jit(solution)/shard_map/ppermute | solution.py:25
  174.8 0.7 collective-permute-start.14
  175.4 7.5 %collective-permute-start.27 = (bf16[192,1536]{1,0:T(8,128)(2,1)S(1)}, bf16[192,1536]{1,0:T(8,128)(2,1)S(1)}, u32[]{:S(2)}, u32[]{:S(2)}) collective-permute-start(bf16[192,1536]{1,0:T(8,128)(2,1)S(1)} %collective-permute-done.16.refs_1_), channel_id=1, source_target_pairs={{0,8},{1,9},{2,10},{3,11},{4,12},{5,13},{6,14},{7,15},{8,0},{9,1},... | collective-permute-start | bytes 1769480 | tf_op jit(solution)/shard_map/ppermute | solution.py:25
  183.0 2.8 %collective-permute-start.23 = (bf16[192,1536]{1,0:T(8,128)(2,1)S(1)}, bf16[192,1536]{1,0:T(8,128)(2,1)S(1)}, u32[]{:S(2)}, u32[]{:S(2)}) collective-permute-start(bf16[192,1536]{1,0:T(8,128)(2,1)S(1)} %collective-permute-done.17.refs_1_), channel_id=1, source_target_pairs={{0,8},{1,9},{2,10},{3,11},{4,12},{5,13},{6,14},{7,15},{8,0},{9,1},... | collective-permute-start | bytes 1769480 | tf_op jit(solution)/shard_map/ppermute | solution.py:25
  185.8 14.4 %solve.1 = (bf16[384,1536]{1,0:T(8,128)(2,1)S(1)}, bf16[192,1536]{1,0:T(8,128)(2,1)S(1)}, f32[8,8]{1,0:T(8,128)S(1)}) custom-call(s32[16]{0:T(128)S(1)} %stack.72.places, bf16[1536,1536]{1,0:T(8,128)(2,1)S(1)} %bitcast.29, bf16[1536,1536]{1,0:T(8,128)(2,1)} %copy-done.5, bf16[1536,256]{1,0:T(8,128)(2,1)S(1)} %copy-done.7, ...), custom_call_target="tpu_custom_call" | custom-call | flops 3623878656 | bytes 21922048 | tf_op jit(solution)/shard_map/solve/pallas_call | solution.py:312
  200.2 0.8 copy-done.16
  201.1 1.0 copy-done.3
  202.1 1.3 copy-done.4
  203.4 1.1 copy-done.17
  204.4 5.9 %fill.1 = (f32[192,1536]{1,0:T(8,128)S(1)}, bf16[192,1536]{1,0:T(8,128)(2,1)}, f32[192,1536]{1,0:T(8,128)}, bf16[192,1536]{1,0:T(8,128)(2,1)S(1)}) custom-call(s32[16]{0:T(128)S(1)} %stack.72.places, bf16[384,1536]{1,0:T(8,128)(2,1)S(1)} %get-tuple-element.31.left, bf16[384,1536]{1,0:T(8,128)(2,1)} %collective-permute-done.13.refs_0_, ...), custom_call_target="tpu_custom_call" | custom-call | flops 1811939328 | bytes 12976128 | tf_op jit(solution)/shard_map/fill/pallas_call | solution.py:312
  210.4 6.0 %collective-permute-start.29 = (bf16[192,1536]{1,0:T(8,128)(2,1)}, bf16[192,1536]{1,0:T(8,128)(2,1)}, u32[]{:S(2)}, u32[]{:S(2)}) collective-permute-start(bf16[192,1536]{1,0:T(8,128)(2,1)} %get-tuple-element.35), channel_id=1, source_target_pairs={{0,0},{1,1},{2,8},{3,9},{4,4},{5,5},{6,12},{7,13},{8,2},{9,3},{10,... | collective-permute-start | bytes 1769480 | tf_op jit(solution)/shard_map/ppermute | solution.py:25
  216.3 2.1 collective-permute-start.28
  218.4 0.8 copy-done.14
  219.3 1.1 copy-done.15
  220.3 4.2 %update.1 = (f32[192,1536]{1,0:T(8,128)S(1)}, bf16[192,1536]{1,0:T(8,128)(2,1)}) custom-call(s32[16]{0:T(128)S(1)} %stack.72.places, bf16[192,1536]{1,0:T(8,128)(2,1)S(1)} %get-tuple-element.23.left, bf16[384,1536]{1,0:T(8,128)(2,1)} %collective-permute-done.13.refs_0_, bf16[192,1536]{1,0:T(8,128)(2,1)S(1)} %collective-permute-done.17.refs_1_, ...), custom_call_target="tpu_custom_call" | custom-call | flops 905969664 | bytes 10616832 | tf_op jit(solution)/shard_map/update/pallas_call | solution.py:312
  224.5 1.7 collective-permute-start.26
  226.3 0.6 collective-permute-start.30
  226.9 32.1 %psum.7 = f32[8,8]{1,0:T(8,128)S(1)} all-reduce(f32[8,8]{1,0:T(8,128)S(1)} %collective-permute-done.30), channel_id=1, replica_groups=mesh['tm'=4,'row'=2,'col'=4] {'tm'}, use_global_device_ids=true, to_apply=%region_1.2 | all-reduce | flops 64 | bytes 512 | tf_op jit(solution)/shard_map/psum | solution.py:389
  259.0 0.6 sub.17
  259.6 2.2 select_bitcast_fusion
  261.8 2.3 add_bitcast_fusion
  (86 shorter events, 0.6 us)
Async XLA Ops:
  0.6 1.9 copy-start.26
  2.5 1.2 copy-start.18
  3.7 1.2 copy-start.20
  4.9 17.9 %collective-permute-start = (bf16[400,1536]{1,0:T(8,128)(2,1)}, bf16[400,1536]{1,0:T(8,128)(2,1)S(1)}, u32[]{:S(2)}, u32[]{:S(2)}) collective-permute-start(bf16[400,1536]{1,0:T(8,128)(2,1)} %fusion.3), channel_id=1, source_target_pairs={{0,4},{1,5},{2,8},{3,9},{4,0},{5,1},{6,12},{7,13},{8,2},{9,3},{10,... | collective-permute-start | bytes 3686408 | tf_op jit(solution)/shard_map/ppermute | solution.py:25
  7.9 30.9 %collective-permute-start.1 = (bf16[400,1536]{1,0:T(8,128)(2,1)}, bf16[400,1536]{1,0:T(8,128)(2,1)S(1)}, u32[]{:S(2)}, u32[]{:S(2)}) collective-permute-start(bf16[400,1536]{1,0:T(8,128)(2,1)} %fusion.3), channel_id=1, source_target_pairs={{0,1},{1,0},{4,5},{5,4},{10,11},{11,10},{14,15},{15,14},{16,17},{1... | collective-permute-start | bytes 3686408 | tf_op jit(solution)/shard_map/ppermute | solution.py:25
  38.8 1.1 copy-start.22
  39.9 22.1 %copy-start.19 = (bf16[192,1536]{1,0:T(8,128)(2,1)S(1)}, bf16[192,1536]{1,0:T(8,128)(2,1)}, u32[]{:S(2)}) copy-start(bf16[192,1536]{1,0:T(8,128)(2,1)} %copy-done.18) | copy-start | bytes 1769476
  39.9 22.1 %copy-start.21 = (bf16[192,1536]{1,0:T(8,128)(2,1)S(1)}, bf16[192,1536]{1,0:T(8,128)(2,1)}, u32[]{:S(2)}) copy-start(bf16[192,1536]{1,0:T(8,128)(2,1)} %copy-done.20) | copy-start | bytes 1769476
  39.9 1.7 collective-permute-start.3
  40.7 1.5 collective-permute-start.4
  41.5 19.9 %collective-permute-start.11 = (bf16[192,1536]{1,0:T(8,128)(2,1)S(1)}, bf16[192,1536]{1,0:T(8,128)(2,1)S(1)}, u32[]{:S(2)}, u32[]{:S(2)}) collective-permute-start(bf16[192,1536]{1,0:T(8,128)(2,1)S(1)} %slice.82), channel_id=1, source_target_pairs={{0,1},{1,0},{2,3},{3,2},{4,5},{5,4},{6,7},{7,6},{8,9},{9,8},{10,11... | collective-permute-start | bytes 1769480 | tf_op jit(solution)/shard_map/ppermute | solution.py:25
  41.5 27.8 %collective-permute-start.5 = (bf16[208,1536]{1,0:T(8,128)(2,1)S(1)}, bf16[208,1536]{1,0:T(8,128)(2,1)S(1)}, u32[]{:S(2)}, u32[]{:S(2)}) collective-permute-start(bf16[208,1536]{1,0:T(8,128)(2,1)S(1)} %collective-permute-done.3), channel_id=1, source_target_pairs={{2,6},{3,7},{6,2},{7,3},{8,12},{9,13},{12,8},{13,9},{18,22},{19,23... | collective-permute-start | bytes 1916936 | tf_op jit(solution)/shard_map/ppermute | solution.py:25
  42.3 20.1 %collective-permute-start.6 = (bf16[192,1536]{1,0:T(8,128)(2,1)S(1)}, bf16[192,1536]{1,0:T(8,128)(2,1)S(1)}, u32[]{:S(2)}, u32[]{:S(2)}) collective-permute-start(bf16[192,1536]{1,0:T(8,128)(2,1)S(1)} %collective-permute-done.4), channel_id=1, source_target_pairs={{2,3},{3,2},{6,7},{7,6},{8,9},{9,8},{12,13},{13,12},{18,19},{19,18... | collective-permute-start | bytes 1769480 | tf_op jit(solution)/shard_map/ppermute | solution.py:25
  43.0 26.4 %copy-start.23 = (bf16[400,1536]{1,0:T(8,128)(2,1)S(1)}, bf16[400,1536]{1,0:T(8,128)(2,1)}, u32[]{:S(2)}) copy-start(bf16[400,1536]{1,0:T(8,128)(2,1)} %copy-done.22) | copy-start | bytes 3686404
  43.0 28.8 %collective-permute-start.2 = (bf16[208,1536]{1,0:T(8,128)(2,1)S(1)}, bf16[208,1536]{1,0:T(8,128)(2,1)S(1)}, u32[]{:S(2)}, u32[]{:S(2)}) collective-permute-start(bf16[208,1536]{1,0:T(8,128)(2,1)S(1)} %get-tuple-element.41), channel_id=1, source_target_pairs={{0,4},{1,5},{2,6},{3,7},{4,0},{5,1},{6,2},{7,3},{8,12},{9,13},{10,... | collective-permute-start | bytes 1916936 | tf_op jit(solution)/shard_map/ppermute | solution.py:25
  44.3 31.5 %collective-permute-start.7 = (bf16[400,1536]{1,0:T(8,128)(2,1)S(1)}, bf16[400,1536]{1,0:T(8,128)(2,1)S(1)}, u32[]{:S(2)}, u32[]{:S(2)}) collective-permute-start(bf16[400,1536]{1,0:T(8,128)(2,1)S(1)} %collective-permute-done.refs_0_.refs_8_), channel_id=1, source_target_pairs={{0,8},{1,9},{2,10},{3,11},{4,12},{5,13},{6,14},{7,15},{8,0},{9,1},... | collective-permute-start | bytes 3686408 | tf_op jit(solution)/shard_map/ppermute | solution.py:25
  61.3 1.0 copy-start.8
  61.3 11.0 %collective-permute-start.12 = (bf16[192,1536]{1,0:T(8,128)(2,1)S(1)}, bf16[192,1536]{1,0:T(8,128)(2,1)S(1)}, u32[]{:S(2)}, u32[]{:S(2)}) collective-permute-start(bf16[192,1536]{1,0:T(8,128)(2,1)S(1)} %collective-permute-done.11.refs_9_), channel_id=1, source_target_pairs={{0,8},{1,9},{2,10},{3,11},{4,12},{5,13},{6,14},{7,15},{8,0},{9,1},... | collective-permute-start | bytes 1769480 | tf_op jit(solution)/shard_map/ppermute | solution.py:25
  62.3 8.4 %copy-start.24 = (bf16[192,1536]{1,0:T(8,128)(2,1)S(1)}, bf16[192,1536]{1,0:T(8,128)(2,1)}, u32[]{:S(2)}) copy-start(bf16[192,1536]{1,0:T(8,128)(2,1)} %get-tuple-element.37) | copy-start | bytes 1769476
  62.3 8.4 %copy-start.25 = (bf16[192,1536]{1,0:T(8,128)(2,1)S(1)}, bf16[192,1536]{1,0:T(8,128)(2,1)}, u32[]{:S(2)}) copy-start(bf16[192,1536]{1,0:T(8,128)(2,1)} %get-tuple-element.39) | copy-start | bytes 1769476
  62.3 21.1 %collective-permute-start.9 = (bf16[400,1536]{1,0:T(8,128)(2,1)S(1)}, bf16[400,1536]{1,0:T(8,128)(2,1)}, u32[]{:S(2)}, u32[]{:S(2)}) collective-permute-start(bf16[400,1536]{1,0:T(8,128)(2,1)S(1)} %maximum_select_fusion.refs_2_.refs_10_), channel_id=1, source_target_pairs={{0,8},{1,9},{2,10},{3,11},{4,12},{5,13},{6,14},{7,15},{8,0},{9,1},... | collective-permute-start | bytes 3686408 | tf_op jit(solution)/shard_map/ppermute | solution.py:25
  70.7 12.8 %collective-permute-start.10 = (bf16[400,1536]{1,0:T(8,128)(2,1)}, bf16[400,1536]{1,0:T(8,128)(2,1)}, u32[]{:S(2)}, u32[]{:S(2)}) collective-permute-start(bf16[400,1536]{1,0:T(8,128)(2,1)} %maximum_select_fusion.1.refs_3_.refs_11_), channel_id=1, source_target_pairs={{0,8},{1,9},{2,10},{3,11},{4,12},{5,13},{6,14},{7,15},{8,0},{9,1},... | collective-permute-start | bytes 3686408 | tf_op jit(solution)/shard_map/ppermute | solution.py:25
  71.8 25.2 %collective-permute-start.13 = (bf16[384,1536]{1,0:T(8,128)(2,1)}, bf16[384,1536]{1,0:T(8,128)(2,1)}, u32[]{:S(2)}, u32[]{:S(2)}) collective-permute-start(bf16[384,1536]{1,0:T(8,128)(2,1)} %pad_maximum_fusion), channel_id=1, source_target_pairs={{0,4},{1,5},{2,8},{3,9},{4,0},{5,1},{6,12},{7,13},{8,2},{9,3},{10,... | collective-permute-start | bytes 3538952 | tf_op jit(solution)/shard_map/ppermute | solution.py:25
  72.3 0.8 copy-start.10
  73.1 30.3 %collective-permute-start.15 = (bf16[384,1536]{1,0:T(8,128)(2,1)}, bf16[384,1536]{1,0:T(8,128)(2,1)}, u32[]{:S(2)}, u32[]{:S(2)}) collective-permute-start(bf16[384,1536]{1,0:T(8,128)(2,1)} %pad_maximum_fusion), channel_id=1, source_target_pairs={{0,1},{1,0},{4,5},{5,4},{10,11},{11,10},{14,15},{15,14},{16,17},{1... | collective-permute-start | bytes 3538952 | tf_op jit(solution)/shard_map/ppermute | solution.py:25
  75.8 1.1 copy-start.1
  76.9 6.6 %collective-permute-start.8 = (bf16[208,1536]{1,0:T(8,128)(2,1)S(1)}, bf16[208,1536]{1,0:T(8,128)(2,1)}, u32[]{:S(2)}, u32[]{:S(2)}) collective-permute-start(bf16[208,1536]{1,0:T(8,128)(2,1)S(1)} %collective-permute-done.2.refs_1_), channel_id=1, source_target_pairs={{0,8},{1,9},{2,10},{3,11},{4,12},{5,13},{6,14},{7,15},{8,0},{9,1},... | collective-permute-start | bytes 1916936 | tf_op jit(solution)/shard_map/ppermute | solution.py:25
  83.5 1.3 copy-start.2
  84.8 1.1 copy-start.9
  85.8 1.1 copy-start.11
  94.8 2.2 copy-start
  103.4 82.4 %slice-start = ((s8[4718592]{0:T(1024)(128)(4,1)}), s8[4194304]{0:T(1024)(128)(4,1)S(1)}, s32[]{:S(2)}) async-start(s8[4718592]{0:T(1024)(128)(4,1)} %bitcast.28), calls=%async_computation | async-start | bytes 8388608
  105.1 54.2 %collective-permute-start.17 = (bf16[192,1536]{1,0:T(8,128)(2,1)S(1)}, bf16[192,1536]{1,0:T(8,128)(2,1)S(1)}, u32[]{:S(2)}, u32[]{:S(2)}) collective-permute-start(bf16[192,1536]{1,0:T(8,128)(2,1)S(1)} %get-tuple-element.46), channel_id=1, source_target_pairs={{0,1},{1,0},{2,3},{3,2},{4,5},{5,4},{6,7},{7,6},{8,9},{9,8},{10,11... | collective-permute-start | bytes 1769480 | tf_op jit(solution)/shard_map/ppermute | solution.py:25
  105.2 54.2 %collective-permute-start.18 = (bf16[192,1536]{1,0:T(8,128)(2,1)S(1)}, bf16[192,1536]{1,0:T(8,128)(2,1)S(1)}, u32[]{:S(2)}, u32[]{:S(2)}) collective-permute-start(bf16[192,1536]{1,0:T(8,128)(2,1)S(1)} %get-tuple-element.46), channel_id=1, source_target_pairs={{2,6},{3,7},{6,2},{7,3},{8,12},{9,13},{12,8},{13,9},{18,22},{19,23... | collective-permute-start | bytes 1769480 | tf_op jit(solution)/shard_map/ppermute | solution.py:25
  106.0 95.0 %collective-permute-start.22 = (bf16[384,1536]{1,0:T(8,128)(2,1)}, bf16[384,1536]{1,0:T(8,128)(2,1)S(1)}, u32[]{:S(2)}, u32[]{:S(2)}) collective-permute-start(bf16[384,1536]{1,0:T(8,128)(2,1)} %collective-permute-done.13.refs_0_), channel_id=1, source_target_pairs={{0,8},{1,9},{2,10},{3,11},{4,12},{5,13},{6,14},{7,15},{8,0},{9,1},... | collective-permute-start | bytes 3538952 | tf_op jit(solution)/shard_map/ppermute | solution.py:25
  109.8 49.5 %collective-permute-start.16 = (bf16[192,1536]{1,0:T(8,128)(2,1)S(1)}, bf16[192,1536]{1,0:T(8,128)(2,1)S(1)}, u32[]{:S(2)}, u32[]{:S(2)}) collective-permute-start(bf16[192,1536]{1,0:T(8,128)(2,1)S(1)} %get-tuple-element.45), channel_id=1, source_target_pairs={{0,4},{1,5},{2,6},{3,7},{4,0},{5,1},{6,2},{7,3},{8,12},{9,13},{10,... | collective-permute-start | bytes 1769480 | tf_op jit(solution)/shard_map/ppermute | solution.py:25
  111.1 48.2 %collective-permute-start.19 = (bf16[192,1536]{1,0:T(8,128)(2,1)S(1)}, bf16[192,1536]{1,0:T(8,128)(2,1)S(1)}, u32[]{:S(2)}, u32[]{:S(2)}) collective-permute-start(bf16[192,1536]{1,0:T(8,128)(2,1)S(1)} %get-tuple-element.44), channel_id=1, source_target_pairs={{2,3},{3,2},{6,7},{7,6},{8,9},{9,8},{12,13},{13,12},{18,19},{19,18... | collective-permute-start | bytes 1769480 | tf_op jit(solution)/shard_map/ppermute | solution.py:25
  112.9 72.9 %slice-start.1 = ((s8[4718592]{0:T(1024)(128)(4,1)}), s8[524288]{0:T(1024)(128)(4,1)S(1)}, s32[]{:S(2)}) async-start(s8[4718592]{0:T(1024)(128)(4,1)} %bitcast.28), calls=%async_computation.1 | async-start | bytes 1048576
  159.3 3.8 %copy-start.5 = (bf16[1536,1536]{1,0:T(8,128)(2,1)}, bf16[1536,1536]{1,0:T(8,128)(2,1)S(1)}, u32[]{:S(2)}) copy-start(bf16[1536,1536]{1,0:T(8,128)(2,1)S(1)} %get-tuple-element.20.low_ref) | copy-start | bytes 14155780
  159.3 3.8 %copy-start.6 = (bf16[1536,256]{1,0:T(8,128)(2,1)}, bf16[1536,256]{1,0:T(8,128)(2,1)S(1)}, u32[]{:S(2)}) copy-start(bf16[1536,256]{1,0:T(8,128)(2,1)S(1)} %get-tuple-element.21.inv) | copy-start | bytes 2359300
  159.3 16.1 %copy-start.12 = (bf16[192,1536]{1,0:T(8,128)(2,1)}, bf16[192,1536]{1,0:T(8,128)(2,1)S(1)}, u32[]{:S(2)}) copy-start(bf16[192,1536]{1,0:T(8,128)(2,1)S(1)} %collective-permute-done.16.refs_1_) | copy-start | bytes 1769476
  159.4 9.0 %collective-permute-start.21 = (bf16[192,1536]{1,0:T(8,128)(2,1)S(1)}, bf16[192,1536]{1,0:T(8,128)(2,1)S(1)}, u32[]{:S(2)}, u32[]{:S(2)}) collective-permute-start(bf16[192,1536]{1,0:T(8,128)(2,1)S(1)} %collective-permute-done.18), channel_id=1, source_target_pairs={{2,3},{3,2},{6,7},{7,6},{8,9},{9,8},{12,13},{13,12},{18,19},{19,18... | collective-permute-start | bytes 1769480 | tf_op jit(solution)/shard_map/ppermute | solution.py:25
  160.1 8.3 %collective-permute-start.20 = (bf16[192,1536]{1,0:T(8,128)(2,1)S(1)}, bf16[192,1536]{1,0:T(8,128)(2,1)S(1)}, u32[]{:S(2)}, u32[]{:S(2)}) collective-permute-start(bf16[192,1536]{1,0:T(8,128)(2,1)S(1)} %collective-permute-done.19), channel_id=1, source_target_pairs={{2,6},{3,7},{6,2},{7,3},{8,12},{9,13},{12,8},{13,9},{18,22},{19,23... | collective-permute-start | bytes 1769480 | tf_op jit(solution)/shard_map/ppermute | solution.py:25
  163.1 11.6 %copy-start.28 = (f32[1,2,8,1536]{3,2,1,0:T(8,128)S(1)}, f32[1,2,8,1536]{3,2,1,0:T(8,128)}, u32[]{:S(2)}) copy-start(f32[1,2,8,1536]{3,2,1,0:T(8,128)} %param.8) | copy-start | bytes 294916
  163.1 37.9 %collective-permute-start.24 = (bf16[384,1536]{1,0:T(8,128)(2,1)S(1)}, bf16[384,1536]{1,0:T(8,128)(2,1)S(1)}, u32[]{:S(2)}, u32[]{:S(2)}) collective-permute-start(bf16[384,1536]{1,0:T(8,128)(2,1)S(1)} %get-tuple-element.42.refs_2_), channel_id=1, source_target_pairs={{0,8},{1,9},{2,10},{3,11},{4,12},{5,13},{6,14},{7,15},{8,0},{9,1},... | collective-permute-start | bytes 3538952 | tf_op jit(solution)/shard_map/ppermute | solution.py:25
  169.9 15.8 %copy-start.7 = (bf16[1536,256]{1,0:T(8,128)(2,1)S(1)}, bf16[1536,256]{1,0:T(8,128)(2,1)}, u32[]{:S(2)}) copy-start(bf16[1536,256]{1,0:T(8,128)(2,1)} %copy-done.6) | copy-start | bytes 2359300
  170.0 31.1 %collective-permute-start.25 = (bf16[384,1536]{1,0:T(8,128)(2,1)S(1)}, bf16[384,1536]{1,0:T(8,128)(2,1)S(1)}, u32[]{:S(2)}, u32[]{:S(2)}) collective-permute-start(bf16[384,1536]{1,0:T(8,128)(2,1)S(1)} %maximum_select_fusion.3.refs_3_), channel_id=1, source_target_pairs={{0,8},{1,9},{2,10},{3,11},{4,12},{5,13},{6,14},{7,15},{8,0},{9,1},... | collective-permute-start | bytes 3538952 | tf_op jit(solution)/shard_map/ppermute | solution.py:25
  174.8 8.2 %collective-permute-start.14 = (f32[16,1536]{1,0:T(8,128)S(1)}, f32[16,1536]{1,0:T(8,128)S(1)}, u32[]{:S(2)}, u32[]{:S(2)}) collective-permute-start(f32[16,1536]{1,0:T(8,128)S(1)} %bitcast.30), channel_id=1, source_target_pairs={{0,0},{1,1},{2,8},{3,9},{4,4},{5,5},{6,12},{7,13},{8,2},{9,3},{10,... | collective-permute-start | bytes 294920 | tf_op jit(solution)/shard_map/ppermute | solution.py:25
  175.4 24.8 %collective-permute-start.27 = (bf16[192,1536]{1,0:T(8,128)(2,1)S(1)}, bf16[192,1536]{1,0:T(8,128)(2,1)S(1)}, u32[]{:S(2)}, u32[]{:S(2)}) collective-permute-start(bf16[192,1536]{1,0:T(8,128)(2,1)S(1)} %collective-permute-done.16.refs_1_), channel_id=1, source_target_pairs={{0,8},{1,9},{2,10},{3,11},{4,12},{5,13},{6,14},{7,15},{8,0},{9,1},... | collective-permute-start | bytes 1769480 | tf_op jit(solution)/shard_map/ppermute | solution.py:25
  183.0 35.4 %collective-permute-start.23 = (bf16[192,1536]{1,0:T(8,128)(2,1)S(1)}, bf16[192,1536]{1,0:T(8,128)(2,1)S(1)}, u32[]{:S(2)}, u32[]{:S(2)}) collective-permute-start(bf16[192,1536]{1,0:T(8,128)(2,1)S(1)} %collective-permute-done.17.refs_1_), channel_id=1, source_target_pairs={{0,8},{1,9},{2,10},{3,11},{4,12},{5,13},{6,14},{7,15},{8,0},{9,1},... | collective-permute-start | bytes 1769480 | tf_op jit(solution)/shard_map/ppermute | solution.py:25
  185.8 16.3 %copy-start.13 = (bf16[192,1536]{1,0:T(8,128)(2,1)S(1)}, bf16[192,1536]{1,0:T(8,128)(2,1)}, u32[]{:S(2)}) copy-start(bf16[192,1536]{1,0:T(8,128)(2,1)} %copy-done.12) | copy-start | bytes 1769476
  200.2 0.8 copy-start.16
  201.1 1.0 copy-start.3
  202.1 1.3 copy-start.4
  203.4 1.1 copy-start.17
  210.4 49.3 %collective-permute-start.29 = (bf16[192,1536]{1,0:T(8,128)(2,1)}, bf16[192,1536]{1,0:T(8,128)(2,1)}, u32[]{:S(2)}, u32[]{:S(2)}) collective-permute-start(bf16[192,1536]{1,0:T(8,128)(2,1)} %get-tuple-element.35), channel_id=1, source_target_pairs={{0,0},{1,1},{2,8},{3,9},{4,4},{5,5},{6,12},{7,13},{8,2},{9,3},{10,... | collective-permute-start | bytes 1769480 | tf_op jit(solution)/shard_map/ppermute | solution.py:25
  216.3 45.5 %collective-permute-start.28 = (bf16[192,1536]{1,0:T(8,128)(2,1)S(1)}, bf16[192,1536]{1,0:T(8,128)(2,1)}, u32[]{:S(2)}, u32[]{:S(2)}) collective-permute-start(bf16[192,1536]{1,0:T(8,128)(2,1)S(1)} %get-tuple-element.33), channel_id=1, source_target_pairs={{0,8},{1,9},{2,16},{3,17},{4,12},{5,13},{6,20},{7,21},{8,10},{9,11... | collective-permute-start | bytes 1769480 | tf_op jit(solution)/shard_map/ppermute | solution.py:25
  218.4 0.8 copy-start.14
  219.3 1.1 copy-start.15
  220.3 38.7 %copy-start.27 = (f32[8,8]{1,0:T(8,128)S(1)}, f32[8,8]{1,0:T(8,128)}, u32[]{:S(2)}) copy-start(f32[8,8]{1,0:T(8,128)} %param.9) | copy-start | bytes 772
  224.5 37.3 %collective-permute-start.26 = (bf16[192,1536]{1,0:T(8,128)(2,1)}, bf16[192,1536]{1,0:T(8,128)(2,1)S(1)}, u32[]{:S(2)}, u32[]{:S(2)}) collective-permute-start(bf16[192,1536]{1,0:T(8,128)(2,1)} %get-tuple-element.30), channel_id=1, source_target_pairs={{0,0},{1,1},{2,8},{3,9},{4,4},{5,5},{6,12},{7,13},{8,2},{9,3},{10,... | collective-permute-start | bytes 1769480 | tf_op jit(solution)/shard_map/ppermute | solution.py:25
  226.3 0.7 collective-permute-start.30

commit v5 on v4

--- a/solution.py
+++ b/solution.py
@@ -89,28 +89,29 @@
         ]
         pieces = [[(w[i], 0) for i in range(rows * 2 * half)] for w in whole]
         places = jnp.arange(rows * 2 * half, dtype=jnp.int32)
-        yield first
-        yield
-        yield pieces, jnp.concatenate([places, places])
+        gate = yield first
+        gate = yield gate, None
+        gate = yield gate
+        yield gate, pieces, jnp.concatenate([places, places])
         return
     gate = yield jnp.where(stays, both, first)
-    if gate is not None:
-        first, second, _ = lax.optimization_barrier((first, second, gate))
+    first, second, gate = lax.optimization_barrier((first, second, gate))
     top_diag = move(jnp.where(stays, second[:cut], first[:cut]), by_row)
     low_diag = move(first[cut:], by_col)
     low_row = move(first[cut:], only(False, by_row))
     top_col = move(first[:cut], only(False, by_col))
     first_core = move(first, by_core)
-    gate = yield (top_diag, low_diag, low_row, top_col)
-    if gate is not None:
-        top_diag, low_diag, low_row, top_col, _ = lax.optimization_barrier(
-            (top_diag, low_diag, low_row, top_col, gate)
-        )
+    sent = yield gate, (top_diag, low_diag, low_row, top_col)
+    top_diag, low_diag, low_row, top_col, gate = lax.optimization_barrier(
+        (top_diag, low_diag, low_row, top_col, sent)
+    )
     top_last = move(top_col, only(False, by_row))
     low_last = move(low_row, only(False, by_col))
     third = jnp.where(stays, both, jnp.concatenate([top_col, low_row], axis=0))
     middle = [top_diag, low_diag, third]
     middle_core = [move(x, by_core) for x in middle]
+    sent = yield gate
+    top_last, low_last, second, gate = lax.optimization_barrier((top_last, low_last, second, sent))
     fourth = jnp.where(stays, second, jnp.concatenate([top_last, low_last], axis=0))
     mine = [first, *middle, fourth]
     other = [first_core, *middle_core, move(fourth, by_core)]
@@ -128,7 +129,7 @@
     lows = [
         (x, f) for side in (mine, other) for x, f in ((side[0], cut), (side[2], 0), (side[3], cut), (side[4], cut))
     ]
-    yield (tops, lows), jnp.stack(places).astype(jnp.int32)
+    yield gate, (tops, lows), jnp.stack(places).astype(jnp.int32)
 
 
 def mm(a, b, dims=NN, precision=None):
@@ -163,69 +164,77 @@
         copy.wait()
 
 
-def keep_lower(whole, size):
-    n = whole.shape[0]
-    for k in range(n // size):
-        rows = pl.ds(k * size, size)
-        row, col = grid_of(size, n, k * size)
-        whole[rows, :] = jnp.where(col <= row, whole[rows, :].astype(F32), 0.0).astype(BF16)
-
-
 def middle_kernel(size, share, firsts, places, *refs):
     count = len(firsts[0])
     tops, lows = refs[:count], refs[count : 2 * count]
-    mid_ref, inverse, rhs, sems = refs[2 * count :]
-    one = copies(firsts[0], share, places, 0, tops, inverse, sems.at[0])
+    mid_ref, packed, inverse, token, rhs, sems = refs[2 * count :]
+    one = copies(firsts[0], share, places, 0, tops, packed, sems.at[0])
     two = copies(firsts[1], share, places, count, lows, rhs, sems.at[1])
+    n = mid_ref.shape[0]
+    at = lambda k: pl.ds(k * size, size)
+    token[...] = jnp.zeros_like(token)
     wait(one)
-    keep_lower(inverse, size)
+    for k in range(n // size):
+        row, col = grid_of(size, n, k * size)
+        inverse[at(k), :] = jnp.where(col <= row, packed[at(k), :].astype(F32), 0.0).astype(BF16)
     wait(two)
-    for k in range(mid_ref.shape[0] // size):
-        rows, depth = pl.ds(k * size, size), pl.ds(0, (k + 1) * size)
-        mid_ref[:, rows] = mm(rhs[:, depth], inverse[rows, depth], NT).astype(BF16)
+    for k in range(n // size):
+        depth = pl.ds(0, (k + 1) * size)
+        mid_ref[:, at(k)] = mm(rhs[:, depth], inverse[at(k), depth], NT).astype(BF16)
 
 
 def spd_inverse(block, quick):
     size = block.shape[0]
     row, col = grid_of(size, size)
     eye = (row == col).astype(F32)
-    start = eye / jnp.sum(jnp.abs(block), axis=0, keepdims=True)
+    across = 1.0 / jnp.sum(jnp.abs(block), axis=0, keepdims=True)
+    down = 1.0 / jnp.sum(jnp.abs(block), axis=1, keepdims=True)
+    start = eye * (2.0 * across) - down * block * across
     parts = split(block)
     guess = start
     for _ in range(quick):
         short = guess.astype(BF16)
         guess = 2.0 * guess - mm(short, mm(parts[0], short).astype(BF16))
 
-    def gap_of(x):
+    def state_of(turn, x):
         gap = eye - mm3(parts, split(x))
-        return gap, jnp.max(jnp.sum(jnp.abs(gap), axis=0, keepdims=True))
-
-    _, worst = gap_of(guess)
-    good = worst < 0.5
-    guess = jnp.where(good, guess, start)
-
-    def go(state):
-        turn, worst, _ = state
-        return jnp.logical_and(turn < 60, worst > 2e-2)
-
-    def step(state):
-        turn, _, x = state
-        gap, _ = gap_of(x)
-        x = x + mm3(split(x), split(gap))
-        return turn + 1, gap_of(x)[1], x
-
-    guess = lax.while_loop(go, step, (0, jnp.where(good, worst, 1.0), guess))[2]
-    return guess + mm3(split(guess), split(gap_of(guess)[0]))
-
-
-def factor_kernel(size, quick, share, firsts, places, mid, diag, *refs):
-    count = len(firsts)
-    tops = refs[:count]
-    low_ref, inv_ref, packed, block, sems = refs[count:]
-    started = copies(firsts, share, places, 0, tops, packed, sems)
+        return turn, jnp.max(jnp.sum(jnp.abs(gap), axis=0, keepdims=True)), x, gap
+
+    def better(state):
+        return state[2] + mm3(split(state[2]), split(state[3]))
+
+    state = state_of(0, guess)
+    state = lax.cond(state[1] < 0.5, lambda: state, lambda: state_of(0, start))
+    state = lax.while_loop(
+        lambda state: jnp.logical_and(state[0] < 60, state[1] > 2e-2),
+        lambda state: state_of(state[0] + 1, better(state)),
+        state,
+    )
+    return better(state)
+
+
+def eliminate(size, quick, tile, low_ref, inv_ref, low_row, first, cut, blocks):
+    at = lambda k: pl.ds(k * size, size)
+    for k in range(first, cut):
+        inverse = spd_inverse(tile(k, k)[...], quick).astype(BF16)
+        inv_ref[at(k - first), :] = inverse
+        for j in range(k + 1, blocks):
+            low_ref[at(j - low_row), at(k - first)] = mm(tile(j, k)[...].astype(BF16), inverse).astype(BF16)
+        for j in range(k + 1, blocks):
+            low = low_ref[at(j - low_row), at(k - first)]
+            for i in range(j, blocks):
+                tile(i, j)[...] -= mm(tile(i, k)[...].astype(BF16), low, NT)
+
+
+def factor_kernel(size, quick, _, __, mid, packed, diag, low_ref, inv_ref, rest, token, block):
     blocks = mid.shape[0] // size
+    cut = blocks // 2
     at = lambda k: pl.ds(k * size, size)
-    wait(started)
+
+    def tile(i, j):
+        return rest.at[at(i - cut), at(j - cut)] if j >= cut else block.at[at(i), at(j)]
+
+    token[...] = jnp.zeros_like(token)
     for k in range(blocks):
         for j in range(k, blocks):
             own = packed[at(k), at(j)].astype(F32)
@@ -235,28 +244,30 @@
                 own = own + own.T + jnp.where(col == row, diag[:, at(k)], 0.0)
             else:
                 own = own.T
-            block[at(j), at(k)] = own - mm(mid[at(j), :], mid[at(k), :], NT)
-    for k in range(blocks):
-        inverse = spd_inverse(block[at(k), at(k)], quick).astype(BF16)
-        inv_ref[at(k), :] = inverse
-        for j in range(k + 1, blocks):
-            low_ref[at(j), at(k)] = mm(block[at(j), at(k)].astype(BF16), inverse).astype(BF16)
-        for j in range(k + 1, blocks):
-            low = low_ref[at(j), at(k)]
-            for i in range(j, blocks):
-                block[at(i), at(j)] -= mm(block[at(i), at(k)].astype(BF16), low, NT)
-
-
-def solve_kernel(size, share, firsts, places, mid, low_ref, inv, own_top, own_low, arrows, *refs):
-    count = len(firsts)
-    tops = refs[:count]
-    upper_ref, left_ref, tip_ref, inverse, top, rows, solved, sems = refs[count:]
-    started = copies(firsts, share, places, 0, tops, inverse, sems)
+            tile(j, k)[...] = own - mm(mid[at(j), :], mid[at(k), :], NT)
+    eliminate(size, quick, tile, low_ref, inv_ref, 0, 0, cut, blocks)
+
+
+def finish_kernel(size, quick, _, __, rest, low_ref, inv_ref, token, block):
+    at = lambda k: pl.ds(k * size, size)
+    token[...] = jnp.zeros_like(token)
+    block[...] = rest[...]
+    blocks = rest.shape[0] // size
+    eliminate(size, quick, lambda i, j: block.at[at(i), at(j)], low_ref, inv_ref, 0, 0, blocks, blocks)
+
+
+def solve_kernel(size, share, _, __, mid, inverse, low_one, inv_one, low_two, inv_two, own_top, own_low, arrows, *refs):
+    upper_ref, left_ref, tip_ref, top, rows, solved = refs
     n = mid.shape[0]
     blocks, fixed = n // size, arrows.shape[0] // 2
+    cut = blocks // 2
     at = lambda k: pl.ds(k * size, size)
-    wait(started)
-    keep_lower(inverse, size)
+
+    def low(k):
+        if k < cut:
+            return low_one[pl.ds((k + 1) * size, n - (k + 1) * size), at(k)]
+        return low_two[pl.ds((k + 1 - cut) * size, n - (k + 1) * size), at(k - cut)]
+
     terms, rest = [], arrows[:fixed]
     for _ in range(3):
         terms.append(rest.astype(BF16).astype(F32))
@@ -273,13 +284,12 @@
     rows[2 * share :] = arrow_two
     for k in range(blocks):
         row = rows[:, at(k)].astype(BF16)
-        solved[:, at(k)] = mm(row, inv[at(k), :])
+        solved[:, at(k)] = mm(row, inv_one[at(k), :] if k < cut else inv_two[at(k - cut), :])
         if k + 1 < blocks:
-            rest = pl.ds((k + 1) * size, n - (k + 1) * size)
-            rows[:, rest] -= mm(row, low_ref[rest, at(k)], NT)
+            rows[:, pl.ds((k + 1) * size, n - (k + 1) * size)] -= mm(row, low(k), NT)
     for k in range(blocks - 2, -1, -1):
-        rest = pl.ds((k + 1) * size, n - (k + 1) * size)
-        solved[:, at(k)] -= mm(solved[:, rest].astype(BF16), low_ref[rest, at(k)])
+        after = solved[:, pl.ds((k + 1) * size, n - (k + 1) * size)]
+        solved[:, at(k)] -= mm(after.astype(BF16), low(k))
     upper_ref[...] = solved[: 2 * share].astype(BF16)
     left = (top[...].astype(F32) - mm(upper_ref[:share], mid[...])).astype(BF16)
     for k in range(blocks):
@@ -315,7 +325,7 @@
         in_specs=[SMEM] + [VMEM] * len(dense) + [ANY] * len(arrays),
         out_specs=[VMEM] * len(outs),
         scratch_shapes=scratch,
-        compiler_params=pltpu.CompilerParams(vmem_limit_bytes=36 << 20),
+        compiler_params=pltpu.CompilerParams(vmem_limit_bytes=26 << 20),
         cost_estimate=pl.CostEstimate(
             flops=flops, bytes_accessed=sum(map(size, [*dense, *arrays, *outs])), transcendentals=0
         ),
@@ -342,36 +352,45 @@
     cut = packed.shape[0]
     one = spread(both, cut, begin(both))
     next(one)
-    gate = one.send(None)
+    _, gate = one.send(())
     both = jnp.concatenate([coupling[0, 2], coupling[0, 0]], axis=0)
     if gate is not None:
         both, _ = lax.optimization_barrier((both, gate))
     two = spread(both, share, begin(both))
     own = next(two)
-    (tops, lows), places = one.send(None)
+    one.send(())
+    _, (tops, lows), places = one.send(())
     own_low, own_top = own[:share], own[share:]
     diag = sum(array[share : share + 1].astype(F32) for array, _ in tops)
 
     firsts = [[f for _, f in p] for p in (tops, lows)]
     count = len(tops)
     whole = pltpu.VMEM((n, n), BF16)
-    (mid,) = call(
+    square_shape, token_shape = shape((n, n), BF16), shape((8, 128), F32)
+    mid, packed, inverse, token = call(
         functools.partial(middle_kernel, size, share, firsts), "middle",
-        [shape((n, n), BF16)], places, [], tops + lows, [whole, whole, dma((2, count))], n**3,
-    )
-    two.send(mid)
-    low, inverses = call(
-        functools.partial(factor_kernel, size, 4, share, firsts[0]), "factor",
-        [shape((n, n), BF16), shape((n, size), BF16)], places, [mid, diag], tops,
-        [whole, pltpu.VMEM((n, n), F32), dma((count,))], 2 * n**3,
-    )
-    (low_pieces, top_pieces), later = two.send(inverses)
+        [square_shape] * 3 + [token_shape], places, [], tops + lows, [whole, dma((2, count))], n**3,
+    )
+    (token, arrows), _ = two.send((token, arrows))
+    cut = n // size // 2 * size
+    rest = n - cut
+    low_one, inv_one, block, token = call(
+        functools.partial(factor_kernel, size, 3), "factor",
+        [shape((n, cut), BF16), shape((cut, size), BF16), shape((rest, rest), F32), token_shape],
+        places, [token, mid, packed, diag], [], [pltpu.VMEM((n, cut), F32)], 2 * n**3,
+    )
+    token = two.send(token)
+    low_two, inv_two, token = call(
+        functools.partial(finish_kernel, size, 3), "finish",
+        [shape((rest, rest), BF16), shape((rest, size), BF16), token_shape],
+        places, [token, block], [], [pltpu.VMEM((rest, rest), F32)], rest**3,
+    )
+    token, (low_pieces, top_pieces), later = two.send(token)
     solved, left, tip_terms = call(
-        functools.partial(solve_kernel, size, share, firsts[0]), "solve",
+        functools.partial(solve_kernel, size, share), "solve",
         [shape((2 * share, n), BF16), shape((share, n), BF16), shape((fixed, fixed), F32)],
-        places, [mid, low, inverses, own_top, own_low, arrows], tops,
-        [whole, pltpu.VMEM((share, n), BF16), pltpu.VMEM((2 * share + fixed, n), F32),
-         pltpu.VMEM((2 * share + fixed, n), F32), dma((count,))], 8 * share * n * n,
+        places, [token, mid, inverse, low_one, inv_one, low_two, inv_two, own_top, own_low, arrows], [],
+        [pltpu.VMEM((share, n), BF16)] + [pltpu.VMEM((2 * share + fixed, n), F32)] * 2, 8 * share * n * n,
     )
     out = [shape((share, n), F32), shape((share, n), BF16)]
     firsts = [[f for _, f in p] for p in (low_pieces, top_pieces)]
@@ -386,7 +405,12 @@
         out, later, [left], top_pieces, [whole, dma((count,))], 2 * share * n * n,
     )
     update_far = move(update_sent, swapped)
-    tip_total = lax.psum(move(tip_terms, swapped), "tm")
+    tip_total = move(tip_terms, swapped)
+    if lax.axis_size("tm") == 4:
+        for bit in (1, 2):
+            tip_total += move(tip_total, lambda t, r, c: (t ^ bit, r, c))
+    else:
+        tip_total = lax.psum(tip_total, "tm")
     fill_block = jnp.where(stays, fill_block, fill_far.astype(F32))
     update = jnp.where(stays, own_update, update_far.astype(F32)) + incoming.astype(F32)
     return (update[None], fill_block[None], tip_block - tip_total)

time: 266 us -> 243 us (0.914)
  the two profiles are of different devices: /device:TPU:0 before, /device:TPU:2 now
where the time goes in v5:
time: 243 us; the launch traced here: 241 us
  starting transfers between devices  81.7 us (34%)
  waiting for transfers between devices  80.7 us (33%)
  Pallas kernels  53.3 us (22%)
  other arithmetic  17.6 us (7%)
  local copies, waits for them, and re-layouts  6.63 us (3%)
    ppermute x33, starting transfers between devices, move(): return lax.ppermute(block, AXES, route)  81.7 us
    ppermute x33, waiting for transfers between devices, move(): return lax.ppermute(block, AXES, route)  80.7 us
    pallas_call x6, Pallas kernels, call(): pl.pallas_call(kernel, out_shape=outs, in_specs=[SMEM] + [VMEM] * len(den...  53.3 us
    unnamed x22, local copies, waits for them, and re-layouts  5.29 us
  transfers between devices with their start and end apart: 33, of which 7 were waited for; matrix products, arithmetic and copies ran while one was open for 5% of the time, Pallas kernels for 22%

profile of v5, /device:TPU:2, one launch (start us, length us, event | category | flops | bytes accessed | tf_op | source)
XLA Modules:
  0.0 241.2 jit_solution(17873163605090266572)
XLA Ops:
  0.7 1.8 fusion.4
  2.5 1.1 slice_bitcast_fusion
  3.6 1.2 fusion.3
  4.8 1.5 collective-permute-start
  6.3 3.5 %collective-permute-start.1 = (bf16[400,1536]{1,0:T(8,128)(2,1)}, bf16[400,1536]{1,0:T(8,128)(2,1)}, u32[]{:S(2)}, u32[]{:S(2)}) collective-permute-start(bf16[400,1536]{1,0:T(8,128)(2,1)} %fusion.3), channel_id=1, source_target_pairs={{0,1},{1,0},{4,5},{5,4},{10,11},{11,10},{14,15},{15,14},{16,17},{1... | collective-permute-start | bytes 3686408 | tf_op jit(solution)/shard_map/ppermute | solution.py:25
  9.8 11.9 %collective-permute-done.refs_0_.refs_8_ = bf16[400,1536]{1,0:T(8,128)(2,1)S(1)} collective-permute-done((bf16[400,1536]{1,0:T(8,128)(2,1)}, bf16[400,1536]{1,0:T(8,128)(2,1)S(1)}, u32[]{:S(2)}, u32[]{:S(2)}) %collective-permute-start) | collective-permute-done | bytes 1228832 | tf_op jit(solution)/shard_map/ppermute | solution.py:25
  21.7 15.6 %collective-permute-done.1 = bf16[400,1536]{1,0:T(8,128)(2,1)} collective-permute-done((bf16[400,1536]{1,0:T(8,128)(2,1)}, bf16[400,1536]{1,0:T(8,128)(2,1)}, u32[]{:S(2)}, u32[]{:S(2)}) %collective-permute-start.1) | collective-permute-done | bytes 1228832 | tf_op jit(solution)/shard_map/ppermute | solution.py:25
  37.3 1.2 fusion.13
  38.5 0.6 collective-permute-start.2
  39.0 0.7 collective-permute-start.5
  39.8 0.8 collective-permute-start.3
  40.6 0.7 collective-permute-start.4
  41.3 14.7 %collective-permute-done.3.refs_9_ = bf16[192,1536]{1,0:T(8,128)(2,1)S(1)} collective-permute-done((bf16[192,1536]{1,0:T(8,128)(2,1)S(1)}, bf16[192,1536]{1,0:T(8,128)(2,1)S(1)}, u32[]{:S(2)}, u32[]{:S(2)}) %collective-permute-start.3) | collective-permute-done | bytes 589856 | tf_op jit(solution)/shard_map/ppermute | solution.py:25
  56.1 0.7 collective-permute-start.8
  56.8 0.7 collective-permute-start.9
  57.5 8.8 %collective-permute-start.10 = (bf16[400,1536]{1,0:T(8,128)(2,1)S(1)}, bf16[400,1536]{1,0:T(8,128)(2,1)S(1)}, u32[]{:S(2)}, u32[]{:S(2)}) collective-permute-start(bf16[400,1536]{1,0:T(8,128)(2,1)S(1)} %collective-permute-done.refs_0_.refs_8_), channel_id=1, source_target_pairs={{0,8},{1,9},{2,10},{3,11},{4,12},{5,13},{6,14},{7,15},{8,0},{9,1},... | collective-permute-start | bytes 3686408 | tf_op jit(solution)/shard_map/ppermute | solution.py:25
  66.3 1.4 maximum_select_fusion.refs_2_.refs_10_
  67.7 0.5 collective-permute-start.14
  68.2 2.6 %maximum_select_fusion.1.refs_3_.refs_11_ = bf16[400,1536]{1,0:T(8,128)(2,1)} fusion(bf16[400,1536]{1,0:T(8,128)(2,1)} %collective-permute-done.1, bf16[192,1536]{1,0:T(8,128)(2,1)S(1)} %collective-permute-done.9, bf16[208,1536]{1,0:T(8,128)(2,1)S(1)} %collective-permute-done.8, pred[]{:T(512)S(6)} %eq.14), kind=kLoop, calls=%fused_computation.7 | loop fusion | flops 3072000 | bytes 3686401 | tf_op jit(solution)/shard_map/jit(_where)/select_n | solution.py:115
  70.9 5.0 %collective-permute-start.13 = (bf16[400,1536]{1,0:T(8,128)(2,1)}, bf16[400,1536]{1,0:T(8,128)(2,1)}, u32[]{:S(2)}, u32[]{:S(2)}) collective-permute-start(bf16[400,1536]{1,0:T(8,128)(2,1)} %maximum_select_fusion.1.refs_3_.refs_11_), channel_id=1, source_target_pairs={{0,8},{1,9},{2,10},{3,11},{4,12},{5,13},{6,14},{7,15},{8,0},{9,1},... | collective-permute-start | bytes 3686408 | tf_op jit(solution)/shard_map/ppermute | solution.py:25
  75.8 1.1 pad_maximum_fusion
  76.9 1.5 collective-permute-start.6
  78.4 1.1 copy-done
  79.5 2.7 %collective-permute-start.7 = (bf16[384,1536]{1,0:T(8,128)(2,1)}, bf16[384,1536]{1,0:T(8,128)(2,1)}, u32[]{:S(2)}, u32[]{:S(2)}) collective-permute-start(bf16[384,1536]{1,0:T(8,128)(2,1)} %pad_maximum_fusion), channel_id=1, source_target_pairs={{0,1},{1,0},{4,5},{5,4},{10,11},{11,10},{14,15},{15,14},{16,17},{1... | collective-permute-start | bytes 3538952 | tf_op jit(solution)/shard_map/ppermute | solution.py:25
  82.2 0.8 copy-done.4
  83.0 1.9 collective-permute-start.11
  84.9 0.1 stack.72.places._
  85.0 1.7 collective-permute-done.11.refs_5_
  86.7 0.7 collective-permute-start.15
  87.4 1.3 copy-done.1
  88.7 1.1 copy-done.3
  89.8 1.1 copy-done.5
  90.8 8.1 %middle.1 = (bf16[1536,1536]{1,0:T(8,128)(2,1)S(1)}, bf16[1536,1536]{1,0:T(8,128)(2,1)S(1)}, bf16[1536,1536]{1,0:T(8,128)(2,1)S(1)}, f32[8,128]{1,0:T(8,128)S(1)}) custom-call(s32[16]{0:T(128)S(1)} %stack.72.places._, bf16[400,1536]{1,0:T(8,128)(2,1)S(1)} %collective-permute-done.refs_0_.refs_8_, bf16[208,1536]{1,0:T(8,128)(2,1)S(1)} %collective-permute-done.2.refs_1_, ...), custom_call_target="tpu_custom_call" | custom-call | flops 3623878656 | bytes 31363072 | tf_op jit(solution)/shard_map/middle/pallas_call | solution.py:322
  99.0 9.4 %collective-permute-done.7 = bf16[384,1536]{1,0:T(8,128)(2,1)} collective-permute-done((bf16[384,1536]{1,0:T(8,128)(2,1)}, bf16[384,1536]{1,0:T(8,128)(2,1)}, u32[]{:S(2)}, u32[]{:S(2)}) %collective-permute-start.7) | collective-permute-done | bytes 1179680 | tf_op jit(solution)/shard_map/ppermute | solution.py:25
  108.4 1.2 fusion.15
  109.6 2.5 %collective-permute-start.17 = (bf16[192,1536]{1,0:T(8,128)(2,1)S(1)}, bf16[192,1536]{1,0:T(8,128)(2,1)S(1)}, u32[]{:S(2)}, u32[]{:S(2)}) collective-permute-start(bf16[192,1536]{1,0:T(8,128)(2,1)S(1)} %get-tuple-element.98), channel_id=1, source_target_pairs={{0,1},{1,0},{2,3},{3,2},{4,5},{5,4},{6,7},{7,6},{8,9},{9,8},{10,11... | collective-permute-start | bytes 1769480 | tf_op jit(solution)/shard_map/ppermute | solution.py:25
  112.1 0.7 collective-permute-start.18
  112.8 1.4 collective-permute-start.22
  114.2 1.5 collective-permute-start.16
  115.6 0.9 collective-permute-start.19
  116.6 0.8 fusion.7.diag
  117.4 18.2 %factor.1 = (bf16[1536,768]{1,0:T(8,128)(2,1)S(1)}, bf16[768,256]{1,0:T(8,128)(2,1)S(1)}, f32[768,768]{1,0:T(8,128)S(1)}, f32[8,128]{1,0:T(8,128)S(1)}) custom-call(s32[16]{0:T(128)S(1)} %stack.72.places._, f32[8,128]{1,0:T(8,128)S(1)} %get-tuple-element.58.__, bf16[1536,1536]{1,0:T(8,128)(2,1)S(1)} %get-tuple-element.59.mid, ...), custom_call_target="tpu_custom_call" | custom-call | flops 7247757312 | bytes 14563328 | tf_op jit(solution)/shard_map/factor/pallas_call | solution.py:322
  135.7 0.7 collective-permute-start.20
  136.4 12.5 %collective-permute-start.21 = (bf16[192,1536]{1,0:T(8,128)(2,1)S(1)}, bf16[192,1536]{1,0:T(8,128)(2,1)S(1)}, u32[]{:S(2)}, u32[]{:S(2)}) collective-permute-start(bf16[192,1536]{1,0:T(8,128)(2,1)S(1)} %collective-permute-done.18), channel_id=1, source_target_pairs={{2,3},{3,2},{6,7},{7,6},{8,9},{9,8},{12,13},{13,12},{18,19},{19,18... | collective-permute-start | bytes 1769480 | tf_op jit(solution)/shard_map/ppermute | solution.py:25
  148.9 1.8 maximum_select_fusion.2
  150.7 5.2 %collective-permute-start.24 = (bf16[384,1536]{1,0:T(8,128)(2,1)S(1)}, bf16[384,1536]{1,0:T(8,128)(2,1)S(1)}, u32[]{:S(2)}, u32[]{:S(2)}) collective-permute-start(bf16[384,1536]{1,0:T(8,128)(2,1)S(1)} %get-tuple-element.92.refs_2_), channel_id=1, source_target_pairs={{0,8},{1,9},{2,10},{3,11},{4,12},{5,13},{6,14},{7,15},{8,0},{9,1},... | collective-permute-start | bytes 3538952 | tf_op jit(solution)/shard_map/ppermute | solution.py:25
  155.9 7.4 %finish.1 = (bf16[768,768]{1,0:T(8,128)(2,1)S(1)}, bf16[768,256]{1,0:T(8,128)(2,1)S(1)}, f32[8,128]{1,0:T(8,128)S(1)}) custom-call(s32[16]{0:T(128)S(1)} %stack.72.places._, f32[8,128]{1,0:T(8,128)S(1)} %get-tuple-element.64.__, f32[768,768]{1,0:T(8,128)S(1)} %get-tuple-element.65.rest), custom_call_target="tpu_custom_call" | custom-call | flops 452984832 | bytes 3940352 | tf_op jit(solution)/shard_map/finish/pallas_call | solution.py:322
  163.4 1.6 maximum_select_fusion.3.refs_3_
  165.0 0.5 collective-permute-start.27
  165.6 0.1 collective-permute-start.23
  165.8 10.4 %solve.1 = (bf16[384,1536]{1,0:T(8,128)(2,1)S(1)}, bf16[192,1536]{1,0:T(8,128)(2,1)S(1)}, f32[8,8]{1,0:T(8,128)S(1)}) custom-call(s32[16]{0:T(128)S(1)} %stack.72.places._, f32[8,128]{1,0:T(8,128)S(1)} %get-tuple-element.67.__, bf16[1536,1536]{1,0:T(8,128)(2,1)S(1)} %get-tuple-element.59.mid, bf16[1536,1536]{1,0:T(8,128)(2,1)S(1)} %get-tuple-element.68.inverse, ...), custom_call_target="tpu_custom_call" | custom-call | flops 3623878656 | bytes 16814336 | tf_op jit(solution)/shard_map/solve/pallas_call | solution.py:322
  176.2 5.8 %fill.1 = (f32[192,1536]{1,0:T(8,128)S(1)}, bf16[192,1536]{1,0:T(8,128)(2,1)S(1)}, f32[192,1536]{1,0:T(8,128)}, bf16[192,1536]{1,0:T(8,128)(2,1)S(1)}) custom-call(s32[16]{0:T(128)S(1)} %stack.72.places._, bf16[384,1536]{1,0:T(8,128)(2,1)S(1)} %get-tuple-element.81.left, bf16[384,1536]{1,0:T(8,128)(2,1)S(1)} %collective-permute-done.6.refs_0_, ...), custom_call_target="tpu_custom_call" | custom-call | flops 1811939328 | bytes 12976128 | tf_op jit(solution)/shard_map/fill/pallas_call | solution.py:322
  182.0 0.7 collective-permute-start.29
  182.7 0.7 collective-permute-start.30
  183.4 19.5 %collective-permute-start.31 = (f32[8,8]{1,0:T(8,128)S(1)}, f32[8,8]{1,0:T(8,128)S(1)}, u32[]{:S(2)}, u32[]{:S(2)}) collective-permute-start(f32[8,8]{1,0:T(8,128)S(1)} %collective-permute-done.30), channel_id=1, source_target_pairs={{0,8},{1,9},{2,10},{3,11},{4,12},{5,13},{6,14},{7,15},{8,0},{9,1},... | collective-permute-start | bytes 776 | tf_op jit(solution)/shard_map/ppermute | solution.py:25
  202.9 0.8 collective-permute-done.31
  203.8 0.5 collective-permute-start.32
  204.3 3.3 %update.1 = (f32[192,1536]{1,0:T(8,128)S(1)}, bf16[192,1536]{1,0:T(8,128)(2,1)S(1)}) custom-call(s32[16]{0:T(128)S(1)} %stack.72.places._, bf16[192,1536]{1,0:T(8,128)(2,1)S(1)} %get-tuple-element.74.left, bf16[384,1536]{1,0:T(8,128)(2,1)S(1)} %collective-permute-done.6.refs_0_, bf16[192,1536]{1,0:T(8,128)(2,1)S(1)} %collective-permute-done.17.refs_1_, ...), custom_call_target="tpu_custom_call" | custom-call | flops 905969664 | bytes 10616832 | tf_op jit(solution)/shard_map/update/pallas_call | solution.py:322
  207.6 0.7 collective-permute-start.26
  208.3 3.3 %collective-permute-start.28 = (bf16[192,1536]{1,0:T(8,128)(2,1)S(1)}, bf16[192,1536]{1,0:T(8,128)(2,1)S(1)}, u32[]{:S(2)}, u32[]{:S(2)}) collective-permute-start(bf16[192,1536]{1,0:T(8,128)(2,1)S(1)} %get-tuple-element.83), channel_id=1, source_target_pairs={{0,8},{1,9},{2,16},{3,17},{4,12},{5,13},{6,20},{7,21},{8,10},{9,11... | collective-permute-start | bytes 1769480 | tf_op jit(solution)/shard_map/ppermute | solution.py:25
  211.6 0.6 add_subtract_fusion
  212.2 1.1 select_bitcast_fusion
  213.4 26.5 %collective-permute-done.28 = bf16[192,1536]{1,0:T(8,128)(2,1)S(1)} collective-permute-done((bf16[192,1536]{1,0:T(8,128)(2,1)S(1)}, bf16[192,1536]{1,0:T(8,128)(2,1)S(1)}, u32[]{:S(2)}, u32[]{:S(2)}) %collective-permute-start.28) | collective-permute-done | bytes 589856 | tf_op jit(solution)/shard_map/ppermute | solution.py:25
  239.8 1.2 add_bitcast_fusion
  (50 shorter events, 0.3 us)
Async XLA Ops:
  0.6 1.9 copy-start.8
  4.8 16.9 %collective-permute-start = (bf16[400,1536]{1,0:T(8,128)(2,1)}, bf16[400,1536]{1,0:T(8,128)(2,1)S(1)}, u32[]{:S(2)}, u32[]{:S(2)}) collective-permute-start(bf16[400,1536]{1,0:T(8,128)(2,1)} %fusion.3), channel_id=1, source_target_pairs={{0,4},{1,5},{2,8},{3,9},{4,0},{5,1},{6,12},{7,13},{8,2},{9,3},{10,... | collective-permute-start | bytes 3686408 | tf_op jit(solution)/shard_map/ppermute | solution.py:25
  6.3 31.0 %collective-permute-start.1 = (bf16[400,1536]{1,0:T(8,128)(2,1)}, bf16[400,1536]{1,0:T(8,128)(2,1)}, u32[]{:S(2)}, u32[]{:S(2)}) collective-permute-start(bf16[400,1536]{1,0:T(8,128)(2,1)} %fusion.3), channel_id=1, source_target_pairs={{0,1},{1,0},{4,5},{5,4},{10,11},{11,10},{14,15},{15,14},{16,17},{1... | collective-permute-start | bytes 3686408 | tf_op jit(solution)/shard_map/ppermute | solution.py:25
  38.5 17.6 %collective-permute-start.2 = (bf16[208,1536]{1,0:T(8,128)(2,1)S(1)}, bf16[208,1536]{1,0:T(8,128)(2,1)S(1)}, u32[]{:S(2)}, u32[]{:S(2)}) collective-permute-start(bf16[208,1536]{1,0:T(8,128)(2,1)S(1)} %get-tuple-element.91), channel_id=1, source_target_pairs={{0,4},{1,5},{2,6},{3,7},{4,0},{5,1},{6,2},{7,3},{8,12},{9,13},{10,... | collective-permute-start | bytes 1916936 | tf_op jit(solution)/shard_map/ppermute | solution.py:25
  39.0 17.0 %collective-permute-start.5 = (bf16[208,1536]{1,0:T(8,128)(2,1)S(1)}, bf16[208,1536]{1,0:T(8,128)(2,1)S(1)}, u32[]{:S(2)}, u32[]{:S(2)}) collective-permute-start(bf16[208,1536]{1,0:T(8,128)(2,1)S(1)} %get-tuple-element.90), channel_id=1, source_target_pairs={{2,3},{3,2},{6,7},{7,6},{8,9},{9,8},{12,13},{13,12},{18,19},{19,18... | collective-permute-start | bytes 1916936 | tf_op jit(solution)/shard_map/ppermute | solution.py:25
  39.8 16.3 %collective-permute-start.3 = (bf16[192,1536]{1,0:T(8,128)(2,1)S(1)}, bf16[192,1536]{1,0:T(8,128)(2,1)S(1)}, u32[]{:S(2)}, u32[]{:S(2)}) collective-permute-start(bf16[192,1536]{1,0:T(8,128)(2,1)S(1)} %slice.66), channel_id=1, source_target_pairs={{0,1},{1,0},{2,3},{3,2},{4,5},{5,4},{6,7},{7,6},{8,9},{9,8},{10,11... | collective-permute-start | bytes 1769480 | tf_op jit(solution)/shard_map/ppermute | solution.py:25
  40.6 15.4 %collective-permute-start.4 = (bf16[192,1536]{1,0:T(8,128)(2,1)S(1)}, bf16[192,1536]{1,0:T(8,128)(2,1)S(1)}, u32[]{:S(2)}, u32[]{:S(2)}) collective-permute-start(bf16[192,1536]{1,0:T(8,128)(2,1)S(1)} %slice.66), channel_id=1, source_target_pairs={{2,6},{3,7},{6,2},{7,3},{8,12},{9,13},{12,8},{13,9},{18,22},{19,23... | collective-permute-start | bytes 1769480 | tf_op jit(solution)/shard_map/ppermute | solution.py:25
  56.1 11.7 %copy-start.2 = (bf16[192,1536]{1,0:T(8,128)(2,1)}, bf16[192,1536]{1,0:T(8,128)(2,1)S(1)}, u32[]{:S(2)}) copy-start(bf16[192,1536]{1,0:T(8,128)(2,1)S(1)} %collective-permute-done.3.refs_9_) | copy-start | bytes 1769476
  56.1 12.1 %collective-permute-start.8 = (bf16[208,1536]{1,0:T(8,128)(2,1)S(1)}, bf16[208,1536]{1,0:T(8,128)(2,1)S(1)}, u32[]{:S(2)}, u32[]{:S(2)}) collective-permute-start(bf16[208,1536]{1,0:T(8,128)(2,1)S(1)} %collective-permute-done.5), channel_id=1, source_target_pairs={{2,6},{3,7},{6,2},{7,3},{8,12},{9,13},{12,8},{13,9},{18,22},{19,23... | collective-permute-start | bytes 1916936 | tf_op jit(solution)/shard_map/ppermute | solution.py:25
  56.8 11.4 %collective-permute-start.9 = (bf16[192,1536]{1,0:T(8,128)(2,1)S(1)}, bf16[192,1536]{1,0:T(8,128)(2,1)S(1)}, u32[]{:S(2)}, u32[]{:S(2)}) collective-permute-start(bf16[192,1536]{1,0:T(8,128)(2,1)S(1)} %collective-permute-done.4), channel_id=1, source_target_pairs={{2,3},{3,2},{6,7},{7,6},{8,9},{9,8},{12,13},{13,12},{18,19},{19,18... | collective-permute-start | bytes 1769480 | tf_op jit(solution)/shard_map/ppermute | solution.py:25
  57.5 20.9 %collective-permute-start.10 = (bf16[400,1536]{1,0:T(8,128)(2,1)S(1)}, bf16[400,1536]{1,0:T(8,128)(2,1)S(1)}, u32[]{:S(2)}, u32[]{:S(2)}) collective-permute-start(bf16[400,1536]{1,0:T(8,128)(2,1)S(1)} %collective-permute-done.refs_0_.refs_8_), channel_id=1, source_target_pairs={{0,8},{1,9},{2,10},{3,11},{4,12},{5,13},{6,14},{7,15},{8,0},{9,1},... | collective-permute-start | bytes 3686408 | tf_op jit(solution)/shard_map/ppermute | solution.py:25
  67.7 8.1 %copy-start.6 = (bf16[192,1536]{1,0:T(8,128)(2,1)S(1)}, bf16[192,1536]{1,0:T(8,128)(2,1)}, u32[]{:S(2)}) copy-start(bf16[192,1536]{1,0:T(8,128)(2,1)} %get-tuple-element.88) | copy-start | bytes 1769476
  67.7 8.1 %copy-start.7 = (bf16[192,1536]{1,0:T(8,128)(2,1)S(1)}, bf16[192,1536]{1,0:T(8,128)(2,1)}, u32[]{:S(2)}) copy-start(bf16[192,1536]{1,0:T(8,128)(2,1)} %get-tuple-element.89) | copy-start | bytes 1769476
  67.7 19.7 %collective-permute-start.12 = (bf16[400,1536]{1,0:T(8,128)(2,1)}, bf16[400,1536]{1,0:T(8,128)(2,1)}, u32[]{:S(2)}, u32[]{:S(2)}) collective-permute-start(bf16[400,1536]{1,0:T(8,128)(2,1)} %maximum_select_fusion.refs_2_.refs_10_), channel_id=1, source_target_pairs={{0,8},{1,9},{2,10},{3,11},{4,12},{5,13},{6,14},{7,15},{8,0},{9,1},... | collective-permute-start | bytes 3686408 | tf_op jit(solution)/shard_map/ppermute | solution.py:25
  67.7 14.5 %collective-permute-start.14 = (bf16[192,1536]{1,0:T(8,128)(2,1)S(1)}, bf16[192,1536]{1,0:T(8,128)(2,1)S(1)}, u32[]{:S(2)}, u32[]{:S(2)}) collective-permute-start(bf16[192,1536]{1,0:T(8,128)(2,1)S(1)} %collective-permute-done.3.refs_9_), channel_id=1, source_target_pairs={{0,8},{1,9},{2,10},{3,11},{4,12},{5,13},{6,14},{7,15},{8,0},{9,1},... | collective-permute-start | bytes 1769480 | tf_op jit(solution)/shard_map/ppermute | solution.py:25
  70.9 16.5 %collective-permute-start.13 = (bf16[400,1536]{1,0:T(8,128)(2,1)}, bf16[400,1536]{1,0:T(8,128)(2,1)}, u32[]{:S(2)}, u32[]{:S(2)}) collective-permute-start(bf16[400,1536]{1,0:T(8,128)(2,1)} %maximum_select_fusion.1.refs_3_.refs_11_), channel_id=1, source_target_pairs={{0,8},{1,9},{2,10},{3,11},{4,12},{5,13},{6,14},{7,15},{8,0},{9,1},... | collective-permute-start | bytes 3686408 | tf_op jit(solution)/shard_map/ppermute | solution.py:25
  75.8 10.9 %copy-start.10 = (f32[1,2,8,1536]{3,2,1,0:T(8,128)S(1)}, f32[1,2,8,1536]{3,2,1,0:T(8,128)}, u32[]{:S(2)}) copy-start(f32[1,2,8,1536]{3,2,1,0:T(8,128)} %param.8) | copy-start | bytes 294916
  76.9 22.0 %collective-permute-start.6 = (bf16[384,1536]{1,0:T(8,128)(2,1)}, bf16[384,1536]{1,0:T(8,128)(2,1)S(1)}, u32[]{:S(2)}, u32[]{:S(2)}) collective-permute-start(bf16[384,1536]{1,0:T(8,128)(2,1)} %pad_maximum_fusion), channel_id=1, source_target_pairs={{0,4},{1,5},{2,8},{3,9},{4,0},{5,1},{6,12},{7,13},{8,2},{9,3},{10,... | collective-permute-start | bytes 3538952 | tf_op jit(solution)/shard_map/ppermute | solution.py:25
  78.4 1.1 copy-start
  79.5 28.9 %collective-permute-start.7 = (bf16[384,1536]{1,0:T(8,128)(2,1)}, bf16[384,1536]{1,0:T(8,128)(2,1)}, u32[]{:S(2)}, u32[]{:S(2)}) collective-permute-start(bf16[384,1536]{1,0:T(8,128)(2,1)} %pad_maximum_fusion), channel_id=1, source_target_pairs={{0,1},{1,0},{4,5},{5,4},{10,11},{11,10},{14,15},{15,14},{16,17},{1... | collective-permute-start | bytes 3538952 | tf_op jit(solution)/shard_map/ppermute | solution.py:25
  82.2 0.8 copy-start.4
  83.0 3.7 %collective-permute-start.11 = (bf16[208,1536]{1,0:T(8,128)(2,1)S(1)}, bf16[208,1536]{1,0:T(8,128)(2,1)}, u32[]{:S(2)}, u32[]{:S(2)}) collective-permute-start(bf16[208,1536]{1,0:T(8,128)(2,1)S(1)} %collective-permute-done.2.refs_1_), channel_id=1, source_target_pairs={{0,8},{1,9},{2,10},{3,11},{4,12},{5,13},{6,14},{7,15},{8,0},{9,1},... | collective-permute-start | bytes 1916936 | tf_op jit(solution)/shard_map/ppermute | solution.py:25
  86.7 12.2 %collective-permute-start.15 = (f32[16,1536]{1,0:T(8,128)S(1)}, f32[16,1536]{1,0:T(8,128)S(1)}, u32[]{:S(2)}, u32[]{:S(2)}) collective-permute-start(f32[16,1536]{1,0:T(8,128)S(1)} %bitcast.28), channel_id=1, source_target_pairs={{0,0},{1,1},{2,8},{3,9},{4,4},{5,5},{6,12},{7,13},{8,2},{9,3},{10,... | collective-permute-start | bytes 294920 | tf_op jit(solution)/shard_map/ppermute | solution.py:25
  87.4 1.3 copy-start.1
  88.7 1.1 copy-start.3
  89.8 1.1 copy-start.5
  109.6 26.1 %collective-permute-start.17 = (bf16[192,1536]{1,0:T(8,128)(2,1)S(1)}, bf16[192,1536]{1,0:T(8,128)(2,1)S(1)}, u32[]{:S(2)}, u32[]{:S(2)}) collective-permute-start(bf16[192,1536]{1,0:T(8,128)(2,1)S(1)} %get-tuple-element.98), channel_id=1, source_target_pairs={{0,1},{1,0},{2,3},{3,2},{4,5},{5,4},{6,7},{7,6},{8,9},{9,8},{10,11... | collective-permute-start | bytes 1769480 | tf_op jit(solution)/shard_map/ppermute | solution.py:25
  112.1 23.6 %collective-permute-start.18 = (bf16[192,1536]{1,0:T(8,128)(2,1)S(1)}, bf16[192,1536]{1,0:T(8,128)(2,1)S(1)}, u32[]{:S(2)}, u32[]{:S(2)}) collective-permute-start(bf16[192,1536]{1,0:T(8,128)(2,1)S(1)} %get-tuple-element.98), channel_id=1, source_target_pairs={{2,6},{3,7},{6,2},{7,3},{8,12},{9,13},{12,8},{13,9},{18,22},{19,23... | collective-permute-start | bytes 1769480 | tf_op jit(solution)/shard_map/ppermute | solution.py:25
  112.8 63.4 %collective-permute-start.22 = (bf16[384,1536]{1,0:T(8,128)(2,1)S(1)}, bf16[384,1536]{1,0:T(8,128)(2,1)S(1)}, u32[]{:S(2)}, u32[]{:S(2)}) collective-permute-start(bf16[384,1536]{1,0:T(8,128)(2,1)S(1)} %collective-permute-done.6.refs_0_), channel_id=1, source_target_pairs={{0,8},{1,9},{2,10},{3,11},{4,12},{5,13},{6,14},{7,15},{8,0},{9,1},... | collective-permute-start | bytes 3538952 | tf_op jit(solution)/shard_map/ppermute | solution.py:25
  114.2 21.5 %collective-permute-start.16 = (bf16[192,1536]{1,0:T(8,128)(2,1)S(1)}, bf16[192,1536]{1,0:T(8,128)(2,1)S(1)}, u32[]{:S(2)}, u32[]{:S(2)}) collective-permute-start(bf16[192,1536]{1,0:T(8,128)(2,1)S(1)} %get-tuple-element.97), channel_id=1, source_target_pairs={{0,4},{1,5},{2,6},{3,7},{4,0},{5,1},{6,2},{7,3},{8,12},{9,13},{10,... | collective-permute-start | bytes 1769480 | tf_op jit(solution)/shard_map/ppermute | solution.py:25
  115.6 20.1 %collective-permute-start.19 = (bf16[192,1536]{1,0:T(8,128)(2,1)S(1)}, bf16[192,1536]{1,0:T(8,128)(2,1)S(1)}, u32[]{:S(2)}, u32[]{:S(2)}) collective-permute-start(bf16[192,1536]{1,0:T(8,128)(2,1)S(1)} %get-tuple-element.96), channel_id=1, source_target_pairs={{2,3},{3,2},{6,7},{7,6},{8,9},{9,8},{12,13},{13,12},{18,19},{19,18... | collective-permute-start | bytes 1769480 | tf_op jit(solution)/shard_map/ppermute | solution.py:25
  135.7 27.7 %collective-permute-start.20 = (bf16[192,1536]{1,0:T(8,128)(2,1)S(1)}, bf16[192,1536]{1,0:T(8,128)(2,1)S(1)}, u32[]{:S(2)}, u32[]{:S(2)}) collective-permute-start(bf16[192,1536]{1,0:T(8,128)(2,1)S(1)} %collective-permute-done.19), channel_id=1, source_target_pairs={{2,6},{3,7},{6,2},{7,3},{8,12},{9,13},{12,8},{13,9},{18,22},{19,23... | collective-permute-start | bytes 1769480 | tf_op jit(solution)/shard_map/ppermute | solution.py:25
  136.4 27.0 %collective-permute-start.21 = (bf16[192,1536]{1,0:T(8,128)(2,1)S(1)}, bf16[192,1536]{1,0:T(8,128)(2,1)S(1)}, u32[]{:S(2)}, u32[]{:S(2)}) collective-permute-start(bf16[192,1536]{1,0:T(8,128)(2,1)S(1)} %collective-permute-done.18), channel_id=1, source_target_pairs={{2,3},{3,2},{6,7},{7,6},{8,9},{9,8},{12,13},{13,12},{18,19},{19,18... | collective-permute-start | bytes 1769480 | tf_op jit(solution)/shard_map/ppermute | solution.py:25
  150.7 25.5 %collective-permute-start.24 = (bf16[384,1536]{1,0:T(8,128)(2,1)S(1)}, bf16[384,1536]{1,0:T(8,128)(2,1)S(1)}, u32[]{:S(2)}, u32[]{:S(2)}) collective-permute-start(bf16[384,1536]{1,0:T(8,128)(2,1)S(1)} %get-tuple-element.92.refs_2_), channel_id=1, source_target_pairs={{0,8},{1,9},{2,10},{3,11},{4,12},{5,13},{6,14},{7,15},{8,0},{9,1},... | collective-permute-start | bytes 3538952 | tf_op jit(solution)/shard_map/ppermute | solution.py:25
  165.0 11.2 %collective-permute-start.25 = (bf16[384,1536]{1,0:T(8,128)(2,1)S(1)}, bf16[384,1536]{1,0:T(8,128)(2,1)S(1)}, u32[]{:S(2)}, u32[]{:S(2)}) collective-permute-start(bf16[384,1536]{1,0:T(8,128)(2,1)S(1)} %maximum_select_fusion.3.refs_3_), channel_id=1, source_target_pairs={{0,8},{1,9},{2,10},{3,11},{4,12},{5,13},{6,14},{7,15},{8,0},{9,1},... | collective-permute-start | bytes 3538952 | tf_op jit(solution)/shard_map/ppermute | solution.py:25
  165.0 11.1 %collective-permute-start.27 = (bf16[192,1536]{1,0:T(8,128)(2,1)S(1)}, bf16[192,1536]{1,0:T(8,128)(2,1)S(1)}, u32[]{:S(2)}, u32[]{:S(2)}) collective-permute-start(bf16[192,1536]{1,0:T(8,128)(2,1)S(1)} %collective-permute-done.16.refs_1_), channel_id=1, source_target_pairs={{0,8},{1,9},{2,10},{3,11},{4,12},{5,13},{6,14},{7,15},{8,0},{9,1},... | collective-permute-start | bytes 1769480 | tf_op jit(solution)/shard_map/ppermute | solution.py:25
  165.6 38.7 %collective-permute-start.23 = (bf16[192,1536]{1,0:T(8,128)(2,1)S(1)}, bf16[192,1536]{1,0:T(8,128)(2,1)S(1)}, u32[]{:S(2)}, u32[]{:S(2)}) collective-permute-start(bf16[192,1536]{1,0:T(8,128)(2,1)S(1)} %collective-permute-done.17.refs_1_), channel_id=1, source_target_pairs={{0,8},{1,9},{2,10},{3,11},{4,12},{5,13},{6,14},{7,15},{8,0},{9,1},... | collective-permute-start | bytes 1769480 | tf_op jit(solution)/shard_map/ppermute | solution.py:25
  182.0 30.2 %collective-permute-start.29 = (bf16[192,1536]{1,0:T(8,128)(2,1)S(1)}, bf16[192,1536]{1,0:T(8,128)(2,1)S(1)}, u32[]{:S(2)}, u32[]{:S(2)}) collective-permute-start(bf16[192,1536]{1,0:T(8,128)(2,1)S(1)} %get-tuple-element.85), channel_id=1, source_target_pairs={{0,0},{1,1},{2,8},{3,9},{4,4},{5,5},{6,12},{7,13},{8,2},{9,3},{10,... | collective-permute-start | bytes 1769480 | tf_op jit(solution)/shard_map/ppermute | solution.py:25
  182.7 0.7 collective-permute-start.30
  183.4 20.3 %collective-permute-start.31 = (f32[8,8]{1,0:T(8,128)S(1)}, f32[8,8]{1,0:T(8,128)S(1)}, u32[]{:S(2)}, u32[]{:S(2)}) collective-permute-start(f32[8,8]{1,0:T(8,128)S(1)} %collective-permute-done.30), channel_id=1, source_target_pairs={{0,8},{1,9},{2,10},{3,11},{4,12},{5,13},{6,14},{7,15},{8,0},{9,1},... | collective-permute-start | bytes 776 | tf_op jit(solution)/shard_map/ppermute | solution.py:25
  203.8 7.9 %collective-permute-start.32 = (f32[8,8]{1,0:T(8,128)S(1)}, f32[8,8]{1,0:T(8,128)S(1)}, u32[]{:S(2)}, u32[]{:S(2)}) collective-permute-start(f32[8,8]{1,0:T(8,128)S(1)} %add.190), channel_id=1, source_target_pairs={{0,16},{1,17},{2,18},{3,19},{4,20},{5,21},{6,22},{7,23},{8,24},{9,... | collective-permute-start | bytes 776 | tf_op jit(solution)/shard_map/ppermute | solution.py:25
  204.3 7.3 %copy-start.9 = (f32[8,8]{1,0:T(8,128)S(1)}, f32[8,8]{1,0:T(8,128)}, u32[]{:S(2)}) copy-start(f32[8,8]{1,0:T(8,128)} %param.9) | copy-start | bytes 772
  207.6 5.8 %collective-permute-start.26 = (bf16[192,1536]{1,0:T(8,128)(2,1)S(1)}, bf16[192,1536]{1,0:T(8,128)(2,1)S(1)}, u32[]{:S(2)}, u32[]{:S(2)}) collective-permute-start(bf16[192,1536]{1,0:T(8,128)(2,1)S(1)} %get-tuple-element.80), channel_id=1, source_target_pairs={{0,0},{1,1},{2,8},{3,9},{4,4},{5,5},{6,12},{7,13},{8,2},{9,3},{10,... | collective-permute-start | bytes 1769480 | tf_op jit(solution)/shard_map/ppermute | solution.py:25
  208.3 31.5 %collective-permute-start.28 = (bf16[192,1536]{1,0:T(8,128)(2,1)S(1)}, bf16[192,1536]{1,0:T(8,128)(2,1)S(1)}, u32[]{:S(2)}, u32[]{:S(2)}) collective-permute-start(bf16[192,1536]{1,0:T(8,128)(2,1)S(1)} %get-tuple-element.83), channel_id=1, source_target_pairs={{0,8},{1,9},{2,16},{3,17},{4,12},{5,13},{6,20},{7,21},{8,10},{9,11... | collective-permute-start | bytes 1769480 | tf_op jit(solution)/shard_map/ppermute | solution.py:25
